TPU v7x, 128 devices: a whole 4x4x4 slice. The times are simulated.
128 devices in a mesh: ctx: 32 (over z, y_lo, x), head: 4 (over y_hi, core).
Axes of the slice: x: 4, y: 4 (y_hi: 2, y_lo: 2; y = y_hi * 2 + y_lo), z: 4, core: 2. Of those that a mesh axis runs over, the one named last changes fastest.
Arguments:
- events: bfloat16 [24576, 1024], P('ctx', 'head'), may hold values from -3 to 3
- norm_gain: float32 [1024], replicated, may hold values from 0.5 to 1.5
- w_uvqk: bfloat16 [1024, 4, 1024], P(None, None, 'head'), may hold values from -4 to 4
- w_out: bfloat16 [1024, 1024], P('head'), may hold values from -0.1875 to 0.1875
- lengths: int32 [8], replicated, may hold values from 1 to 13824, 24576 in all
Outputs:
- mixed: bfloat16 [24576, 1024], P('ctx', 'head')
Inputs may be any that keep to these rules, and one draw needn't show every extreme that they name: The lengths sum to 24576; the longest is exactly 13824.
All inputs are finite; a program needn't handle non-finite values.
Results may differ from a plain program's by a relative error of at most 0.0062.
Values may be sent and summed in bfloat16 or wider, within the bound.
No kernel may reach another device: no remote copies, remote signals or barrier semaphores. Data moves between devices by JAX's collectives and lax.ppermute only.
A program may use at most 128 MiB of HBM per device.

v0:
```python
import jax
import jax.numpy as jnp
import numpy as np
from jax import lax
from jax.experimental import pallas as pl
from jax.experimental.pallas import tpu as pltpu
from jax.sharding import Mesh
from jax.sharding import PartitionSpec as P


D = 1024
HDIM = 128
ROWS = 768
SUB = 384
TILES = 16
KEYS = 256
KEY_TILES = 24
TAIL = 16
EPS = 1e-05
AXES = ("z", "yl", "x", "yh", "core")
SIZES = (4, 2, 4, 2, 2)
HALF_SCALE = 0.5 * HDIM ** (-0.5)
FAR = 1 << 24
BF = jnp.bfloat16
F32 = jnp.float32


def send(array, target):
    pairs = []
    for source in range(int(np.prod(SIZES))):
        place = np.unravel_index(source, SIZES)
        dest = [int(t) % n for t, n in zip(target(*[int(p) for p in place]), SIZES)]
        pairs.append((source, int(np.ravel_multi_index(dest, SIZES))))
    return lax.ppermute(array, AXES, pairs)


def flip_core(array):
    return send(array, lambda z, yl, x, yh, c: (z, yl, x, yh, 1 - c))


def to_p1(array):
    return send(array, lambda z, yl, x, yh, c: (z, 1 - yl, x, yh, c))


def to_p2(array):
    return send(array, lambda z, yl, x, yh, c: (z, 1 - yl, x, 1 - yh, c))


def to_p3(array):
    return send(array, lambda z, yl, x, yh, c: (z, yl, x, 1 - yh, c))


def shift_z(array, d):
    return send(array, lambda z, yl, x, yh, c: (z + d, yl, x, yh, c))


def shift_x(array, d):
    return send(array, lambda z, yl, x, yh, c: (z, yl, x + d, yh, c))


def silu_of_half(h):
    return h + h * jnp.tanh(h)


def whole(shape):
    return pl.BlockSpec(shape, lambda i, s: (0,) * len(shape))


def pack_kernel(info, w_ref, w_out):
    for j in range(4):
        rows = pl.ds(pl.multiple_of((info[3] ^ j) * 256, 256), 256)
        for k, g in enumerate((0, 1, 2, 3)):
            cols = pl.ds(pl.multiple_of(g * 256 + info[1] * HDIM, HDIM), HDIM)
            w_out[j * 256 : (j + 1) * 256, k * HDIM : (k + 1) * HDIM] = w_ref[rows, cols]


def pack_weights(info, w):
    return pl.pallas_call(
        pack_kernel,
        grid_spec=pltpu.PrefetchScalarGridSpec(
            num_scalar_prefetch=1, grid=(1,), in_specs=[whole((D, D))], out_specs=whole((D, 4 * HDIM))
        ),
        out_shape=jax.ShapeDtypeStruct((D, 4 * HDIM), BF),
        name="pack_weights",
    )(info, w)


PIECE = 128


def project_rows(info, parts, gain_ref, w_ref, put):
    for r in range(SUB // PIECE):
        at = slice(r * PIECE, (r + 1) * PIECE)
        xs = [p[at, :].astype(F32) for p in parts]
        total = sum(jnp.sum(v, axis=1, keepdims=True) for v in xs)
        mean = total * (1.0 / D)
        xs = [v - mean for v in xs]
        var = sum(jnp.sum(v * v, axis=1, keepdims=True) for v in xs) * (1.0 / D)
        inv = lax.rsqrt(var + EPS)
        acc = None
        for j, v in enumerate(xs):
            n = (v * inv * gain_ref[pl.ds(info[3] ^ j, 1), :]).astype(BF)
            part = jnp.dot(n, w_ref[j * 256 : (j + 1) * 256, :], preferred_element_type=F32)
            acc = part if acc is None else acc + part
        put(at, silu_of_half(acc * 0.5).astype(BF))


def other_kernel(info, *refs):
    blocks, gain_ref, w_ref = refs[:4], refs[4], refs[5]
    gate_ref, q_ref, kv_ref = refs[6:]

    def put(at, y):
        gate_ref[at, :] = y[:, :128]
        q_ref[at, :] = y[:, 256:384]
        kv_ref[at, :128] = y[:, 384:]
        kv_ref[at, 128:] = y[:, 128:256]

    project_rows(info, blocks, gain_ref, w_ref, put)


def own_kernel(info, *refs):
    blocks, gain_ref, w_ref, q_other = refs[:4], refs[4], refs[5], refs[6]
    gate_ref, kv_ref, q_refs, q_vmem = refs[7], refs[8], refs[9:13], refs[13]
    step = pl.program_id(0)

    def put(at, y):
        gate_ref[at, :] = y[:, :128]
        q_vmem[at, :] = y[:, 256:384]
        kv_ref[at, :128] = y[:, 384:]
        kv_ref[at, 128:] = y[:, 128:256]

    project_rows(info, blocks, gain_ref, w_ref, put)
    for rel, source in ((0, q_vmem), (1, q_other)):
        shift = lax.rem(((2 * rel + step) ^ (2 * info[1])) - info[0] + 4, 4)
        for d in range(4):

            @pl.when(shift == d)
            def _():
                q_refs[d][...] = source[...]


def project_other(info, blocks, gain, w):
    rows = lambda width: pl.BlockSpec((SUB, width), lambda i, s: (i, 0))
    return pl.pallas_call(
        other_kernel,
        grid_spec=pltpu.PrefetchScalarGridSpec(
            num_scalar_prefetch=1,
            grid=(2,),
            in_specs=[rows(256)] * 4 + [whole((4, 256)), whole((D, 4 * HDIM))],
            out_specs=[rows(HDIM), rows(HDIM), rows(2 * HDIM)],
        ),
        out_shape=[
            jax.ShapeDtypeStruct((ROWS, HDIM), BF),
            jax.ShapeDtypeStruct((ROWS, HDIM), BF),
            jax.ShapeDtypeStruct((ROWS, 2 * HDIM), BF),
        ],
        name="project_other",
    )(info, *blocks, gain, w)


def project_own(info, blocks, gain, w, q_other):
    rows = lambda width: pl.BlockSpec((SUB, width), lambda i, s: (i, 0))
    return pl.pallas_call(
        own_kernel,
        grid_spec=pltpu.PrefetchScalarGridSpec(
            num_scalar_prefetch=1,
            grid=(2,),
            in_specs=[rows(256)] * 4 + [whole((4, 256)), whole((D, 4 * HDIM)), rows(HDIM)],
            out_specs=[rows(HDIM), rows(2 * HDIM)] + [whole((SUB, HDIM))] * 4,
            scratch_shapes=[pltpu.VMEM((SUB, HDIM), BF)],
        ),
        out_shape=[
            jax.ShapeDtypeStruct((ROWS, HDIM), BF),
            jax.ShapeDtypeStruct((ROWS, 2 * HDIM), BF),
        ]
        + [jax.ShapeDtypeStruct((SUB, HDIM), BF)] * 4,
        name="project_own",
    )(info, *blocks, gain, w, q_other)


def attend_body(info, q_refs, kv_parts, late, q, kv, acc, full_list, edge_list, sem, more=()):
    z, yl, x = info[0], info[1], info[2]
    copies = list(more)
    for e, ref in q_refs:
        for d in range(4):
            tile = lax.rem(z - d + 4, 4) * 4 + lax.rem(x - e + 4, 4)
            copies.append(
                pltpu.make_async_copy(
                    ref.at[pl.ds(d * SUB, SUB)],
                    q.at[pl.ds(pl.multiple_of(tile * SUB, SUB), SUB)],
                    sem.at[4 * e + d],
                )
            )
    for k, (ref, row, d, rel) in enumerate(kv_parts):
        block = lax.rem(z - d + 4, 4) * 2 + (yl ^ rel)
        copies.append(
            pltpu.make_async_copy(
                ref.at[pl.ds(row, ROWS)],
                kv.at[pl.ds(pl.multiple_of(block * ROWS, ROWS), ROWS)],
                sem.at[16 + k],
            )
        )
    for c in copies:
        c.start()

    def start_of(position):
        s = jnp.int32(0)
        for i in range(8):
            e = info[4 + i]
            s = jnp.maximum(s, jnp.where(e <= position, e, 0))
        return s

    def tiles_upto(position):
        t = position - x * ROWS
        m = lax.div(t, 4 * ROWS)
        r = lax.div(t - m * (4 * ROWS), KEYS)
        count = 3 * m + 1 + jnp.minimum(r, 2)
        return jnp.minimum(jnp.where(t < 0, 0, count), KEY_TILES)

    def query_first(t):
        return ((t >> 2) * 8 + (z >> 1) * 4 + (t & 3)) * ROWS + (z & 1) * SUB

    def key_first_of(n):
        m = lax.div(n, 3)
        return (m * 4 + x) * ROWS + (n - 3 * m) * KEYS

    far_z, far_x = lax.rem(z + 2, 4), lax.rem(x + 2, 4)

    def list_queries(t, counts):
        first = query_first(t)
        begin_last = start_of(first + SUB - 1)
        low = tiles_upto(start_of(first) - KEYS)
        high = tiles_upto(first + SUB - 1)
        if late:
            near = (t & 3) != far_x
            low = jnp.where(near, jnp.maximum(low, far_z * 6), low)
            high = jnp.where(near, jnp.minimum(high, far_z * 6 + 6), high)
        else:
            high = jnp.where((t & 3) == far_x, low, high)

        def list_keys(n, counts):
            nf, ne = counts
            k = key_first_of(n)
            full = ((k + KEYS - 1 <= first) & (k >= begin_last)).astype(jnp.int32)
            use = 1 if late else (lax.div(n, 6) != far_z).astype(jnp.int32)
            entry = t * 32 + n
            full_list[nf] = entry
            edge_list[ne] = entry
            return nf + full * use, ne + (1 - full) * use

        return lax.fori_loop(low, high, list_keys, counts)

    nf, ne = lax.fori_loop(0, TILES, list_queries, (jnp.int32(0), jnp.int32(0)))
    groups = nf >> 2

    def move(i, ne):
        edge_list[ne] = full_list[i]
        return ne + 1

    ne = lax.fori_loop(groups * 4, nf, move, ne)
    edge_list[ne] = 512 + (z * 4 + x) * 32 + z * 6

    for c in copies:
        c.wait()

    def scores(entry):
        t, n = (entry >> 5) & 15, entry & 31
        q_rows = pl.ds(pl.multiple_of(t * SUB, SUB), SUB)
        k_rows = pl.ds(pl.multiple_of(n * KEYS, KEYS), KEYS)
        s = lax.dot_general(
            q[q_rows, :], kv[k_rows, 0:HDIM], (((1,), (1,)), ((), ())), preferred_element_type=F32
        )
        return silu_of_half(s * HALF_SCALE), q_rows, k_rows, t, n

    def add(w, q_rows, k_rows):
        acc[q_rows, :] += jnp.dot(w.astype(BF), kv[k_rows, HDIM:], preferred_element_type=F32)

    def full_tiles(i, carry):
        for u in range(4):
            w, q_rows, k_rows, _, _ = scores(full_list[4 * i + u])
            add(w, q_rows, k_rows)
        return carry

    lax.fori_loop(0, groups, full_tiles, 0)

    def edge_tiles(i, carry):
        for u in range(2):
            entry = edge_list[2 * i + u]
            w, q_rows, k_rows, t, n = scores(entry)
            first = query_first(t)
            col = key_first_of(n) + lax.broadcasted_iota(jnp.int32, (1, KEYS), 1)
            ends = jnp.full((1, KEYS), FAR, jnp.int32)
            for j in range(8):
                e = info[4 + j]
                ends = jnp.minimum(ends, jnp.where(col < e, e, FAR))
            row = lax.broadcasted_iota(jnp.int32, (SUB, KEYS), 0)
            skip = (entry >> 9) * FAR
            allowed = (row >= col + (skip - first)) & (row < ends - first)
            add(jnp.where(allowed, w, 0.0), q_rows, k_rows)
        return carry

    lax.fori_loop(0, (ne + 1) >> 1, edge_tiles, 0)


ATTEND_SCRATCH = [
    pltpu.VMEM((TILES * SUB, HDIM), BF),
    pltpu.VMEM((TILES * SUB, 2 * HDIM), BF),
    pltpu.SMEM((400,), jnp.int32),
    pltpu.SMEM((400,), jnp.int32),
    pltpu.SemaphoreType.DMA((25,)),
]
ANYWHERE = pl.BlockSpec(memory_space=pl.ANY)


def early_kernel(info, *refs):
    q_refs, kv_refs, acc = list(zip((0, 1, 3), refs[:3])), refs[3:9], refs[9]
    q, kv, full_list, edge_list, sem = refs[10:]
    acc[...] = jnp.zeros(acc.shape, F32)
    parts = [(kv_refs[2 * k + r], 0, d, r) for k, d in enumerate((0, 1, 3)) for r in range(2)]
    attend_body(info, q_refs, parts, False, q, kv, acc, full_list, edge_list, sem)


def attend_early(info, queries, keyvals):
    return pl.pallas_call(
        early_kernel,
        grid_spec=pltpu.PrefetchScalarGridSpec(
            num_scalar_prefetch=1,
            grid=(1,),
            in_specs=[ANYWHERE] * 9,
            out_specs=whole((TILES * SUB, HDIM)),
            scratch_shapes=ATTEND_SCRATCH,
        ),
        out_shape=jax.ShapeDtypeStruct((TILES * SUB, HDIM), F32),
        name="attend_early",
    )(info, *queries, *keyvals)


def late_kernel(info, *refs):
    q_refs, kv_refs, acc_in, out = list(zip((0, 1, 3, 2), refs[:4])), refs[4:12], refs[12], refs[13]
    q, kv, full_list, edge_list, sem, acc = refs[14:]
    more = [pltpu.make_async_copy(acc_in, acc, sem.at[24])]
    parts = [(kv_refs[2 * k + r], 0, d, r) for k, d in enumerate((0, 1, 3, 2)) for r in range(2)]
    attend_body(info, q_refs, parts, True, q, kv, acc, full_list, edge_list, sem, more)
    for t in range(TILES):
        out[t] = acc[t * SUB : (t + 1) * SUB, :].astype(BF)


def attend_late(info, queries, keyvals, acc):
    return pl.pallas_call(
        late_kernel,
        grid_spec=pltpu.PrefetchScalarGridSpec(
            num_scalar_prefetch=1,
            grid=(1,),
            in_specs=[ANYWHERE] * 13,
            out_specs=whole((TILES, SUB, HDIM)),
            scratch_shapes=ATTEND_SCRATCH + [pltpu.VMEM((TILES * SUB, HDIM), F32)],
        ),
        out_shape=jax.ShapeDtypeStruct((TILES, SUB, HDIM), BF),
        name="attend_late",
    )(info, *queries, *keyvals, acc)


def gate_kernel(info, part_ref, gate_own, gate_other, own_ref, other_ref):
    ones = jnp.ones((8, HDIM), F32)
    for rel, gate_ref, out in ((0, gate_own, own_ref), (1, gate_other, other_ref)):
        high, low = [], []
        for half in range(2):
            a = (2 * rel + half) ^ (2 * info[1])
            total = part_ref[4 * a].astype(F32)
            for b in range(1, 4):
                total = total + part_ref[4 * a + b].astype(F32)
            at = slice(half * SUB, (half + 1) * SUB)
            out[at, :] = (total * gate_ref[at, :].astype(F32)).astype(BF)
            sums = lax.dot_general(
                ones,
                total * total,
                (((1,), (1,)), ((), ())),
                precision=lax.Precision.HIGHEST,
                preferred_element_type=F32,
            )
            for c in range(SUB // HDIM):
                value = sums[0:1, c * HDIM : (c + 1) * HDIM]
                top = value.astype(BF).astype(F32)
                high.append(top)
                low.append(value - top)
        zero = jnp.zeros((4, HDIM), F32)
        out[ROWS:, :] = jnp.concatenate(high + low + [zero], axis=0).astype(BF)


def gate_rows(info, parts, gate_own, gate_other):
    shape = jax.ShapeDtypeStruct((ROWS + TAIL, HDIM), BF)
    return pl.pallas_call(
        gate_kernel,
        grid_spec=pltpu.PrefetchScalarGridSpec(
            num_scalar_prefetch=1,
            grid=(1,),
            in_specs=[whole((TILES, SUB, HDIM))] + [whole((ROWS, HDIM))] * 2,
            out_specs=[whole((ROWS + TAIL, HDIM))] * 2,
        ),
        out_shape=[shape, shape],
        name="gate_rows",
    )(info, parts, gate_own, gate_other)


def mix_kernel(info, *refs):
    rows, w_here, w_there = refs[:4], refs[4], refs[5]
    mine_ref, theirs_ref, squares_ref = refs[6:]
    core = info[3] & 1
    for out, c in ((theirs_ref, 1 - core), (mine_ref, core)):
        cols = pl.ds(pl.multiple_of(c * 256, 256), 256)
        acc = None
        for r, w, flip in zip(rows, (w_here, w_here, w_there, w_there), (0, 1, 1, 0)):
            at = pl.ds(pl.multiple_of((info[1] ^ flip) * HDIM, HDIM), HDIM)
            part = jnp.dot(r[0:ROWS, :], w[at, cols], preferred_element_type=F32)
            acc = part if acc is None else acc + part
        out[0:ROWS, :] = acc
    tail = sum(r[ROWS:, :].astype(F32) for r in rows)
    squares = jnp.concatenate([tail[0:6] + tail[6:12], jnp.zeros((2, HDIM), F32)], axis=0)
    squares_ref[...] = squares
    theirs_ref[ROWS:, 0:HDIM] = squares
    theirs_ref[ROWS:, HDIM:] = squares


def mix(info, gated, w_here, w_there):
    return pl.pallas_call(
        mix_kernel,
        grid_spec=pltpu.PrefetchScalarGridSpec(
            num_scalar_prefetch=1,
            grid=(1,),
            in_specs=[whole((ROWS + TAIL, HDIM))] * 4 + [whole((256, 512))] * 2,
            out_specs=[whole((ROWS, 256)), whole((ROWS + 8, 256)), whole((8, HDIM))],
        ),
        out_shape=[
            jax.ShapeDtypeStruct((ROWS, 256), F32),
            jax.ShapeDtypeStruct((ROWS + 8, 256), F32),
            jax.ShapeDtypeStruct((8, HDIM), F32),
        ],
        name="mix",
    )(info, *gated, w_here, w_there)


def finish_kernel(mine_ref, got_ref, tail_ref, squares_ref, ev_ref, out_ref):
    step = pl.program_id(0)
    inv = lax.rsqrt((squares_ref[...] + tail_ref[:, 0:HDIM]) * (1.0 / D) + EPS)
    which = lax.broadcasted_iota(jnp.int32, (8, HDIM), 0)
    eye = lax.broadcasted_iota(jnp.int32, (HDIM, HDIM), 0) == lax.broadcasted_iota(jnp.int32, (HDIM, HDIM), 1)
    for k in range(2):
        line = jnp.sum(jnp.where(which == 2 * step + k, inv, 0.0), axis=0, keepdims=True)
        column = jnp.sum(jnp.where(eye, line, 0.0), axis=1, keepdims=True)
        at = slice(k * HDIM, (k + 1) * HDIM)
        total = mine_ref[at, :] + got_ref[at, :]
        out_ref[at, :] = (ev_ref[at, :].astype(F32) + total * column).astype(BF)


def finish(mine, got, squares, events):
    rows = pl.BlockSpec((256, 256), lambda i: (i, 0))
    tail = pl.BlockSpec((8, 256), lambda i: (ROWS // 8, 0))
    return pl.pallas_call(
        finish_kernel,
        grid=(ROWS // 256,),
        in_specs=[rows, rows, tail, pl.BlockSpec((8, HDIM), lambda i: (0, 0)), rows],
        out_specs=rows,
        out_shape=jax.ShapeDtypeStruct((ROWS, 256), BF),
        name="finish",
    )(mine, got, got, squares, events)


def layer(events, norm_gain, w_uvqk, w_out, lengths):
    z, yl, x = (lax.axis_index(a).astype(jnp.int32) for a in ("z", "yl", "x"))
    yh = lax.axis_index("yh").astype(jnp.int32)
    o = yh * 2 + lax.axis_index("core").astype(jnp.int32)
    info = jnp.concatenate([jnp.stack([z, yl, x, o]), jnp.cumsum(lengths).astype(jnp.int32)])

    c0 = flip_core(events)
    p1, p2, p3 = to_p1(events), to_p2(events), to_p3(events)
    w_in = pack_weights(info, w_uvqk.reshape(D, 4 * 256))
    gain = norm_gain.reshape(4, 256)
    p1, w_in, info, gain = lax.optimization_barrier((p1, w_in, info, gain))
    c1, c2, c3 = flip_core(p1), flip_core(p2), flip_core(p3)

    gate_other, q_other, kv_other = project_other(info, (p1, c1, p2, c2), gain, w_in)
    gate_own, kv_own, *pieces = project_own(info, (events, c0, p3, c3), gain, w_in, q_other)

    pieces = [pieces[0]] + [shift_z(pieces[d], d) for d in (1, 2, 3)]
    up_other, down_other = shift_z(kv_other, 1), shift_z(kv_other, -1)
    up_own, down_own = shift_z(kv_own, 1), shift_z(kv_own, -1)

    q_mine = jnp.concatenate(pieces, axis=0)
    queries = [q_mine] + [shift_x(q_mine, e) for e in (1, 3, 2)]
    near, away = shift_z(up_own, 1), shift_z(down_other, -1)

    keyvals = [kv_own, kv_other, up_own, up_other, down_own, down_other]
    acc = attend_early(info, queries[:3], keyvals)
    parts = attend_late(info, queries, keyvals + [near, away], acc)

    w_here = lax.dynamic_slice_in_dim(w_out, yh * 512, 512, 1)
    w_away = lax.dynamic_slice_in_dim(w_out, (1 - yh) * 512, 512, 1)
    w_away, _ = lax.optimization_barrier((w_away, q_mine))
    w_there = to_p3(w_away)

    parts = lax.all_to_all(parts, ("z", "x"), 0, 0)
    own, other = gate_rows(info, parts, gate_own, gate_other)
    gated = [own, to_p1(other), to_p2(other), to_p3(own)]
    mine, theirs, squares = mix(info, gated, w_here, w_there)
    return finish(mine, flip_core(theirs), squares, events)


def solution(mesh):
    fine = Mesh(mesh.devices.reshape(SIZES), AXES)
    ctx, head = ("z", "yl", "x"), ("yh", "core")
    in_specs = (P(ctx, head), P(), P(None, None, head), P(head, None), P())
    return jax.shard_map(layer, mesh=fine, in_specs=in_specs, out_specs=P(ctx, head), check_vma=False)
```

profile of v0, /device:TPU:1, one launch (start us, length us, event | category | flops | bytes accessed | tf_op | source)
XLA Modules:
  0.0 170.1 jit_solution(7069928463647529025)
XLA Ops:
  0.0 2.1 %collective-permute-start = (bf16[768,256]{1,0:T(8,128)(2,1)}, bf16[768,256]{1,0:T(8,128)(2,1)S(1)}, u32[]{:S(2)}, u32[]{:S(2)}) collective-permute-start(bf16[768,256]{1,0:T(8,128)(2,1)} %ev_ref.1), channel_id=1, source_target_pairs={{0,16},{1,17},{2,18},{3,19},{4,20},{5,21},{6,22},{7,23},{8,24},{9,... | collective-permute-start | bytes 1179656 | tf_op jit(solution)/shard_map/ppermute | solution.py:34
  2.1 1.9 %collective-permute-start.5 = (bf16[768,256]{1,0:T(8,128)(2,1)}, bf16[768,256]{1,0:T(8,128)(2,1)S(1)}, u32[]{:S(2)}, u32[]{:S(2)}) collective-permute-start(bf16[768,256]{1,0:T(8,128)(2,1)} %ev_ref.1), channel_id=1, source_target_pairs={{0,18},{1,19},{2,16},{3,17},{4,22},{5,23},{6,20},{7,21},{8,26},{9,... | collective-permute-start | bytes 1179656 | tf_op jit(solution)/shard_map/ppermute | solution.py:34
  4.0 0.7 collective-permute-start.2
  4.7 3.5 %copy.6 = bf16[128,8,4,256]{3,1,2,0:T(8,128)(2,1)} copy(bf16[128,8,4,256]{3,2,1,0:T(4,128)(2,1)} %bitcast.9) | data formatting | bytes 4194304
  8.2 0.6 reshape.35.refs_4_
  8.8 0.2 reduce-window.9
  9.0 0.7 concatenate.6.info
  9.7 3.5 %pack_weights.1.refs_5_ = bf16[1024,512]{1,0:T(8,128)(2,1)} custom-call(s32[12]{0:T(128)} %concatenate.6.info, bf16[1024,1024]{1,0:T(8,128)(2,1)} %bitcast.8), custom_call_target="tpu_custom_call" | custom-call | tf_op jit(solution)/shard_map/pack_weights/pallas_call | solution.py:78
  13.2 0.0 collective-permute-done.refs_0_
  13.2 1.2 collective-permute-start.4
  14.4 5.7 %collective-permute-done.5.refs_2_ = bf16[768,256]{1,0:T(8,128)(2,1)S(1)} collective-permute-done((bf16[768,256]{1,0:T(8,128)(2,1)}, bf16[768,256]{1,0:T(8,128)(2,1)S(1)}, u32[]{:S(2)}, u32[]{:S(2)}) %collective-permute-start.5) | collective-permute-done | bytes 393248 | tf_op jit(solution)/shard_map/ppermute | solution.py:34
  20.1 2.0 %collective-permute-start.6 = (bf16[768,256]{1,0:T(8,128)(2,1)S(1)}, bf16[768,256]{1,0:T(8,128)(2,1)S(1)}, u32[]{:S(2)}, u32[]{:S(2)}) collective-permute-start(bf16[768,256]{1,0:T(8,128)(2,1)S(1)} %collective-permute-done.5.refs_2_), channel_id=1, source_target_pairs={{0,1},{1,0},{2,3},{3,2},{4,5},{5,4},{6,7},{7,6},{8,9},{9,8},{10,11... | collective-permute-start | bytes 1179656 | tf_op jit(solution)/shard_map/ppermute | solution.py:34
  22.1 0.0 collective-permute-start.1
  22.1 1.4 collective-permute-start.3
  23.5 0.0 collective-permute-done.4.refs_1_
  23.5 0.0 collective-permute-done.6.refs_3_
  23.5 0.8 copy-done.19
  24.3 0.7 copy-done.20
  25.0 5.1 %project_other.1 = (bf16[768,128]{1,0:T(8,128)(2,1)}, bf16[768,128]{1,0:T(8,128)(2,1)}, bf16[768,256]{1,0:T(8,128)(2,1)}) custom-call(s32[12]{0:T(128)} %concatenate.6.info, bf16[768,256]{1,0:T(8,128)(2,1)} %copy-done.17, bf16[768,256]{1,0:T(8,128)(2,1)} %copy-done.19, bf16[768,256]{1,0:T(8,128)(2,1)} %copy-done.18, bf16[768,256]{1,0:T(8,128)(2,1)} %copy-done.20, ...), custom_call_target="tpu_custom_call" | custom-call | tf_op jit(solution)/shard_map/project_other/pallas_call | solution.py:144
  30.1 0.0 collective-permute-done.1.refs_1_
  30.1 0.0 copy-start.15
  30.1 0.0 collective-permute-done.3.refs_3_
  30.1 0.7 copy-done.15
  30.8 0.1 copy-done.16
  31.0 5.3 %project_own.1 = (bf16[768,128]{1,0:T(8,128)(2,1)}, bf16[768,256]{1,0:T(8,128)(2,1)}, bf16[384,128]{1,0:T(8,128)(2,1)}, bf16[384,128]{1,0:T(8,128)(2,1)}, bf16[3...) custom-call(s32[12]{0:T(128)} %concatenate.6.info, bf16[768,256]{1,0:T(8,128)(2,1)} %ev_ref.1, bf16[768,256]{1,0:T(8,128)(2,1)} %copy-done.15, ...), custom_call_target="tpu_custom_call" | custom-call | tf_op jit(solution)/shard_map/project_own/pallas_call | solution.py:163
  36.3 1.7 %collective-permute-start.13 = (bf16[768,256]{1,0:T(8,128)(2,1)}, bf16[768,256]{1,0:T(8,128)(2,1)S(1)}, u32[]{:S(2)}, u32[]{:S(2)}) collective-permute-start(bf16[768,256]{1,0:T(8,128)(2,1)} %get-tuple-element.33.refs_3_.refs_4_), channel_id=1, source_target_pairs={{0,32},{1,33},{2,34},{3,35},{4,36},{5,37},{6,38},{7,39},{8,40},{9,... | collective-permute-start | bytes 1179656 | tf_op jit(solution)/shard_map/ppermute | solution.py:34
  38.0 2.2 %collective-permute-start.15 = (bf16[768,256]{1,0:T(8,128)(2,1)}, bf16[768,256]{1,0:T(8,128)(2,1)S(1)}, u32[]{:S(2)}, u32[]{:S(2)}) collective-permute-start(bf16[768,256]{1,0:T(8,128)(2,1)} %get-tuple-element.33.refs_3_.refs_4_), channel_id=1, source_target_pairs={{0,96},{1,97},{2,98},{3,99},{4,100},{5,101},{6,102},{7,103},{8,104... | collective-permute-start | bytes 1179656 | tf_op jit(solution)/shard_map/ppermute | solution.py:34
  40.2 2.7 %collective-permute-start.16 = (bf16[768,256]{1,0:T(8,128)(2,1)S(1)}, bf16[768,256]{1,0:T(8,128)(2,1)S(1)}, u32[]{:S(2)}, u32[]{:S(2)}) collective-permute-start(bf16[768,256]{1,0:T(8,128)(2,1)S(1)} %copy-done.4), channel_id=1, source_target_pairs={{0,96},{1,97},{2,98},{3,99},{4,100},{5,101},{6,102},{7,103},{8,104... | collective-permute-start | bytes 1179656 | tf_op jit(solution)/shard_map/ppermute | solution.py:34
  42.9 0.9 constant_dynamic-update-slice_fusion.3
  43.8 16.5 %collective-permute-done.7 = bf16[384,128]{1,0:T(8,128)(2,1)S(1)} collective-permute-done((bf16[384,128]{1,0:T(8,128)(2,1)}, bf16[384,128]{1,0:T(8,128)(2,1)S(1)}, u32[]{:S(2)}, u32[]{:S(2)}) %collective-permute-start.7) | collective-permute-done | bytes 98336 | tf_op jit(solution)/shard_map/ppermute | solution.py:34
  60.3 1.0 collective-permute-start.8
  61.4 4.1 %collective-permute-done.8 = bf16[384,128]{1,0:T(8,128)(2,1)S(1)} collective-permute-done((bf16[384,128]{1,0:T(8,128)(2,1)}, bf16[384,128]{1,0:T(8,128)(2,1)S(1)}, u32[]{:S(2)}, u32[]{:S(2)}) %collective-permute-start.8) | collective-permute-done | bytes 98336 | tf_op jit(solution)/shard_map/ppermute | solution.py:34
  65.5 1.2 collective-permute-start.9
  66.7 2.5 %collective-permute-done.9 = bf16[384,128]{1,0:T(8,128)(2,1)S(1)} collective-permute-done((bf16[384,128]{1,0:T(8,128)(2,1)}, bf16[384,128]{1,0:T(8,128)(2,1)S(1)}, u32[]{:S(2)}, u32[]{:S(2)}) %collective-permute-start.9) | collective-permute-done | bytes 98336 | tf_op jit(solution)/shard_map/ppermute | solution.py:34
  69.2 0.0 copy-start.2
  69.2 1.3 collective-permute-start.10
  70.5 1.5 collective-permute-start.11
  72.0 1.5 collective-permute-start.12
  73.5 2.7 %collective-permute-start.18 = (bf16[768,256]{1,0:T(8,128)(2,1)S(1)}, bf16[768,256]{1,0:T(8,128)(2,1)S(1)}, u32[]{:S(2)}, u32[]{:S(2)}) collective-permute-start(bf16[768,256]{1,0:T(8,128)(2,1)S(1)} %collective-permute-done.16.refs_8_.refs_9_), channel_id=1, source_target_pairs={{0,96},{1,97},{2,98},{3,99},{4,100},{5,101},{6,102},{7,103},{8,104... | collective-permute-start | bytes 1179656 | tf_op jit(solution)/shard_map/ppermute | solution.py:34
  76.2 2.1 %collective-permute-done.10.refs_1_ = bf16[1536,128]{1,0:T(8,128)(2,1)S(1)} collective-permute-done((bf16[1536,128]{1,0:T(8,128)(2,1)S(1)}, bf16[1536,128]{1,0:T(8,128)(2,1)S(1)}, u32[]{:S(2)}, u32[]{:S(2)}) %collective-permute-start.10) | collective-permute-done | bytes 393248 | tf_op jit(solution)/shard_map/ppermute | solution.py:34
  78.3 0.7 copy-done.9
  79.0 0.7 copy-done.10
  79.8 12.6 %attend_early.1.refs_12_ = f32[6144,128]{1,0:T(8,128)} custom-call(s32[12]{0:T(128)} %concatenate.6.info, bf16[1536,128]{1,0:T(8,128)(2,1)} %copy-done.2, bf16[1536,128]{1,0:T(8,128)(2,1)} %copy-done.9, bf16[1536,128]{1,0:T(8,128)(2,1)} %copy-done.10, bf16[768,256]{1,0:T(8,128)(2,1)} %get-tuple-element.33.refs_3_.refs_4_, ...), custom_call_target="tpu_custom_call" | custom-call | tf_op jit(solution)/shard_map/attend_early/pallas_call | solution.py:324
  92.4 0.7 copy-done.12
  93.1 0.8 copy-done.13
  93.8 15.1 %attend_late.1 = bf16[16,384,128]{2,1,0:T(8,128)(2,1)} custom-call(s32[12]{0:T(128)} %concatenate.6.info, bf16[1536,128]{1,0:T(8,128)(2,1)} %copy-done.2, bf16[1536,128]{1,0:T(8,128)(2,1)} %copy-done.9, bf16[1536,128]{1,0:T(8,128)(2,1)} %copy-done.10, bf16[1536,128]{1,0:T(8,128)(2,1)} %copy-done.12, bf16[768,256]{1,0:T(8,128)(2,1)} %get-tuple-element.33.refs_3_.refs_4_, ...), custom_call_target="tpu_custom_call" | custom-call | tf_op jit(solution)/shard_map/attend_late/pallas_call | solution.py:349
  109.0 0.0 copy-start.11
  109.0 5.0 %all-to-all-start = ((bf16[16,384,128]{2,1,0:T(8,128)(2,1)}), bf16[16,384,128]{2,1,0:T(8,128)(2,1)S(1)}, u32[]{:S(2)}, u32[]{:S(2)}) async-start(bf16[16,384,128]{2,1,0:T(8,128)(2,1)} %attend_late.1), calls=%async_computation | async-start | bytes 3145728 | tf_op jit(solution)/shard_map/all_to_all | solution.py:501
  114.0 0.7 constant_dynamic-slice_fusion
  114.7 1.7 collective-permute-start.22
  116.4 13.7 %all-to-all-done.part_ref = bf16[16,384,128]{2,1,0:T(8,128)(2,1)S(1)} async-done(((bf16[16,384,128]{2,1,0:T(8,128)(2,1)}), bf16[16,384,128]{2,1,0:T(8,128)(2,1)S(1)}, u32[]{:S(2)}, u32[]{:S(2)}) %all-to-all-start) | async-done | bytes 1572896 | tf_op jit(solution)/shard_map/all_to_all | solution.py:501
  130.1 1.2 copy-done
  131.3 3.9 %gate_rows.1 = (bf16[784,128]{1,0:T(8,128)(2,1)}, bf16[784,128]{1,0:T(8,128)(2,1)}) custom-call(s32[12]{0:T(128)} %concatenate.6.info, bf16[16,384,128]{2,1,0:T(8,128)(2,1)} %copy-done, bf16[768,128]{1,0:T(8,128)(2,1)} %get-tuple-element.35.gate_own, bf16[768,128]{1,0:T(8,128)(2,1)} %get-tuple-element.36.gate_other), custom_call_target="tpu_custom_call" | custom-call | tf_op jit(solution)/shard_map/gate_rows/pallas_call | solution.py:392
  135.2 2.2 %collective-permute-start.20 = (bf16[784,128]{1,0:T(8,128)(2,1)}, bf16[784,128]{1,0:T(8,128)(2,1)S(1)}, u32[]{:S(2)}, u32[]{:S(2)}) collective-permute-start(bf16[784,128]{1,0:T(8,128)(2,1)} %get-tuple-element.38), channel_id=1, source_target_pairs={{0,18},{1,19},{2,16},{3,17},{4,22},{5,23},{6,20},{7,21},{8,26},{9,... | collective-permute-start | bytes 602120 | tf_op jit(solution)/shard_map/ppermute | solution.py:34
  137.4 1.2 collective-permute-start.21
  138.6 1.4 collective-permute-done.19.refs_1_
  140.0 2.6 %collective-permute-done.20.refs_2_ = bf16[784,128]{1,0:T(8,128)(2,1)S(1)} collective-permute-done((bf16[784,128]{1,0:T(8,128)(2,1)}, bf16[784,128]{1,0:T(8,128)(2,1)S(1)}, u32[]{:S(2)}, u32[]{:S(2)}) %collective-permute-start.20) | collective-permute-done | bytes 200736 | tf_op jit(solution)/shard_map/ppermute | solution.py:34
  142.5 1.5 collective-permute-done.21.refs_3_
  144.0 0.7 copy-done.24
  144.7 4.2 %mix.1 = (f32[768,256]{1,0:T(8,128)}, f32[776,256]{1,0:T(8,128)}, f32[8,128]{1,0:T(8,128)}) custom-call(s32[12]{0:T(128)} %concatenate.6.info, bf16[784,128]{1,0:T(8,128)(2,1)} %get-tuple-element.37.refs_0_, bf16[784,128]{1,0:T(8,128)(2,1)} %copy-done.22, bf16[784,128]{1,0:T(8,128)(2,1)} %copy-done.23, bf16[784,128]{1,0:T(8,128)(2,1)} %copy-done.24, ...), custom_call_target="tpu_custom_call" | custom-call | tf_op jit(solution)/shard_map/mix/pallas_call | solution.py:425
  148.9 15.0 %collective-permute-start.23 = (f32[776,256]{1,0:T(8,128)}, f32[776,256]{1,0:T(8,128)S(1)}, u32[]{:S(2)}, u32[]{:S(2)}) collective-permute-start(f32[776,256]{1,0:T(8,128)} %get-tuple-element.41), channel_id=1, source_target_pairs={{0,1},{1,0},{2,3},{3,2},{4,5},{5,4},{6,7},{7,6},{8,9},{9,8},{10,11... | collective-permute-start | bytes 2383880 | tf_op jit(solution)/shard_map/ppermute | solution.py:34
  163.9 2.1 %collective-permute-done.23.got_ref.tail_ref = f32[776,256]{1,0:T(8,128)S(1)} collective-permute-done((f32[776,256]{1,0:T(8,128)}, f32[776,256]{1,0:T(8,128)S(1)}, u32[]{:S(2)}, u32[]{:S(2)}) %collective-permute-start.23) | collective-permute-done | bytes 794656 | tf_op jit(solution)/shard_map/ppermute | solution.py:34
  166.0 0.9 copy-done.1
  166.9 3.2 %finish.1 = bf16[768,256]{1,0:T(8,128)(2,1)} custom-call(f32[768,256]{1,0:T(8,128)} %get-tuple-element.40.mine_ref, f32[776,256]{1,0:T(8,128)} %copy-done.1, f32[776,256]{1,0:T(8,128)} %copy-done.1, f32[8,128]{1,0:T(8,128)} %get-tuple-element.42.squares_ref, bf16[768,256]{1,0:T(8,128)(2,1)} %ev_ref.1), custom_call_target="tpu_custom_call" | custom-call | tf_op jit(solution)/shard_map/finish/pallas_call | solution.py:458
  (57 shorter events, 0.2 us)
Async XLA Ops:
  0.0 13.2 %collective-permute-start = (bf16[768,256]{1,0:T(8,128)(2,1)}, bf16[768,256]{1,0:T(8,128)(2,1)S(1)}, u32[]{:S(2)}, u32[]{:S(2)}) collective-permute-start(bf16[768,256]{1,0:T(8,128)(2,1)} %ev_ref.1), channel_id=1, source_target_pairs={{0,16},{1,17},{2,18},{3,19},{4,20},{5,21},{6,22},{7,23},{8,24},{9,... | collective-permute-start | bytes 1179656 | tf_op jit(solution)/shard_map/ppermute | solution.py:34
  2.1 18.0 %collective-permute-start.5 = (bf16[768,256]{1,0:T(8,128)(2,1)}, bf16[768,256]{1,0:T(8,128)(2,1)S(1)}, u32[]{:S(2)}, u32[]{:S(2)}) collective-permute-start(bf16[768,256]{1,0:T(8,128)(2,1)} %ev_ref.1), channel_id=1, source_target_pairs={{0,18},{1,19},{2,16},{3,17},{4,22},{5,23},{6,20},{7,21},{8,26},{9,... | collective-permute-start | bytes 1179656 | tf_op jit(solution)/shard_map/ppermute | solution.py:34
  4.0 18.1 %collective-permute-start.2 = (bf16[768,256]{1,0:T(8,128)(2,1)}, bf16[768,256]{1,0:T(8,128)(2,1)S(1)}, u32[]{:S(2)}, u32[]{:S(2)}) collective-permute-start(bf16[768,256]{1,0:T(8,128)(2,1)} %ev_ref.1), channel_id=1, source_target_pairs={{0,2},{1,3},{2,0},{3,1},{4,6},{5,7},{6,4},{7,5},{8,10},{9,11},{10,... | collective-permute-start | bytes 1179656 | tf_op jit(solution)/shard_map/ppermute | solution.py:34
  4.7 3.5 %copy-start.25 = (f32[1024]{0:T(1024)S(1)}, f32[1024]{0:T(1024)}, u32[]{:S(2)}) copy-start(f32[1024]{0:T(1024)} %param.6) | copy-start | bytes 12292
  4.7 4.1 %copy-start.26 = (s32[8]{0:T(128)S(1)}, s32[8]{0:T(128)}, u32[]{:S(2)}) copy-start(s32[8]{0:T(128)} %param.9) | copy-start | bytes 100
  8.2 13.9 %copy-start.3 = (bf16[768,256]{1,0:T(8,128)(2,1)S(1)}, bf16[768,256]{1,0:T(8,128)(2,1)}, u32[]{:S(2)}) copy-start(bf16[768,256]{1,0:T(8,128)(2,1)} %ev_ref.1) | copy-start | bytes 1179652
  13.2 10.3 %copy-start.17 = (bf16[768,256]{1,0:T(8,128)(2,1)}, bf16[768,256]{1,0:T(8,128)(2,1)S(1)}, u32[]{:S(2)}) copy-start(bf16[768,256]{1,0:T(8,128)(2,1)S(1)} %collective-permute-done.refs_0_) | copy-start | bytes 1179652
  13.2 10.3 %collective-permute-start.4 = (bf16[768,256]{1,0:T(8,128)(2,1)S(1)}, bf16[768,256]{1,0:T(8,128)(2,1)S(1)}, u32[]{:S(2)}, u32[]{:S(2)}) collective-permute-start(bf16[768,256]{1,0:T(8,128)(2,1)S(1)} %collective-permute-done.refs_0_), channel_id=1, source_target_pairs={{0,1},{1,0},{2,3},{3,2},{4,5},{5,4},{6,7},{7,6},{8,9},{9,8},{10,11... | collective-permute-start | bytes 1179656 | tf_op jit(solution)/shard_map/ppermute | solution.py:34
  20.1 3.4 %copy-start.18 = (bf16[768,256]{1,0:T(8,128)(2,1)}, bf16[768,256]{1,0:T(8,128)(2,1)S(1)}, u32[]{:S(2)}) copy-start(bf16[768,256]{1,0:T(8,128)(2,1)S(1)} %collective-permute-done.5.refs_2_) | copy-start | bytes 1179652
  20.1 3.4 %collective-permute-start.6 = (bf16[768,256]{1,0:T(8,128)(2,1)S(1)}, bf16[768,256]{1,0:T(8,128)(2,1)S(1)}, u32[]{:S(2)}, u32[]{:S(2)}) collective-permute-start(bf16[768,256]{1,0:T(8,128)(2,1)S(1)} %collective-permute-done.5.refs_2_), channel_id=1, source_target_pairs={{0,1},{1,0},{2,3},{3,2},{4,5},{5,4},{6,7},{7,6},{8,9},{9,8},{10,11... | collective-permute-start | bytes 1179656 | tf_op jit(solution)/shard_map/ppermute | solution.py:34
  22.1 8.0 %collective-permute-start.1 = (bf16[768,256]{1,0:T(8,128)(2,1)S(1)}, bf16[768,256]{1,0:T(8,128)(2,1)S(1)}, u32[]{:S(2)}, u32[]{:S(2)}) collective-permute-start(bf16[768,256]{1,0:T(8,128)(2,1)S(1)} %copy-done.3), channel_id=1, source_target_pairs={{0,1},{1,0},{2,3},{3,2},{4,5},{5,4},{6,7},{7,6},{8,9},{9,8},{10,11... | collective-permute-start | bytes 1179656 | tf_op jit(solution)/shard_map/ppermute | solution.py:34
  22.1 8.0 %copy-start.14 = (bf16[768,256]{1,0:T(8,128)(2,1)}, bf16[768,256]{1,0:T(8,128)(2,1)S(1)}, u32[]{:S(2)}) copy-start(bf16[768,256]{1,0:T(8,128)(2,1)S(1)} %collective-permute-done.2.refs_2_) | copy-start | bytes 1179652
  22.1 8.0 %collective-permute-start.3 = (bf16[768,256]{1,0:T(8,128)(2,1)S(1)}, bf16[768,256]{1,0:T(8,128)(2,1)S(1)}, u32[]{:S(2)}, u32[]{:S(2)}) collective-permute-start(bf16[768,256]{1,0:T(8,128)(2,1)S(1)} %collective-permute-done.2.refs_2_), channel_id=1, source_target_pairs={{0,1},{1,0},{2,3},{3,2},{4,5},{5,4},{6,7},{7,6},{8,9},{9,8},{10,11... | collective-permute-start | bytes 1179656 | tf_op jit(solution)/shard_map/ppermute | solution.py:34
  23.5 0.8 copy-start.19
  24.3 0.7 copy-start.20
  30.1 10.1 %copy-start.4 = (bf16[768,256]{1,0:T(8,128)(2,1)S(1)}, bf16[768,256]{1,0:T(8,128)(2,1)}, u32[]{:S(2)}) copy-start(bf16[768,256]{1,0:T(8,128)(2,1)} %get-tuple-element.34.refs_4_.refs_5_) | copy-start | bytes 1179652
  30.1 0.7 copy-start.15
  30.1 0.9 copy-start.16
  36.3 34.2 %collective-permute-start.13 = (bf16[768,256]{1,0:T(8,128)(2,1)}, bf16[768,256]{1,0:T(8,128)(2,1)S(1)}, u32[]{:S(2)}, u32[]{:S(2)}) collective-permute-start(bf16[768,256]{1,0:T(8,128)(2,1)} %get-tuple-element.33.refs_3_.refs_4_), channel_id=1, source_target_pairs={{0,32},{1,33},{2,34},{3,35},{4,36},{5,37},{6,38},{7,39},{8,40},{9,... | collective-permute-start | bytes 1179656 | tf_op jit(solution)/shard_map/ppermute | solution.py:34
  38.0 34.0 %collective-permute-start.15 = (bf16[768,256]{1,0:T(8,128)(2,1)}, bf16[768,256]{1,0:T(8,128)(2,1)S(1)}, u32[]{:S(2)}, u32[]{:S(2)}) collective-permute-start(bf16[768,256]{1,0:T(8,128)(2,1)} %get-tuple-element.33.refs_3_.refs_4_), channel_id=1, source_target_pairs={{0,96},{1,97},{2,98},{3,99},{4,100},{5,101},{6,102},{7,103},{8,104... | collective-permute-start | bytes 1179656 | tf_op jit(solution)/shard_map/ppermute | solution.py:34
  40.2 33.3 %collective-permute-start.14 = (bf16[768,256]{1,0:T(8,128)(2,1)S(1)}, bf16[768,256]{1,0:T(8,128)(2,1)S(1)}, u32[]{:S(2)}, u32[]{:S(2)}) collective-permute-start(bf16[768,256]{1,0:T(8,128)(2,1)S(1)} %copy-done.4), channel_id=1, source_target_pairs={{0,32},{1,33},{2,34},{3,35},{4,36},{5,37},{6,38},{7,39},{8,40},{9,... | collective-permute-start | bytes 1179656 | tf_op jit(solution)/shard_map/ppermute | solution.py:34
  40.2 33.3 %collective-permute-start.16 = (bf16[768,256]{1,0:T(8,128)(2,1)S(1)}, bf16[768,256]{1,0:T(8,128)(2,1)S(1)}, u32[]{:S(2)}, u32[]{:S(2)}) collective-permute-start(bf16[768,256]{1,0:T(8,128)(2,1)S(1)} %copy-done.4), channel_id=1, source_target_pairs={{0,96},{1,97},{2,98},{3,99},{4,100},{5,101},{6,102},{7,103},{8,104... | collective-permute-start | bytes 1179656 | tf_op jit(solution)/shard_map/ppermute | solution.py:34
  42.9 17.4 %collective-permute-start.7 = (bf16[384,128]{1,0:T(8,128)(2,1)}, bf16[384,128]{1,0:T(8,128)(2,1)S(1)}, u32[]{:S(2)}, u32[]{:S(2)}) collective-permute-start(bf16[384,128]{1,0:T(8,128)(2,1)} %get-tuple-element.30), channel_id=1, source_target_pairs={{0,32},{1,33},{2,34},{3,35},{4,36},{5,37},{6,38},{7,39},{8,40},{9,... | collective-permute-start | bytes 294920 | tf_op jit(solution)/shard_map/ppermute | solution.py:34
  60.3 5.2 %collective-permute-start.8 = (bf16[384,128]{1,0:T(8,128)(2,1)}, bf16[384,128]{1,0:T(8,128)(2,1)S(1)}, u32[]{:S(2)}, u32[]{:S(2)}) collective-permute-start(bf16[384,128]{1,0:T(8,128)(2,1)} %get-tuple-element.31), channel_id=1, source_target_pairs={{0,64},{1,65},{2,66},{3,67},{4,68},{5,69},{6,70},{7,71},{8,72},{9,... | collective-permute-start | bytes 294920 | tf_op jit(solution)/shard_map/ppermute | solution.py:34
  65.5 3.7 %collective-permute-start.9 = (bf16[384,128]{1,0:T(8,128)(2,1)}, bf16[384,128]{1,0:T(8,128)(2,1)S(1)}, u32[]{:S(2)}, u32[]{:S(2)}) collective-permute-start(bf16[384,128]{1,0:T(8,128)(2,1)} %get-tuple-element.32), channel_id=1, source_target_pairs={{0,96},{1,97},{2,98},{3,99},{4,100},{5,101},{6,102},{7,103},{8,104... | collective-permute-start | bytes 294920 | tf_op jit(solution)/shard_map/ppermute | solution.py:34
  69.2 9.1 %copy-start.2 = (bf16[1536,128]{1,0:T(8,128)(2,1)}, bf16[1536,128]{1,0:T(8,128)(2,1)S(1)}, u32[]{:S(2)}) copy-start(bf16[1536,128]{1,0:T(8,128)(2,1)S(1)} %constant_dynamic-update-slice_fusion.refs_0_) | copy-start | bytes 1179652
  69.2 9.0 %collective-permute-start.10 = (bf16[1536,128]{1,0:T(8,128)(2,1)S(1)}, bf16[1536,128]{1,0:T(8,128)(2,1)S(1)}, u32[]{:S(2)}, u32[]{:S(2)}) collective-permute-start(bf16[1536,128]{1,0:T(8,128)(2,1)S(1)} %constant_dynamic-update-slice_fusion.refs_0_), channel_id=1, source_target_pairs={{0,4},{1,5},{2,6},{3,7},{4,8},{5,9},{6,10},{7,11},{8,12},{9,13},{1... | collective-permute-start | bytes 1179656 | tf_op jit(solution)/shard_map/ppermute | solution.py:34
  70.5 7.8 %copy-start.5 = (bf16[768,256]{1,0:T(8,128)(2,1)}, bf16[768,256]{1,0:T(8,128)(2,1)S(1)}, u32[]{:S(2)}) copy-start(bf16[768,256]{1,0:T(8,128)(2,1)S(1)} %collective-permute-done.13.refs_5_.refs_6_) | copy-start | bytes 1179652
  70.5 7.8 %collective-permute-start.11 = (bf16[1536,128]{1,0:T(8,128)(2,1)S(1)}, bf16[1536,128]{1,0:T(8,128)(2,1)S(1)}, u32[]{:S(2)}, u32[]{:S(2)}) collective-permute-start(bf16[1536,128]{1,0:T(8,128)(2,1)S(1)} %constant_dynamic-update-slice_fusion.refs_0_), channel_id=1, source_target_pairs={{0,12},{1,13},{2,14},{3,15},{4,0},{5,1},{6,2},{7,3},{8,4},{9,5},{1... | collective-permute-start | bytes 1179656 | tf_op jit(solution)/shard_map/ppermute | solution.py:34
  72.0 6.3 %copy-start.6 = (bf16[768,256]{1,0:T(8,128)(2,1)}, bf16[768,256]{1,0:T(8,128)(2,1)S(1)}, u32[]{:S(2)}) copy-start(bf16[768,256]{1,0:T(8,128)(2,1)S(1)} %collective-permute-done.15.refs_7_.refs_8_) | copy-start | bytes 1179652
  72.0 20.4 %collective-permute-start.12 = (bf16[1536,128]{1,0:T(8,128)(2,1)S(1)}, bf16[1536,128]{1,0:T(8,128)(2,1)S(1)}, u32[]{:S(2)}, u32[]{:S(2)}) collective-permute-start(bf16[1536,128]{1,0:T(8,128)(2,1)S(1)} %constant_dynamic-update-slice_fusion.refs_0_), channel_id=1, source_target_pairs={{0,8},{1,9},{2,10},{3,11},{4,12},{5,13},{6,14},{7,15},{8,0},{9,1},... | collective-permute-start | bytes 1179656 | tf_op jit(solution)/shard_map/ppermute | solution.py:34
  73.5 4.8 %copy-start.7 = (bf16[768,256]{1,0:T(8,128)(2,1)}, bf16[768,256]{1,0:T(8,128)(2,1)S(1)}, u32[]{:S(2)}) copy-start(bf16[768,256]{1,0:T(8,128)(2,1)S(1)} %collective-permute-done.14.refs_6_.refs_7_) | copy-start | bytes 1179652
  73.5 18.8 %collective-permute-start.17 = (bf16[768,256]{1,0:T(8,128)(2,1)S(1)}, bf16[768,256]{1,0:T(8,128)(2,1)}, u32[]{:S(2)}, u32[]{:S(2)}) collective-permute-start(bf16[768,256]{1,0:T(8,128)(2,1)S(1)} %collective-permute-done.13.refs_5_.refs_6_), channel_id=1, source_target_pairs={{0,32},{1,33},{2,34},{3,35},{4,36},{5,37},{6,38},{7,39},{8,40},{9,... | collective-permute-start | bytes 1179656 | tf_op jit(solution)/shard_map/ppermute | solution.py:34
  73.5 4.8 %copy-start.8 = (bf16[768,256]{1,0:T(8,128)(2,1)}, bf16[768,256]{1,0:T(8,128)(2,1)S(1)}, u32[]{:S(2)}) copy-start(bf16[768,256]{1,0:T(8,128)(2,1)S(1)} %collective-permute-done.16.refs_8_.refs_9_) | copy-start | bytes 1179652
  73.5 18.8 %collective-permute-start.18 = (bf16[768,256]{1,0:T(8,128)(2,1)S(1)}, bf16[768,256]{1,0:T(8,128)(2,1)S(1)}, u32[]{:S(2)}, u32[]{:S(2)}) collective-permute-start(bf16[768,256]{1,0:T(8,128)(2,1)S(1)} %collective-permute-done.16.refs_8_.refs_9_), channel_id=1, source_target_pairs={{0,96},{1,97},{2,98},{3,99},{4,100},{5,101},{6,102},{7,103},{8,104... | collective-permute-start | bytes 1179656 | tf_op jit(solution)/shard_map/ppermute | solution.py:34
  78.3 0.7 copy-start.9
  79.0 0.8 copy-start.10
  92.3 0.8 copy-start.12
  93.1 0.8 copy-start.13
  109.0 5.0 %copy-start.11 = (bf16[256,1024]{1,0:T(8,128)(2,1)S(1)}, bf16[256,1024]{1,0:T(8,128)(2,1)}, u32[]{:S(2)}) copy-start(bf16[256,1024]{1,0:T(8,128)(2,1)} %param.8) | copy-start | bytes 1572868
  109.0 21.2 %all-to-all-start = ((bf16[16,384,128]{2,1,0:T(8,128)(2,1)}), bf16[16,384,128]{2,1,0:T(8,128)(2,1)S(1)}, u32[]{:S(2)}, u32[]{:S(2)}) async-start(bf16[16,384,128]{2,1,0:T(8,128)(2,1)} %attend_late.1), calls=%async_computation | async-start | bytes 3145728 | tf_op jit(solution)/shard_map/all_to_all | solution.py:501
  114.7 23.8 %collective-permute-start.22 = (bf16[256,512]{1,0:T(8,128)(2,1)S(1)}, bf16[256,512]{1,0:T(8,128)(2,1)S(1)}, u32[]{:S(2)}, u32[]{:S(2)}) collective-permute-start(bf16[256,512]{1,0:T(8,128)(2,1)S(1)} %get-tuple-element.39), channel_id=1, source_target_pairs={{0,2},{1,3},{2,0},{3,1},{4,6},{5,7},{6,4},{7,5},{8,10},{9,11},{10,... | collective-permute-start | bytes 786440 | tf_op jit(solution)/shard_map/ppermute | solution.py:34
  130.1 1.2 copy-start
  135.2 4.8 %collective-permute-start.19 = (bf16[784,128]{1,0:T(8,128)(2,1)}, bf16[784,128]{1,0:T(8,128)(2,1)S(1)}, u32[]{:S(2)}, u32[]{:S(2)}) collective-permute-start(bf16[784,128]{1,0:T(8,128)(2,1)} %get-tuple-element.38), channel_id=1, source_target_pairs={{0,16},{1,17},{2,18},{3,19},{4,20},{5,21},{6,22},{7,23},{8,24},{9,... | collective-permute-start | bytes 602120 | tf_op jit(solution)/shard_map/ppermute | solution.py:34
  135.2 7.3 %collective-permute-start.20 = (bf16[784,128]{1,0:T(8,128)(2,1)}, bf16[784,128]{1,0:T(8,128)(2,1)S(1)}, u32[]{:S(2)}, u32[]{:S(2)}) collective-permute-start(bf16[784,128]{1,0:T(8,128)(2,1)} %get-tuple-element.38), channel_id=1, source_target_pairs={{0,18},{1,19},{2,16},{3,17},{4,22},{5,23},{6,20},{7,21},{8,26},{9,... | collective-permute-start | bytes 602120 | tf_op jit(solution)/shard_map/ppermute | solution.py:34
  137.4 6.6 %collective-permute-start.21 = (bf16[784,128]{1,0:T(8,128)(2,1)}, bf16[784,128]{1,0:T(8,128)(2,1)S(1)}, u32[]{:S(2)}, u32[]{:S(2)}) collective-permute-start(bf16[784,128]{1,0:T(8,128)(2,1)} %get-tuple-element.37.refs_0_), channel_id=1, source_target_pairs={{0,2},{1,3},{2,0},{3,1},{4,6},{5,7},{6,4},{7,5},{8,10},{9,11},{10,... | collective-permute-start | bytes 602120 | tf_op jit(solution)/shard_map/ppermute | solution.py:34
  138.6 5.5 %copy-start.21 = (bf16[256,512]{1,0:T(8,128)(2,1)}, bf16[256,512]{1,0:T(8,128)(2,1)S(1)}, u32[]{:S(2)}) copy-start(bf16[256,512]{1,0:T(8,128)(2,1)S(1)} %collective-permute-done.22.refs_5_) | copy-start | bytes 786436
  140.0 4.1 %copy-start.22 = (bf16[784,128]{1,0:T(8,128)(2,1)}, bf16[784,128]{1,0:T(8,128)(2,1)S(1)}, u32[]{:S(2)}) copy-start(bf16[784,128]{1,0:T(8,128)(2,1)S(1)} %collective-permute-done.19.refs_1_) | copy-start | bytes 602116
  142.5 1.5 copy-start.23
  144.0 0.7 copy-start.24
  148.9 17.1 %collective-permute-start.23 = (f32[776,256]{1,0:T(8,128)}, f32[776,256]{1,0:T(8,128)S(1)}, u32[]{:S(2)}, u32[]{:S(2)}) collective-permute-start(f32[776,256]{1,0:T(8,128)} %get-tuple-element.41), channel_id=1, source_target_pairs={{0,1},{1,0},{2,3},{3,2},{4,5},{5,4},{6,7},{7,6},{8,9},{9,8},{10,11... | collective-permute-start | bytes 2383880 | tf_op jit(solution)/shard_map/ppermute | solution.py:34
  166.0 0.9 copy-start.1
where the time goes:
time: 171 us; the launch traced here: 170 us
  Pallas kernels  52.8 us (31%)
  waiting for transfers between devices  52.3 us (31%)
  starting transfers between devices  50.1 us (29%)
  local copies, waits for them, and re-layouts  14.5 us (8%)
    ppermute x24, starting transfers between devices, send(): return lax.ppermute(array, AXES, pairs)  45.1 us
    ppermute x24, waiting for transfers between devices, send(): return lax.ppermute(array, AXES, pairs)  38.6 us
    pallas_call x1, Pallas kernels, attend_late(): pl.pallas_call(late_kernel, grid_spec=pltpu.PrefetchScalarGridSpec(num_sc...  15.1 us
    all_to_all x1, waiting for transfers between devices, layer(): parts = lax.all_to_all(parts, ('z', 'x'), 0, 0)  13.7 us
    pallas_call x1, Pallas kernels, attend_early(): pl.pallas_call(early_kernel, grid_spec=pltpu.PrefetchScalarGridSpec(num_s...  12.6 us
    unnamed x58, local copies, waits for them, and re-layouts  12.5 us
    pallas_call x1, Pallas kernels, project_own(): pl.pallas_call(own_kernel, grid_spec=pltpu.PrefetchScalarGridSpec(num_sca...  5.31 us
    pallas_call x1, Pallas kernels, project_other(): pl.pallas_call(other_kernel, grid_spec=pltpu.PrefetchScalarGridSpec(num_s...  5.05 us
  transfers between devices with their start and end apart: 25, of which 10 were waited for; matrix products, arithmetic and copies ran while one was open for 4% of the time, Pallas kernels for 15%

commit v1 on v0

v1 whole, which is shorter than its diff:
```python
import functools

import jax
import jax.numpy as jnp
import numpy as np
from jax import lax
from jax.experimental import pallas as pl
from jax.experimental.pallas import tpu as pltpu
from jax.sharding import Mesh
from jax.sharding import PartitionSpec as P


D = 1024
HDIM = 128
ROWS = 768
SUB = 384
TILES = 16
KEYS = 256
KEY_TILES = 24
TAIL = 16
EPS = 1e-05
AXES = ("z", "yl", "x", "yh", "core")
SIZES = (4, 2, 4, 2, 2)
HALF_SCALE = 0.5 * HDIM ** (-0.5)
FAR = 1 << 24
BF = jnp.bfloat16
F32 = jnp.float32


def send(array, target):
    pairs = []
    for source in range(int(np.prod(SIZES))):
        place = np.unravel_index(source, SIZES)
        dest = [int(t) % n for t, n in zip(target(*[int(p) for p in place]), SIZES)]
        pairs.append((source, int(np.ravel_multi_index(dest, SIZES))))
    return lax.ppermute(array, AXES, pairs)


def flip_core(array):
    return send(array, lambda z, yl, x, yh, c: (z, yl, x, yh, 1 - c))


def to_p1(array):
    return send(array, lambda z, yl, x, yh, c: (z, 1 - yl, x, yh, c))


def to_p2(array):
    return send(array, lambda z, yl, x, yh, c: (z, 1 - yl, x, 1 - yh, c))


def to_p3(array):
    return send(array, lambda z, yl, x, yh, c: (z, yl, x, 1 - yh, c))


def shift_z(array, d):
    return send(array, lambda z, yl, x, yh, c: (z + d, yl, x, yh, c))


def shift_x(array, d):
    return send(array, lambda z, yl, x, yh, c: (z, yl, x + d, yh, c))


def silu_of_half(h):
    return h + h * jnp.tanh(h)


ANYWHERE = pl.BlockSpec(memory_space=pl.ANY)


def whole(shape):
    return pl.BlockSpec(shape, lambda i, *s: (0,) * len(shape))


PIECE = 128


def half_kernel(second, info, *refs):
    blocks, gain_ref, w_ref = refs[:4], refs[4], refs[5]
    if second:
        q_first, outs = refs[6], refs[11:]
    else:
        outs = refs[6:]
    gate_mine, gate_away, kv_mine, kv_away = outs[:4]
    q_refs, y = outs[4:-1], outs[-1]
    for r in range(SUB // PIECE):
        at = slice(r * PIECE, (r + 1) * PIECE)
        xs = [p[at, :].astype(F32) for p in blocks]
        total = sum(jnp.sum(v, axis=1, keepdims=True) for v in xs)
        mean = total * (1.0 / D)
        xs = [v - mean for v in xs]
        var = sum(jnp.sum(v * v, axis=1, keepdims=True) for v in xs) * (1.0 / D)
        inv = lax.rsqrt(var + EPS)
        acc = None
        for j, v in enumerate(xs):
            n = (v * inv * gain_ref[pl.ds(info[3] ^ j, 1), :]).astype(BF)
            w = w_ref[pl.ds(pl.multiple_of((info[3] ^ j) * 256, 256), 256), :]
            part = jnp.dot(n, w, preferred_element_type=F32)
            acc = part if acc is None else acc + part
        y[at, :] = silu_of_half(acc * 0.5).astype(BF)

    def columns(group, head):
        return y[:, pl.ds(pl.multiple_of(group * 256 + head * HDIM, HDIM), HDIM)]

    for gate, kv, head in ((gate_mine, kv_mine, info[1]), (gate_away, kv_away, 1 - info[1])):
        gate[...] = columns(0, head)
        kv[:, :HDIM] = columns(3, head)
        kv[:, HDIM:] = columns(1, head)
    if not second:
        for head in range(2):
            q_refs[0][head] = columns(2, head)
        return
    for half in range(2):
        for head in range(2):
            turn = info[0] ^ (2 * half + head)
            for k in range(4):

                @pl.when(turn == k)
                def _():
                    q_refs[k][...] = columns(2, head) if half else q_first[head]


def project_half(info, half, blocks, gain, w, before=()):
    part = lambda width: pl.BlockSpec((SUB, width), lambda i, s: (half, 0))
    full = lambda width: jax.ShapeDtypeStruct((ROWS, width), BF)
    widths = (HDIM, HDIM, 2 * HDIM, 2 * HDIM)
    in_specs = [part(256)] * 2 + [whole((SUB, 256))] * 2 + [whole((4, 256)), whole((D, D))]
    if half:
        in_specs = in_specs + [whole((2, SUB, HDIM))] + [ANYWHERE] * 4
        q_specs, q_shape = [whole((SUB, HDIM))] * 4, [jax.ShapeDtypeStruct((SUB, HDIM), BF)] * 4
        before = [before[4], *before[:4]]
    else:
        q_specs, q_shape = [whole((2, SUB, HDIM))], [jax.ShapeDtypeStruct((2, SUB, HDIM), BF)]
    return pl.pallas_call(
        functools.partial(half_kernel, bool(half)),
        grid_spec=pltpu.PrefetchScalarGridSpec(
            num_scalar_prefetch=1,
            grid=(1,),
            in_specs=in_specs,
            out_specs=[part(n) for n in widths] + q_specs,
            scratch_shapes=[pltpu.VMEM((SUB, D), BF)],
        ),
        out_shape=[full(n) for n in widths] + q_shape,
        input_output_aliases={8 + i: i for i in range(4)} if half else {},
        name="project_second" if half else "project_first",
    )(info, *blocks, gain, w, *before)


LIST = 416


def plan_kernel(info, full_early, edge_early, full_late, edge_late):
    z, yl, x = info[0], info[1], info[2]
    far_z, far_x = lax.rem(z + 2, 4), lax.rem(x + 2, 4)

    def start_of(position):
        s = jnp.int32(0)
        for i in range(8):
            e = info[4 + i]
            s = jnp.maximum(s, jnp.where(e <= position, e, 0))
        return s

    def tiles_upto(position):
        t = position - x * ROWS
        m = lax.div(t, 4 * ROWS)
        r = lax.div(t - m * (4 * ROWS), KEYS)
        count = 3 * m + 1 + jnp.minimum(r, 2)
        return jnp.minimum(jnp.where(t < 0, 0, count), KEY_TILES)

    def list_queries(t, counts):
        first = query_first(info, t)
        begin_last = start_of(first + SUB - 1)
        low = tiles_upto(start_of(first) - KEYS)
        high = tiles_upto(first + SUB - 1)
        near = (t & 3) != far_x

        def list_keys(n, counts):
            fe, ee, fl, el = counts
            k = key_first(info, n)
            block = lax.div(n, 3)
            bz, rel = block >> 1, (block & 1) ^ yl
            early = near & (((rel == 0) & (bz != far_z)) | (bz == z))
            full = (k + KEYS - 1 <= first) & (k >= begin_last)
            entry = t * 32 + n
            full_early[fe] = entry
            edge_early[ee] = entry
            full_late[fl] = entry
            edge_late[el] = entry
            early, full = early.astype(jnp.int32), full.astype(jnp.int32)
            return (
                fe + early * full,
                ee + early * (1 - full),
                fl + (1 - early) * full,
                el + (1 - early) * (1 - full),
            )

        return lax.fori_loop(low, high, list_keys, counts)

    zero = jnp.int32(0)
    fe, ee, fl, el = lax.fori_loop(0, TILES, list_queries, (zero, zero, zero, zero))
    for fulls, nf, edges, ne in ((full_early, fe, edge_early, ee), (full_late, fl, edge_late, el)):
        groups = nf >> 2

        def move(i, ne):
            edges[ne] = fulls[i]
            return ne + 1

        ne = lax.fori_loop(groups * 4, nf, move, ne)
        edges[ne] = 512 + (z * 4 + x) * 32 + z * 6 + 3 * yl
        fulls[LIST - 1] = groups
        edges[LIST - 1] = (ne + 1) >> 1


def query_first(info, t):
    return ((t >> 2) * 8 + (info[0] >> 1) * 4 + (t & 3)) * ROWS + (info[0] & 1) * SUB


def key_first(info, n):
    m = lax.div(n, 3)
    return (m * 4 + info[2]) * ROWS + (n - 3 * m) * KEYS


def plan(info):
    smem = pl.BlockSpec(memory_space=pltpu.SMEM)
    return pl.pallas_call(
        plan_kernel,
        grid_spec=pltpu.PrefetchScalarGridSpec(num_scalar_prefetch=1, grid=(1,), in_specs=[], out_specs=[smem] * 4),
        out_shape=[jax.ShapeDtypeStruct((LIST,), jnp.int32)] * 4,
        name="plan",
    )(info)


def attend_kernel(info, *refs):
    lists, q_refs, kv_refs, out = refs[:4], refs[4:8], refs[8:16], refs[16]
    q, kv, acc, sem = refs[17:]
    z, yl, x = info[0], info[1], info[2]

    def load_queries(e, ref):
        copies = []
        for k in range(4):
            tile = ((2 * (z & 1) + yl) ^ k) * 4 + lax.rem(x - e + 4, 4)
            copies.append(
                pltpu.make_async_copy(
                    ref.at[pl.ds(k * SUB, SUB)],
                    q.at[pl.ds(pl.multiple_of(tile * SUB, SUB), SUB)],
                    sem.at[4 * e + k],
                )
            )
        return copies

    def load_keys(k, ref, d, rel):
        block = lax.rem(z - d + 4, 4) * 2 + (yl ^ rel)
        to = kv.at[pl.ds(pl.multiple_of(block * ROWS, ROWS), ROWS)]
        return [pltpu.make_async_copy(ref, to, sem.at[16 + k])]

    queries = [load_queries(e, ref) for e, ref in zip((0, 1, 3, 2), q_refs)]
    places = zip(kv_refs, (0, 0, 1, 3, 1, 3, 2, 2), (0, 1, 0, 0, 1, 1, 0, 1))
    keys = [load_keys(k, *place) for k, place in enumerate(places)]
    early, late = sum(keys[:4] + queries[:3], []), sum(keys[4:] + queries[3:], [])
    for c in early + late:
        c.start()
    acc[...] = jnp.zeros(acc.shape, F32)
    for c in early:
        c.wait()

    def scores(entry):
        t, n = (entry >> 5) & 15, entry & 31
        q_rows = pl.ds(pl.multiple_of(t * SUB, SUB), SUB)
        k_rows = pl.ds(pl.multiple_of(n * KEYS, KEYS), KEYS)
        s = lax.dot_general(
            q[q_rows, :], kv[k_rows, 0:HDIM], (((1,), (1,)), ((), ())), preferred_element_type=F32
        )
        return silu_of_half(s * HALF_SCALE), q_rows, k_rows, t, n

    def add(w, q_rows, k_rows):
        acc[q_rows, :] += jnp.dot(w.astype(BF), kv[k_rows, HDIM:], preferred_element_type=F32)

    def run(full_list, edge_list):
        def full_tiles(i, carry):
            for u in range(4):
                w, q_rows, k_rows, _, _ = scores(full_list[4 * i + u])
                add(w, q_rows, k_rows)
            return carry

        lax.fori_loop(0, full_list[LIST - 1], full_tiles, 0)

        def edge_tiles(i, carry):
            for u in range(2):
                entry = edge_list[2 * i + u]
                w, q_rows, k_rows, t, n = scores(entry)
                first = query_first(info, t)
                col = key_first(info, n) + lax.broadcasted_iota(jnp.int32, (1, KEYS), 1)
                ends = jnp.full((1, KEYS), FAR, jnp.int32)
                for j in range(8):
                    e = info[4 + j]
                    ends = jnp.minimum(ends, jnp.where(col < e, e, FAR))
                row = lax.broadcasted_iota(jnp.int32, (SUB, KEYS), 0)
                skip = (entry >> 9) * FAR
                allowed = (row >= col + (skip - first)) & (row < ends - first)
                add(jnp.where(allowed, w, 0.0), q_rows, k_rows)
            return carry

        lax.fori_loop(0, edge_list[LIST - 1], edge_tiles, 0)

    run(lists[0], lists[1])
    for c in late:
        c.wait()
    run(lists[2], lists[3])
    for t in range(TILES):
        out[t] = acc[t * SUB : (t + 1) * SUB, :].astype(BF)


def attend(info, lists, queries, keyvals):
    return pl.pallas_call(
        attend_kernel,
        grid_spec=pltpu.PrefetchScalarGridSpec(
            num_scalar_prefetch=5,
            grid=(1,),
            in_specs=[ANYWHERE] * 12,
            out_specs=whole((TILES, SUB, HDIM)),
            scratch_shapes=[
                pltpu.VMEM((TILES * SUB, HDIM), BF),
                pltpu.VMEM((TILES * SUB, 2 * HDIM), BF),
                pltpu.VMEM((TILES * SUB, HDIM), F32),
                pltpu.SemaphoreType.DMA((24,)),
            ],
        ),
        out_shape=jax.ShapeDtypeStruct((TILES, SUB, HDIM), BF),
        name="attend",
    )(info, *lists, *queries, *keyvals)


def gate_kernel(info, part_ref, gate_mine, gate_other, own_ref, other_ref):
    step = pl.program_id(0)
    total = part_ref[0].astype(F32)
    for b in range(1, 4):
        total = total + part_ref[b].astype(F32)
    sums = lax.dot_general(
        jnp.ones((8, HDIM), F32),
        total * total,
        (((1,), (1,)), ((), ())),
        precision=lax.Precision.HIGHEST,
        preferred_element_type=F32,
    )
    for i, gate_ref, out in ((0, gate_mine, own_ref), (1, gate_mine, own_ref), (2, gate_other, other_ref), (3, gate_other, other_ref)):
        half = i & 1

        @pl.when(step == i)
        def _():
            out[half * SUB : (half + 1) * SUB, :] = (total * gate_ref[...].astype(F32)).astype(BF)
            for c in range(SUB // HDIM):
                value = sums[:, c * HDIM : (c + 1) * HDIM]
                top = value.astype(BF)
                at = ROWS + TAIL * (3 * half + c)
                out[at : at + 8, :] = top
                out[at + 8 : at + 16, :] = (value - top.astype(F32)).astype(BF)


def gate_rows(info, parts, gate_mine, gate_other):
    shape = jax.ShapeDtypeStruct((ROWS + 6 * TAIL, HDIM), BF)
    return pl.pallas_call(
        gate_kernel,
        grid_spec=pltpu.PrefetchScalarGridSpec(
            num_scalar_prefetch=1,
            grid=(4,),
            in_specs=[
                pl.BlockSpec((4, SUB, HDIM), lambda i, s: (i ^ (2 * s[1]), 0, 0)),
                pl.BlockSpec((SUB, HDIM), lambda i, s: (jnp.minimum(i, 1), 0)),
                pl.BlockSpec((SUB, HDIM), lambda i, s: (jnp.maximum(i - 2, 0), 0)),
            ],
            out_specs=[whole((ROWS + 6 * TAIL, HDIM))] * 2,
        ),
        out_shape=[shape, shape],
        name="gate_rows",
    )(info, parts, gate_mine, gate_other)


def mix_kernel(info, *refs):
    rows, w_here, w_there = refs[:4], refs[4], refs[5]
    mine_ref, theirs_ref, squares_ref = refs[6:]
    core = info[3] & 1
    for out, c in ((theirs_ref, 1 - core), (mine_ref, core)):
        cols = pl.ds(pl.multiple_of(c * 256, 256), 256)
        acc = None
        for r, w, flip in zip(rows, (w_here, w_here, w_there, w_there), (0, 1, 1, 0)):
            at = pl.ds(pl.multiple_of((info[1] ^ flip) * HDIM, HDIM), HDIM)
            part = jnp.dot(r[0:ROWS, :], w[at, cols], preferred_element_type=F32)
            acc = part if acc is None else acc + part
        out[0:ROWS, :] = acc
    tail = sum(r[ROWS:, :].astype(F32) for r in rows)
    lines = [tail[TAIL * c : TAIL * c + 1] + tail[TAIL * c + 8 : TAIL * c + 9] for c in range(6)]
    squares = jnp.concatenate(lines + [jnp.zeros((2, HDIM), F32)], axis=0)
    squares_ref[...] = squares
    theirs_ref[ROWS:, 0:HDIM] = squares
    theirs_ref[ROWS:, HDIM:] = squares


def mix(info, gated, w_here, w_there):
    return pl.pallas_call(
        mix_kernel,
        grid_spec=pltpu.PrefetchScalarGridSpec(
            num_scalar_prefetch=1,
            grid=(1,),
            in_specs=[whole((ROWS + 6 * TAIL, HDIM))] * 4 + [whole((256, 512))] * 2,
            out_specs=[whole((ROWS, 256)), whole((ROWS + 8, 256)), whole((8, HDIM))],
        ),
        out_shape=[
            jax.ShapeDtypeStruct((ROWS, 256), F32),
            jax.ShapeDtypeStruct((ROWS + 8, 256), F32),
            jax.ShapeDtypeStruct((8, HDIM), F32),
        ],
        name="mix",
    )(info, *gated, w_here, w_there)


def finish_kernel(mine_ref, got_ref, tail_ref, squares_ref, ev_ref, out_ref):
    step = pl.program_id(0)
    inv = lax.rsqrt((squares_ref[...] + tail_ref[:, 0:HDIM]) * (1.0 / D) + EPS)
    which = lax.broadcasted_iota(jnp.int32, (8, HDIM), 0)
    eye = lax.broadcasted_iota(jnp.int32, (HDIM, HDIM), 0) == lax.broadcasted_iota(jnp.int32, (HDIM, HDIM), 1)
    for k in range(2):
        line = jnp.sum(jnp.where(which == 2 * step + k, inv, 0.0), axis=0, keepdims=True)
        column = jnp.sum(jnp.where(eye, line, 0.0), axis=1, keepdims=True)
        at = slice(k * HDIM, (k + 1) * HDIM)
        total = mine_ref[at, :] + got_ref[at, :]
        out_ref[at, :] = (ev_ref[at, :].astype(F32) + total * column).astype(BF)


def finish(mine, got, squares, events):
    rows = pl.BlockSpec((256, 256), lambda i: (i, 0))
    tail = pl.BlockSpec((8, 256), lambda i: (ROWS // 8, 0))
    return pl.pallas_call(
        finish_kernel,
        grid=(ROWS // 256,),
        in_specs=[rows, rows, tail, pl.BlockSpec((8, HDIM), lambda i: (0, 0)), rows],
        out_specs=rows,
        out_shape=jax.ShapeDtypeStruct((ROWS, 256), BF),
        name="finish",
    )(mine, got, got, squares, events)


def layer(events, norm_gain, w_uvqk, w_out, lengths):
    z, yl, x = (lax.axis_index(a).astype(jnp.int32) for a in ("z", "yl", "x"))
    yh = lax.axis_index("yh").astype(jnp.int32)
    o = yh * 2 + lax.axis_index("core").astype(jnp.int32)
    info = jnp.concatenate([jnp.stack([z, yl, x, o]), jnp.cumsum(lengths).astype(jnp.int32)])

    p3 = [to_p3(events[h * SUB : (h + 1) * SUB]) for h in range(2)]
    c0 = flip_core(events)
    w_in = w_uvqk.reshape(D, 4 * 256)
    gain = norm_gain.reshape(4, 256)
    lists = plan(info)
    p3[0], w_in, info, gain, lists = lax.optimization_barrier((p3[0], w_in, info, gain, lists))
    c3 = [flip_core(p3[h]) for h in range(2)]

    first = project_half(info, 0, (events, c0, p3[0], c3[0]), gain, w_in)
    gate_mine, gate_away, kv_mine, kv_away, *pieces = project_half(
        info, 1, (events, c0, p3[1], c3[1]), gain, w_in, first
    )

    def to_class(k):
        def target(z, yl, x, yh, c):
            half, head = (z ^ k) >> 1, (z ^ k) & 1
            return 2 * yl + half, head, x, yh, c

        return target

    pieces = [send(pieces[k], to_class(k)) for k in range(4)]
    up_mine, down_mine = shift_z(kv_mine, 1), shift_z(kv_mine, -1)
    kv_other = to_p1(kv_away)
    gate_other = to_p1(gate_away)
    up_other, down_other = shift_z(kv_other, 1), shift_z(kv_other, -1)

    q_mine = jnp.concatenate(pieces, axis=0)
    queries = [q_mine] + [shift_x(q_mine, e) for e in (1, 3, 2)]
    near, away = shift_z(up_mine, 1), shift_z(down_other, -1)

    keyvals = [kv_mine, kv_other, up_mine, down_mine, up_other, down_other, near, away]
    parts = attend(info, lists, queries, keyvals)

    w_here = lax.dynamic_slice_in_dim(w_out, yh * 512, 512, 1)
    w_away = lax.dynamic_slice_in_dim(w_out, (1 - yh) * 512, 512, 1)
    w_away, _ = lax.optimization_barrier((w_away, q_mine))
    w_there = to_p3(w_away)

    parts = lax.all_to_all(parts, ("z", "x"), 0, 0)
    own, other = gate_rows(info, parts, gate_mine, gate_other)
    gated = [own, to_p1(other), to_p2(other), to_p3(own)]
    mine, theirs, squares = mix(info, gated, w_here, w_there)
    return finish(mine, flip_core(theirs), squares, events)


def solution(mesh):
    fine = Mesh(mesh.devices.reshape(SIZES), AXES)
    ctx, head = ("z", "yl", "x"), ("yh", "core")
    in_specs = (P(ctx, head), P(), P(None, None, head), P(head, None), P())
    return jax.shard_map(layer, mesh=fine, in_specs=in_specs, out_specs=P(ctx, head), check_vma=False)
```

time: 171 us -> 161 us (0.942)
  starting transfers between devices: 50.1 us -> 45.7 us
  Pallas kernels: 52.8 us -> 48.9 us
  local copies, waits for them, and re-layouts: 14.5 us -> 12.3 us
    pallas_call x5 -> x4, Pallas kernels: 41.5 us -> 36.8 us  [the longest x1 22 us: attend(): pl.pallas_call(attend_kernel, grid_spec=pltpu.PrefetchScalarGridSpec(num_...]
    ppermute x24 -> x25, starting transfers between devices: 45.1 us -> 41.9 us  [send(): return lax.ppermute(array, AXES, pairs)]
    unnamed x58 -> x54, local copies, waits for them, and re-layouts: 12.5 us -> 9.26 us
    ppermute x24 -> x25, waiting for transfers between devices: 38.6 us -> 38.6 us  [send(): return lax.ppermute(array, AXES, pairs)]
  transfers between devices with their start and end apart: 25 -> 26, of which waited for: 10 -> 14; matrix products, arithmetic and copies ran while one was open for 4% -> 4% of each run, Pallas kernels for 15% -> 9%
where the time goes in v1:
time: 161 us; the launch traced here: 160 us
  waiting for transfers between devices  52.1 us (32%)
  Pallas kernels  48.9 us (30%)
  starting transfers between devices  45.7 us (28%)
  local copies, waits for them, and re-layouts  12.3 us (8%)
    ppermute x25, starting transfers between devices, send(): return lax.ppermute(array, AXES, pairs)  41.9 us
    ppermute x25, waiting for transfers between devices, send(): return lax.ppermute(array, AXES, pairs)  38.6 us
    pallas_call x1, Pallas kernels, attend(): pl.pallas_call(attend_kernel, grid_spec=pltpu.PrefetchScalarGridSpec(num_...  22 us
    all_to_all x1, waiting for transfers between devices, layer(): parts = lax.all_to_all(parts, ('z', 'x'), 0, 0)  13.5 us
    pallas_call x2, Pallas kernels, project_half(): pl.pallas_call(functools.partial(half_kernel, bool(half)), grid_spec=pltp...  10.6 us
    unnamed x54, local copies, waits for them, and re-layouts  9.26 us
    pallas_call x1, Pallas kernels, gate_rows(): pl.pallas_call(gate_kernel, grid_spec=pltpu.PrefetchScalarGridSpec(num_sc...  4.71 us
    pallas_call x1, Pallas kernels, plan(): pl.pallas_call(plan_kernel, grid_spec=pltpu.PrefetchScalarGridSpec(num_sc...  4.26 us
  transfers between devices with their start and end apart: 26, of which 14 were waited for; matrix products, arithmetic and copies ran while one was open for 4% of the time, Pallas kernels for 9%

profile of v1, /device:TPU:1, one launch (start us, length us, event | category | flops | bytes accessed | tf_op | source)
XLA Modules:
  0.0 160.2 jit_solution(12577189409719597459)
XLA Ops:
  0.0 1.0 fusion
  1.1 3.8 %collective-permute-start = (bf16[384,256]{1,0:T(8,128)(2,1)S(1)}, bf16[384,256]{1,0:T(8,128)(2,1)S(1)}, u32[]{:S(2)}, u32[]{:S(2)}) collective-permute-start(bf16[384,256]{1,0:T(8,128)(2,1)S(1)} %get-tuple-element.70), channel_id=1, source_target_pairs={{0,2},{1,3},{2,0},{3,1},{4,6},{5,7},{6,4},{7,5},{8,10},{9,11},{10,... | collective-permute-start | bytes 589832 | tf_op jit(solution)/shard_map/ppermute | solution.py:36
  4.9 1.0 collective-permute-start.1
  5.8 0.0 collective-permute-start.2
  5.8 0.8 reduce-window.9
  6.7 0.7 concatenate.6.info
  7.3 4.3 %plan.1 = (s32[416]{0:T(512)}, s32[416]{0:T(512)}, s32[416]{0:T(512)}, s32[416]{0:T(512)}) custom-call(s32[12]{0:T(128)} %concatenate.6.info), custom_call_target="tpu_custom_call" | custom-call | tf_op jit(solution)/shard_map/plan/pallas_call | solution.py:224
  11.6 0.0 copy-start.24
  11.6 3.4 %copy.10 = bf16[128,8,4,256]{3,1,2,0:T(8,128)(2,1)} copy(bf16[128,8,4,256]{3,2,1,0:T(4,128)(2,1)} %bitcast.10) | data formatting | bytes 4194304
  15.0 0.6 reshape.35.refs_4_
  15.6 0.0 collective-permute-done.refs_2_
  15.6 0.2 collective-permute-start.4
  15.8 0.3 collective-permute-start.3
  16.1 0.9 collective-permute-done.4.refs_3_
  17.1 0.7 copy-done.23
  17.7 0.7 copy-done.2
  18.5 5.2 %project_first.1 = (bf16[768,128]{1,0:T(8,128)(2,1)}, bf16[768,128]{1,0:T(8,128)(2,1)}, bf16[768,256]{1,0:T(8,128)(2,1)}, bf16[768,256]{1,0:T(8,128)(2,1)}, bf16[2,384,128]{2,1,0:T(8,128)(2,1)}) custom-call(s32[12]{0:T(128)} %concatenate.6.info, bf16[768,256]{1,0:T(8,128)(2,1)} %ev_ref.1, bf16[768,256]{1,0:T(8,128)(2,1)} %copy-done.2, ...), custom_call_target="tpu_custom_call" | custom-call | tf_op jit(solution)/shard_map/project_first/pallas_call | solution.py:133
  23.7 0.7 copy-done.19
  24.4 5.4 %project_second.1 = (bf16[768,128]{1,0:T(8,128)(2,1)}, bf16[768,128]{1,0:T(8,128)(2,1)}, bf16[768,256]{1,0:T(8,128)(2,1)}, bf16[768,256]{1,0:T(8,128)(2,1)}, bf1...) custom-call(s32[12]{0:T(128)} %concatenate.6.info, ...), custom_call_target="tpu_custom_call", output_to_operand_aliasing={{0}: (8, {}), {1}: (9, {}), {2}: (10, {}), {3}: (11, {})} | custom-call | tf_op jit(solution)/shard_map/project_second/pallas_call | solution.py:133
  29.7 1.5 collective-permute-start.5
  31.3 2.9 %collective-permute-start.13 = (bf16[768,256]{1,0:T(8,128)(2,1)}, bf16[768,256]{1,0:T(8,128)(2,1)S(1)}, u32[]{:S(2)}, u32[]{:S(2)}) collective-permute-start(bf16[768,256]{1,0:T(8,128)(2,1)} %get-tuple-element.57.refs_8_), channel_id=1, source_target_pairs={{0,32},{1,33},{2,34},{3,35},{4,36},{5,37},{6,38},{7,39},{8,40},{9,... | collective-permute-start | bytes 1179656 | tf_op jit(solution)/shard_map/ppermute | solution.py:36
  34.2 2.7 %collective-permute-start.14 = (bf16[768,256]{1,0:T(8,128)(2,1)}, bf16[768,256]{1,0:T(8,128)(2,1)S(1)}, u32[]{:S(2)}, u32[]{:S(2)}) collective-permute-start(bf16[768,256]{1,0:T(8,128)(2,1)} %get-tuple-element.57.refs_8_), channel_id=1, source_target_pairs={{0,96},{1,97},{2,98},{3,99},{4,100},{5,101},{6,102},{7,103},{8,104... | collective-permute-start | bytes 1179656 | tf_op jit(solution)/shard_map/ppermute | solution.py:36
  36.9 2.0 %collective-permute-start.6 = (bf16[384,128]{1,0:T(8,128)(2,1)}, bf16[384,128]{1,0:T(8,128)(2,1)S(1)}, u32[]{:S(2)}, u32[]{:S(2)}) collective-permute-start(bf16[384,128]{1,0:T(8,128)(2,1)} %get-tuple-element.54), channel_id=1, source_target_pairs={{0,16},{1,17},{2,18},{3,19},{4,20},{5,21},{6,22},{7,23},{8,24},{9,... | collective-permute-start | bytes 294920 | tf_op jit(solution)/shard_map/ppermute | solution.py:36
  38.9 0.6 collective-permute-start.12
  39.5 6.9 %collective-permute-done.6 = bf16[384,128]{1,0:T(8,128)(2,1)S(1)} collective-permute-done((bf16[384,128]{1,0:T(8,128)(2,1)}, bf16[384,128]{1,0:T(8,128)(2,1)S(1)}, u32[]{:S(2)}, u32[]{:S(2)}) %collective-permute-start.6) | collective-permute-done | bytes 98336 | tf_op jit(solution)/shard_map/ppermute | solution.py:36
  46.4 1.9 %collective-permute-start.8 = (bf16[384,128]{1,0:T(8,128)(2,1)}, bf16[384,128]{1,0:T(8,128)(2,1)S(1)}, u32[]{:S(2)}, u32[]{:S(2)}) collective-permute-start(bf16[384,128]{1,0:T(8,128)(2,1)} %get-tuple-element.56), channel_id=1, source_target_pairs={{0,48},{1,49},{2,50},{3,51},{4,52},{5,53},{6,54},{7,55},{8,56},{9,... | collective-permute-start | bytes 294920 | tf_op jit(solution)/shard_map/ppermute | solution.py:36
  48.3 3.0 %collective-permute-done.7 = bf16[384,128]{1,0:T(8,128)(2,1)S(1)} collective-permute-done((bf16[384,128]{1,0:T(8,128)(2,1)}, bf16[384,128]{1,0:T(8,128)(2,1)S(1)}, u32[]{:S(2)}, u32[]{:S(2)}) %collective-permute-start.7) | collective-permute-done | bytes 98336 | tf_op jit(solution)/shard_map/ppermute | solution.py:36
  51.3 1.8 %collective-permute-done.8 = bf16[384,128]{1,0:T(8,128)(2,1)S(1)} collective-permute-done((bf16[384,128]{1,0:T(8,128)(2,1)}, bf16[384,128]{1,0:T(8,128)(2,1)S(1)}, u32[]{:S(2)}, u32[]{:S(2)}) %collective-permute-start.8) | collective-permute-done | bytes 98336 | tf_op jit(solution)/shard_map/ppermute | solution.py:36
  53.2 0.0 copy-start.3
  53.2 2.4 %collective-permute-start.10 = (bf16[1536,128]{1,0:T(8,128)(2,1)S(1)}, bf16[1536,128]{1,0:T(8,128)(2,1)S(1)}, u32[]{:S(2)}, u32[]{:S(2)}) collective-permute-start(bf16[1536,128]{1,0:T(8,128)(2,1)S(1)} %constant_dynamic-update-slice_fusion.refs_4_), channel_id=1, source_target_pairs={{0,12},{1,13},{2,14},{3,15},{4,0},{5,1},{6,2},{7,3},{8,4},{9,5},{1... | collective-permute-start | bytes 1179656 | tf_op jit(solution)/shard_map/ppermute | solution.py:36
  55.6 0.0 collective-permute-done.12.refs_9_
  55.6 3.2 %collective-permute-start.16 = (bf16[768,256]{1,0:T(8,128)(2,1)S(1)}, bf16[768,256]{1,0:T(8,128)(2,1)S(1)}, u32[]{:S(2)}, u32[]{:S(2)}) collective-permute-start(bf16[768,256]{1,0:T(8,128)(2,1)S(1)} %collective-permute-done.12.refs_9_), channel_id=1, source_target_pairs={{0,96},{1,97},{2,98},{3,99},{4,100},{5,101},{6,102},{7,103},{8,104... | collective-permute-start | bytes 1179656 | tf_op jit(solution)/shard_map/ppermute | solution.py:36
  58.7 0.6 collective-permute-start.11
  59.3 0.4 collective-permute-start.9
  59.8 2.0 %collective-permute-done.10.refs_6_ = bf16[1536,128]{1,0:T(8,128)(2,1)S(1)} collective-permute-done((bf16[1536,128]{1,0:T(8,128)(2,1)S(1)}, bf16[1536,128]{1,0:T(8,128)(2,1)S(1)}, u32[]{:S(2)}, u32[]{:S(2)}) %collective-permute-start.10) | collective-permute-done | bytes 393248 | tf_op jit(solution)/shard_map/ppermute | solution.py:36
  61.8 2.3 %collective-permute-done.16.refs_13_ = bf16[768,256]{1,0:T(8,128)(2,1)S(1)} collective-permute-done((bf16[768,256]{1,0:T(8,128)(2,1)S(1)}, bf16[768,256]{1,0:T(8,128)(2,1)S(1)}, u32[]{:S(2)}, u32[]{:S(2)}) %collective-permute-start.16) | collective-permute-done | bytes 393248 | tf_op jit(solution)/shard_map/ppermute | solution.py:36
  64.1 3.4 %collective-permute-start.18 = (bf16[768,256]{1,0:T(8,128)(2,1)S(1)}, bf16[768,256]{1,0:T(8,128)(2,1)}, u32[]{:S(2)}, u32[]{:S(2)}) collective-permute-start(bf16[768,256]{1,0:T(8,128)(2,1)S(1)} %collective-permute-done.16.refs_13_), channel_id=1, source_target_pairs={{0,96},{1,97},{2,98},{3,99},{4,100},{5,101},{6,102},{7,103},{8,104... | collective-permute-start | bytes 1179656 | tf_op jit(solution)/shard_map/ppermute | solution.py:36
  67.5 0.1 collective-permute-done.11.refs_7_
  67.6 12.1 %collective-permute-done.9.refs_5_ = bf16[1536,128]{1,0:T(8,128)(2,1)S(1)} collective-permute-done((bf16[1536,128]{1,0:T(8,128)(2,1)S(1)}, bf16[1536,128]{1,0:T(8,128)(2,1)S(1)}, u32[]{:S(2)}, u32[]{:S(2)}) %collective-permute-start.9) | collective-permute-done | bytes 393248 | tf_op jit(solution)/shard_map/ppermute | solution.py:36
  79.7 0.0 collective-permute-done.17.refs_14_
  79.7 0.8 copy-done.13
  80.6 0.1 copy-done.12
  80.7 22.0 %attend.1 = bf16[16,384,128]{2,1,0:T(8,128)(2,1)} custom-call(s32[12]{0:T(128)} %concatenate.6.info, s32[416]{0:T(512)} %get-tuple-element.41.refs_0_, s32[416]{0:T(512)} %get-tuple-element.42.refs_1_, s32[416]{0:T(512)} %get-tuple-element.43.refs_2_, s32[416]{0:T(512)} %get-tuple-element.44.refs_3_, bf16[1536,128]{1,0:T(8,128)(2,1)} %copy-done.3, ...), custom_call_target="tpu_custom_call" | custom-call | tf_op jit(solution)/shard_map/attend/pallas_call | solution.py:313
  102.8 0.0 copy-start.4
  102.8 3.9 %all-to-all-start = ((bf16[16,384,128]{2,1,0:T(8,128)(2,1)}), bf16[16,384,128]{2,1,0:T(8,128)(2,1)S(1)}, u32[]{:S(2)}, u32[]{:S(2)}) async-start(bf16[16,384,128]{2,1,0:T(8,128)(2,1)} %attend.1), calls=%async_computation | async-start | bytes 3145728 | tf_op jit(solution)/shard_map/all_to_all | solution.py:485
  106.7 0.1 collective-permute-start.19
  106.8 0.7 constant_dynamic-slice_fusion
  107.5 2.6 %collective-permute-start.23 = (bf16[256,512]{1,0:T(8,128)(2,1)S(1)}, bf16[256,512]{1,0:T(8,128)(2,1)S(1)}, u32[]{:S(2)}, u32[]{:S(2)}) collective-permute-start(bf16[256,512]{1,0:T(8,128)(2,1)S(1)} %get-tuple-element.63), channel_id=1, source_target_pairs={{0,2},{1,3},{2,0},{3,1},{4,6},{5,7},{6,4},{7,5},{8,10},{9,11},{10,... | collective-permute-start | bytes 786440 | tf_op jit(solution)/shard_map/ppermute | solution.py:36
  110.2 1.1 collective-permute-done.19.gate_other
  111.3 13.5 %all-to-all-done.part_ref = bf16[16,384,128]{2,1,0:T(8,128)(2,1)S(1)} async-done(((bf16[16,384,128]{2,1,0:T(8,128)(2,1)}), bf16[16,384,128]{2,1,0:T(8,128)(2,1)S(1)}, u32[]{:S(2)}, u32[]{:S(2)}) %all-to-all-start) | async-done | bytes 1572896 | tf_op jit(solution)/shard_map/all_to_all | solution.py:485
  124.8 1.1 copy-done
  125.9 4.7 %gate_rows.1 = (bf16[864,128]{1,0:T(8,128)(2,1)}, bf16[864,128]{1,0:T(8,128)(2,1)}) custom-call(s32[12]{0:T(128)} %concatenate.6.info, bf16[16,384,128]{2,1,0:T(8,128)(2,1)} %copy-done, bf16[768,128]{1,0:T(8,128)(2,1)} %get-tuple-element.59.gate_mine, bf16[768,128]{1,0:T(8,128)(2,1)} %copy-done.21), custom_call_target="tpu_custom_call" | custom-call | tf_op jit(solution)/shard_map/gate_rows/pallas_call | solution.py:360
  130.6 0.0 collective-permute-start.20
  130.7 2.9 %collective-permute-start.21 = (bf16[864,128]{1,0:T(8,128)(2,1)}, bf16[864,128]{1,0:T(8,128)(2,1)S(1)}, u32[]{:S(2)}, u32[]{:S(2)}) collective-permute-start(bf16[864,128]{1,0:T(8,128)(2,1)} %get-tuple-element.62), channel_id=1, source_target_pairs={{0,18},{1,19},{2,16},{3,17},{4,22},{5,23},{6,20},{7,21},{8,26},{9,... | collective-permute-start | bytes 663560 | tf_op jit(solution)/shard_map/ppermute | solution.py:36
  133.6 0.3 collective-permute-start.22
  133.9 1.7 %collective-permute-done.20.refs_1_ = bf16[864,128]{1,0:T(8,128)(2,1)S(1)} collective-permute-done((bf16[864,128]{1,0:T(8,128)(2,1)}, bf16[864,128]{1,0:T(8,128)(2,1)S(1)}, u32[]{:S(2)}, u32[]{:S(2)}) %collective-permute-start.20) | collective-permute-done | bytes 221216 | tf_op jit(solution)/shard_map/ppermute | solution.py:36
  135.6 3.5 %collective-permute-done.21.refs_2_ = bf16[864,128]{1,0:T(8,128)(2,1)S(1)} collective-permute-done((bf16[864,128]{1,0:T(8,128)(2,1)}, bf16[864,128]{1,0:T(8,128)(2,1)S(1)}, u32[]{:S(2)}, u32[]{:S(2)}) %collective-permute-start.21) | collective-permute-done | bytes 221216 | tf_op jit(solution)/shard_map/ppermute | solution.py:36
  139.2 0.9 collective-permute-done.22.refs_3_
  140.1 0.7 copy-done.17
  140.8 4.2 %mix.1 = (f32[768,256]{1,0:T(8,128)}, f32[776,256]{1,0:T(8,128)}, f32[8,128]{1,0:T(8,128)}) custom-call(s32[12]{0:T(128)} %concatenate.6.info, bf16[864,128]{1,0:T(8,128)(2,1)} %get-tuple-element.61.refs_0_, bf16[864,128]{1,0:T(8,128)(2,1)} %copy-done.15, bf16[864,128]{1,0:T(8,128)(2,1)} %copy-done.16, bf16[864,128]{1,0:T(8,128)(2,1)} %copy-done.17, ...), custom_call_target="tpu_custom_call" | custom-call | tf_op jit(solution)/shard_map/mix/pallas_call | solution.py:398
  145.0 9.0 %collective-permute-start.24 = (f32[776,256]{1,0:T(8,128)}, f32[776,256]{1,0:T(8,128)S(1)}, u32[]{:S(2)}, u32[]{:S(2)}) collective-permute-start(f32[776,256]{1,0:T(8,128)} %get-tuple-element.65), channel_id=1, source_target_pairs={{0,1},{1,0},{2,3},{3,2},{4,5},{5,4},{6,7},{7,6},{8,9},{9,8},{10,11... | collective-permute-start | bytes 2383880 | tf_op jit(solution)/shard_map/ppermute | solution.py:36
  154.0 2.1 %collective-permute-done.24.got_ref.tail_ref = f32[776,256]{1,0:T(8,128)S(1)} collective-permute-done((f32[776,256]{1,0:T(8,128)}, f32[776,256]{1,0:T(8,128)S(1)}, u32[]{:S(2)}, u32[]{:S(2)}) %collective-permute-start.24) | collective-permute-done | bytes 794656 | tf_op jit(solution)/shard_map/ppermute | solution.py:36
  156.1 0.9 copy-done.1
  157.0 3.2 %finish.1 = bf16[768,256]{1,0:T(8,128)(2,1)} custom-call(f32[768,256]{1,0:T(8,128)} %get-tuple-element.64.mine_ref, f32[776,256]{1,0:T(8,128)} %copy-done.1, f32[776,256]{1,0:T(8,128)} %copy-done.1, f32[8,128]{1,0:T(8,128)} %get-tuple-element.66.squares_ref, bf16[768,256]{1,0:T(8,128)(2,1)} %ev_ref.1), custom_call_target="tpu_custom_call" | custom-call | tf_op jit(solution)/shard_map/finish/pallas_call | solution.py:431
  (55 shorter events, 0.2 us)
Async XLA Ops:
  1.1 14.5 %collective-permute-start = (bf16[384,256]{1,0:T(8,128)(2,1)S(1)}, bf16[384,256]{1,0:T(8,128)(2,1)S(1)}, u32[]{:S(2)}, u32[]{:S(2)}) collective-permute-start(bf16[384,256]{1,0:T(8,128)(2,1)S(1)} %get-tuple-element.70), channel_id=1, source_target_pairs={{0,2},{1,3},{2,0},{3,1},{4,6},{5,7},{6,4},{7,5},{8,10},{9,11},{10,... | collective-permute-start | bytes 589832 | tf_op jit(solution)/shard_map/ppermute | solution.py:36
  4.9 12.2 %collective-permute-start.1 = (bf16[768,256]{1,0:T(8,128)(2,1)}, bf16[768,256]{1,0:T(8,128)(2,1)S(1)}, u32[]{:S(2)}, u32[]{:S(2)}) collective-permute-start(bf16[768,256]{1,0:T(8,128)(2,1)} %ev_ref.1), channel_id=1, source_target_pairs={{0,1},{1,0},{2,3},{3,2},{4,5},{5,4},{6,7},{7,6},{8,9},{9,8},{10,11... | collective-permute-start | bytes 1179656 | tf_op jit(solution)/shard_map/ppermute | solution.py:36
  5.8 10.0 %collective-permute-start.2 = (bf16[384,256]{1,0:T(8,128)(2,1)S(1)}, bf16[384,256]{1,0:T(8,128)(2,1)S(1)}, u32[]{:S(2)}, u32[]{:S(2)}) collective-permute-start(bf16[384,256]{1,0:T(8,128)(2,1)S(1)} %get-tuple-element.69), channel_id=1, source_target_pairs={{0,2},{1,3},{2,0},{3,1},{4,6},{5,7},{6,4},{7,5},{8,10},{9,11},{10,... | collective-permute-start | bytes 589832 | tf_op jit(solution)/shard_map/ppermute | solution.py:36
  11.6 3.4 %copy-start.24 = (f32[1024]{0:T(1024)S(1)}, f32[1024]{0:T(1024)}, u32[]{:S(2)}) copy-start(f32[1024]{0:T(1024)} %param.6) | copy-start | bytes 12292
  15.6 1.5 copy-start.22
  15.6 1.4 collective-permute-start.4
  15.8 7.9 %copy-start.18 = (bf16[384,256]{1,0:T(8,128)(2,1)}, bf16[384,256]{1,0:T(8,128)(2,1)S(1)}, u32[]{:S(2)}) copy-start(bf16[384,256]{1,0:T(8,128)(2,1)S(1)} %collective-permute-done.2.refs_2_) | copy-start | bytes 589828
  15.8 7.9 %collective-permute-start.3 = (bf16[384,256]{1,0:T(8,128)(2,1)S(1)}, bf16[384,256]{1,0:T(8,128)(2,1)S(1)}, u32[]{:S(2)}, u32[]{:S(2)}) collective-permute-start(bf16[384,256]{1,0:T(8,128)(2,1)S(1)} %collective-permute-done.2.refs_2_), channel_id=1, source_target_pairs={{0,1},{1,0},{2,3},{3,2},{4,5},{5,4},{6,7},{7,6},{8,9},{9,8},{10,11... | collective-permute-start | bytes 589832 | tf_op jit(solution)/shard_map/ppermute | solution.py:36
  17.0 0.7 copy-start.23
  17.7 0.7 copy-start.2
  23.7 0.7 copy-start.19
  29.7 9.2 %collective-permute-start.5 = (bf16[384,128]{1,0:T(8,128)(2,1)}, bf16[384,128]{1,0:T(8,128)(2,1)S(1)}, u32[]{:S(2)}, u32[]{:S(2)}) collective-permute-start(bf16[384,128]{1,0:T(8,128)(2,1)} %get-tuple-element.53), channel_id=1, source_target_pairs={{0,0},{1,1},{2,2},{3,3},{4,4},{5,5},{6,6},{7,7},{8,8},{9,9},{10,10... | collective-permute-start | bytes 294920 | tf_op jit(solution)/shard_map/ppermute | solution.py:36
  31.3 28.0 %collective-permute-start.13 = (bf16[768,256]{1,0:T(8,128)(2,1)}, bf16[768,256]{1,0:T(8,128)(2,1)S(1)}, u32[]{:S(2)}, u32[]{:S(2)}) collective-permute-start(bf16[768,256]{1,0:T(8,128)(2,1)} %get-tuple-element.57.refs_8_), channel_id=1, source_target_pairs={{0,32},{1,33},{2,34},{3,35},{4,36},{5,37},{6,38},{7,39},{8,40},{9,... | collective-permute-start | bytes 1179656 | tf_op jit(solution)/shard_map/ppermute | solution.py:36
  34.2 25.5 %collective-permute-start.14 = (bf16[768,256]{1,0:T(8,128)(2,1)}, bf16[768,256]{1,0:T(8,128)(2,1)S(1)}, u32[]{:S(2)}, u32[]{:S(2)}) collective-permute-start(bf16[768,256]{1,0:T(8,128)(2,1)} %get-tuple-element.57.refs_8_), channel_id=1, source_target_pairs={{0,96},{1,97},{2,98},{3,99},{4,100},{5,101},{6,102},{7,103},{8,104... | collective-permute-start | bytes 1179656 | tf_op jit(solution)/shard_map/ppermute | solution.py:36
  36.9 9.5 %collective-permute-start.6 = (bf16[384,128]{1,0:T(8,128)(2,1)}, bf16[384,128]{1,0:T(8,128)(2,1)S(1)}, u32[]{:S(2)}, u32[]{:S(2)}) collective-permute-start(bf16[384,128]{1,0:T(8,128)(2,1)} %get-tuple-element.54), channel_id=1, source_target_pairs={{0,16},{1,17},{2,18},{3,19},{4,20},{5,21},{6,22},{7,23},{8,24},{9,... | collective-permute-start | bytes 294920 | tf_op jit(solution)/shard_map/ppermute | solution.py:36
  38.9 12.4 %collective-permute-start.7 = (bf16[384,128]{1,0:T(8,128)(2,1)}, bf16[384,128]{1,0:T(8,128)(2,1)S(1)}, u32[]{:S(2)}, u32[]{:S(2)}) collective-permute-start(bf16[384,128]{1,0:T(8,128)(2,1)} %get-tuple-element.55), channel_id=1, source_target_pairs={{0,32},{1,33},{2,34},{3,35},{4,36},{5,37},{6,38},{7,39},{8,40},{9,... | collective-permute-start | bytes 294920 | tf_op jit(solution)/shard_map/ppermute | solution.py:36
  38.9 16.6 %collective-permute-start.12 = (bf16[768,256]{1,0:T(8,128)(2,1)}, bf16[768,256]{1,0:T(8,128)(2,1)S(1)}, u32[]{:S(2)}, u32[]{:S(2)}) collective-permute-start(bf16[768,256]{1,0:T(8,128)(2,1)} %get-tuple-element.58), channel_id=1, source_target_pairs={{0,16},{1,17},{2,18},{3,19},{4,20},{5,21},{6,22},{7,23},{8,24},{9,... | collective-permute-start | bytes 1179656 | tf_op jit(solution)/shard_map/ppermute | solution.py:36
  46.4 6.8 %collective-permute-start.8 = (bf16[384,128]{1,0:T(8,128)(2,1)}, bf16[384,128]{1,0:T(8,128)(2,1)S(1)}, u32[]{:S(2)}, u32[]{:S(2)}) collective-permute-start(bf16[384,128]{1,0:T(8,128)(2,1)} %get-tuple-element.56), channel_id=1, source_target_pairs={{0,48},{1,49},{2,50},{3,51},{4,52},{5,53},{6,54},{7,55},{8,56},{9,... | collective-permute-start | bytes 294920 | tf_op jit(solution)/shard_map/ppermute | solution.py:36
  53.2 27.4 %copy-start.3 = (bf16[1536,128]{1,0:T(8,128)(2,1)}, bf16[1536,128]{1,0:T(8,128)(2,1)S(1)}, u32[]{:S(2)}) copy-start(bf16[1536,128]{1,0:T(8,128)(2,1)S(1)} %constant_dynamic-update-slice_fusion.refs_4_) | copy-start | bytes 1179652
  53.2 8.6 %collective-permute-start.10 = (bf16[1536,128]{1,0:T(8,128)(2,1)S(1)}, bf16[1536,128]{1,0:T(8,128)(2,1)S(1)}, u32[]{:S(2)}, u32[]{:S(2)}) collective-permute-start(bf16[1536,128]{1,0:T(8,128)(2,1)S(1)} %constant_dynamic-update-slice_fusion.refs_4_), channel_id=1, source_target_pairs={{0,12},{1,13},{2,14},{3,15},{4,0},{5,1},{6,2},{7,3},{8,4},{9,5},{1... | collective-permute-start | bytes 1179656 | tf_op jit(solution)/shard_map/ppermute | solution.py:36
  55.6 25.0 %copy-start.7 = (bf16[768,256]{1,0:T(8,128)(2,1)}, bf16[768,256]{1,0:T(8,128)(2,1)S(1)}, u32[]{:S(2)}) copy-start(bf16[768,256]{1,0:T(8,128)(2,1)S(1)} %collective-permute-done.12.refs_9_) | copy-start | bytes 1179652
  55.6 8.5 %collective-permute-start.16 = (bf16[768,256]{1,0:T(8,128)(2,1)S(1)}, bf16[768,256]{1,0:T(8,128)(2,1)S(1)}, u32[]{:S(2)}, u32[]{:S(2)}) collective-permute-start(bf16[768,256]{1,0:T(8,128)(2,1)S(1)} %collective-permute-done.12.refs_9_), channel_id=1, source_target_pairs={{0,96},{1,97},{2,98},{3,99},{4,100},{5,101},{6,102},{7,103},{8,104... | collective-permute-start | bytes 1179656 | tf_op jit(solution)/shard_map/ppermute | solution.py:36
  58.7 8.8 %collective-permute-start.11 = (bf16[1536,128]{1,0:T(8,128)(2,1)S(1)}, bf16[1536,128]{1,0:T(8,128)(2,1)S(1)}, u32[]{:S(2)}, u32[]{:S(2)}) collective-permute-start(bf16[1536,128]{1,0:T(8,128)(2,1)S(1)} %constant_dynamic-update-slice_fusion.refs_4_), channel_id=1, source_target_pairs={{0,8},{1,9},{2,10},{3,11},{4,12},{5,13},{6,14},{7,15},{8,0},{9,1},... | collective-permute-start | bytes 1179656 | tf_op jit(solution)/shard_map/ppermute | solution.py:36
  59.3 21.2 %copy-start.5 = (bf16[768,256]{1,0:T(8,128)(2,1)}, bf16[768,256]{1,0:T(8,128)(2,1)S(1)}, u32[]{:S(2)}) copy-start(bf16[768,256]{1,0:T(8,128)(2,1)S(1)} %collective-permute-done.13.refs_10_) | copy-start | bytes 1179652
  59.3 20.4 %collective-permute-start.9 = (bf16[1536,128]{1,0:T(8,128)(2,1)S(1)}, bf16[1536,128]{1,0:T(8,128)(2,1)S(1)}, u32[]{:S(2)}, u32[]{:S(2)}) collective-permute-start(bf16[1536,128]{1,0:T(8,128)(2,1)S(1)} %constant_dynamic-update-slice_fusion.refs_4_), channel_id=1, source_target_pairs={{0,4},{1,5},{2,6},{3,7},{4,8},{5,9},{6,10},{7,11},{8,12},{9,13},{1... | collective-permute-start | bytes 1179656 | tf_op jit(solution)/shard_map/ppermute | solution.py:36
  59.8 20.8 %copy-start.6 = (bf16[768,256]{1,0:T(8,128)(2,1)}, bf16[768,256]{1,0:T(8,128)(2,1)S(1)}, u32[]{:S(2)}) copy-start(bf16[768,256]{1,0:T(8,128)(2,1)S(1)} %collective-permute-done.14.refs_11_) | copy-start | bytes 1179652
  59.8 20.0 %collective-permute-start.15 = (bf16[768,256]{1,0:T(8,128)(2,1)S(1)}, bf16[768,256]{1,0:T(8,128)(2,1)S(1)}, u32[]{:S(2)}, u32[]{:S(2)}) collective-permute-start(bf16[768,256]{1,0:T(8,128)(2,1)S(1)} %collective-permute-done.12.refs_9_), channel_id=1, source_target_pairs={{0,32},{1,33},{2,34},{3,35},{4,36},{5,37},{6,38},{7,39},{8,40},{9,... | collective-permute-start | bytes 1179656 | tf_op jit(solution)/shard_map/ppermute | solution.py:36
  61.8 18.8 %copy-start.8 = (bf16[1536,128]{1,0:T(8,128)(2,1)}, bf16[1536,128]{1,0:T(8,128)(2,1)S(1)}, u32[]{:S(2)}) copy-start(bf16[1536,128]{1,0:T(8,128)(2,1)S(1)} %collective-permute-done.10.refs_6_) | copy-start | bytes 1179652
  61.8 17.9 %collective-permute-start.17 = (bf16[768,256]{1,0:T(8,128)(2,1)S(1)}, bf16[768,256]{1,0:T(8,128)(2,1)S(1)}, u32[]{:S(2)}, u32[]{:S(2)}) collective-permute-start(bf16[768,256]{1,0:T(8,128)(2,1)S(1)} %collective-permute-done.13.refs_10_), channel_id=1, source_target_pairs={{0,32},{1,33},{2,34},{3,35},{4,36},{5,37},{6,38},{7,39},{8,40},{9,... | collective-permute-start | bytes 1179656 | tf_op jit(solution)/shard_map/ppermute | solution.py:36
  64.1 16.5 %copy-start.9 = (bf16[768,256]{1,0:T(8,128)(2,1)}, bf16[768,256]{1,0:T(8,128)(2,1)S(1)}, u32[]{:S(2)}) copy-start(bf16[768,256]{1,0:T(8,128)(2,1)S(1)} %collective-permute-done.16.refs_13_) | copy-start | bytes 1179652
  64.1 16.5 %collective-permute-start.18 = (bf16[768,256]{1,0:T(8,128)(2,1)S(1)}, bf16[768,256]{1,0:T(8,128)(2,1)}, u32[]{:S(2)}, u32[]{:S(2)}) collective-permute-start(bf16[768,256]{1,0:T(8,128)(2,1)S(1)} %collective-permute-done.16.refs_13_), channel_id=1, source_target_pairs={{0,96},{1,97},{2,98},{3,99},{4,100},{5,101},{6,102},{7,103},{8,104... | collective-permute-start | bytes 1179656 | tf_op jit(solution)/shard_map/ppermute | solution.py:36
  67.6 13.0 %copy-start.10 = (bf16[1536,128]{1,0:T(8,128)(2,1)}, bf16[1536,128]{1,0:T(8,128)(2,1)S(1)}, u32[]{:S(2)}) copy-start(bf16[1536,128]{1,0:T(8,128)(2,1)S(1)} %collective-permute-done.11.refs_7_) | copy-start | bytes 1179652
  79.7 0.9 copy-start.11
  79.7 1.0 copy-start.12
  79.7 0.8 copy-start.13
  102.8 3.9 %copy-start.20 = (bf16[768,128]{1,0:T(8,128)(2,1)S(1)}, bf16[768,128]{1,0:T(8,128)(2,1)}, u32[]{:S(2)}) copy-start(bf16[768,128]{1,0:T(8,128)(2,1)} %get-tuple-element.60) | copy-start | bytes 589828
  102.8 4.0 %copy-start.4 = (bf16[256,1024]{1,0:T(8,128)(2,1)S(1)}, bf16[256,1024]{1,0:T(8,128)(2,1)}, u32[]{:S(2)}) copy-start(bf16[256,1024]{1,0:T(8,128)(2,1)} %param.8) | copy-start | bytes 1572868
  102.8 22.0 %all-to-all-start = ((bf16[16,384,128]{2,1,0:T(8,128)(2,1)}), bf16[16,384,128]{2,1,0:T(8,128)(2,1)S(1)}, u32[]{:S(2)}, u32[]{:S(2)}) async-start(bf16[16,384,128]{2,1,0:T(8,128)(2,1)} %attend.1), calls=%async_computation | async-start | bytes 3145728 | tf_op jit(solution)/shard_map/all_to_all | solution.py:485
  106.7 4.6 %collective-permute-start.19 = (bf16[768,128]{1,0:T(8,128)(2,1)S(1)}, bf16[768,128]{1,0:T(8,128)(2,1)S(1)}, u32[]{:S(2)}, u32[]{:S(2)}) collective-permute-start(bf16[768,128]{1,0:T(8,128)(2,1)S(1)} %copy-done.20), channel_id=1, source_target_pairs={{0,16},{1,17},{2,18},{3,19},{4,20},{5,21},{6,22},{7,23},{8,24},{9,... | collective-permute-start | bytes 589832 | tf_op jit(solution)/shard_map/ppermute | solution.py:36
  107.5 26.4 %collective-permute-start.23 = (bf16[256,512]{1,0:T(8,128)(2,1)S(1)}, bf16[256,512]{1,0:T(8,128)(2,1)S(1)}, u32[]{:S(2)}, u32[]{:S(2)}) collective-permute-start(bf16[256,512]{1,0:T(8,128)(2,1)S(1)} %get-tuple-element.63), channel_id=1, source_target_pairs={{0,2},{1,3},{2,0},{3,1},{4,6},{5,7},{6,4},{7,5},{8,10},{9,11},{10,... | collective-permute-start | bytes 786440 | tf_op jit(solution)/shard_map/ppermute | solution.py:36
  111.3 13.5 %copy-start.21 = (bf16[768,128]{1,0:T(8,128)(2,1)}, bf16[768,128]{1,0:T(8,128)(2,1)S(1)}, u32[]{:S(2)}) copy-start(bf16[768,128]{1,0:T(8,128)(2,1)S(1)} %collective-permute-done.19.gate_other) | copy-start | bytes 589828
  124.8 1.1 copy-start
  130.6 5.0 %collective-permute-start.20 = (bf16[864,128]{1,0:T(8,128)(2,1)}, bf16[864,128]{1,0:T(8,128)(2,1)S(1)}, u32[]{:S(2)}, u32[]{:S(2)}) collective-permute-start(bf16[864,128]{1,0:T(8,128)(2,1)} %get-tuple-element.62), channel_id=1, source_target_pairs={{0,16},{1,17},{2,18},{3,19},{4,20},{5,21},{6,22},{7,23},{8,24},{9,... | collective-permute-start | bytes 663560 | tf_op jit(solution)/shard_map/ppermute | solution.py:36
  130.7 8.5 %collective-permute-start.21 = (bf16[864,128]{1,0:T(8,128)(2,1)}, bf16[864,128]{1,0:T(8,128)(2,1)S(1)}, u32[]{:S(2)}, u32[]{:S(2)}) collective-permute-start(bf16[864,128]{1,0:T(8,128)(2,1)} %get-tuple-element.62), channel_id=1, source_target_pairs={{0,18},{1,19},{2,16},{3,17},{4,22},{5,23},{6,20},{7,21},{8,26},{9,... | collective-permute-start | bytes 663560 | tf_op jit(solution)/shard_map/ppermute | solution.py:36
  133.6 6.5 %collective-permute-start.22 = (bf16[864,128]{1,0:T(8,128)(2,1)}, bf16[864,128]{1,0:T(8,128)(2,1)S(1)}, u32[]{:S(2)}, u32[]{:S(2)}) collective-permute-start(bf16[864,128]{1,0:T(8,128)(2,1)} %get-tuple-element.61.refs_0_), channel_id=1, source_target_pairs={{0,2},{1,3},{2,0},{3,1},{4,6},{5,7},{6,4},{7,5},{8,10},{9,11},{10,... | collective-permute-start | bytes 663560 | tf_op jit(solution)/shard_map/ppermute | solution.py:36
  133.9 6.2 %copy-start.14 = (bf16[256,512]{1,0:T(8,128)(2,1)}, bf16[256,512]{1,0:T(8,128)(2,1)S(1)}, u32[]{:S(2)}) copy-start(bf16[256,512]{1,0:T(8,128)(2,1)S(1)} %collective-permute-done.23.refs_5_) | copy-start | bytes 786436
  135.6 4.4 %copy-start.15 = (bf16[864,128]{1,0:T(8,128)(2,1)}, bf16[864,128]{1,0:T(8,128)(2,1)S(1)}, u32[]{:S(2)}) copy-start(bf16[864,128]{1,0:T(8,128)(2,1)S(1)} %collective-permute-done.20.refs_1_) | copy-start | bytes 663556
  139.1 0.9 copy-start.16
  140.1 0.7 copy-start.17
  145.0 11.1 %collective-permute-start.24 = (f32[776,256]{1,0:T(8,128)}, f32[776,256]{1,0:T(8,128)S(1)}, u32[]{:S(2)}, u32[]{:S(2)}) collective-permute-start(f32[776,256]{1,0:T(8,128)} %get-tuple-element.65), channel_id=1, source_target_pairs={{0,1},{1,0},{2,3},{3,2},{4,5},{5,4},{6,7},{7,6},{8,9},{9,8},{10,11... | collective-permute-start | bytes 2383880 | tf_op jit(solution)/shard_map/ppermute | solution.py:36
  156.1 0.9 copy-start.1

commit v2 on v1

v2 whole, which is shorter than its diff:
```python
import jax
import jax.numpy as jnp
import numpy as np
from jax import lax
from jax.experimental import pallas as pl
from jax.experimental.pallas import tpu as pltpu
from jax.sharding import Mesh
from jax.sharding import PartitionSpec as P


D = 1024
HDIM = 128
ROWS = 768
SUB = 384
TILES = 16
KEYS = 256
KEY_TILES = 24
TAIL = 16
EPS = 1e-05
AXES = ("z", "yl", "x", "yh", "core")
SIZES = (4, 2, 4, 2, 2)
HALF_SCALE = 0.5 * HDIM ** (-0.5)
FAR = 1 << 24
BF = jnp.bfloat16
F32 = jnp.float32


def send(array, target):
    pairs = []
    for source in range(int(np.prod(SIZES))):
        place = np.unravel_index(source, SIZES)
        dest = [int(t) % n for t, n in zip(target(*[int(p) for p in place]), SIZES)]
        pairs.append((source, int(np.ravel_multi_index(dest, SIZES))))
    return lax.ppermute(array, AXES, pairs)


def flip_core(array):
    return send(array, lambda z, yl, x, yh, c: (z, yl, x, yh, 1 - c))


def to_p1(array):
    return send(array, lambda z, yl, x, yh, c: (z, 1 - yl, x, yh, c))


def to_p2(array):
    return send(array, lambda z, yl, x, yh, c: (z, 1 - yl, x, 1 - yh, c))


def to_p3(array):
    return send(array, lambda z, yl, x, yh, c: (z, yl, x, 1 - yh, c))


def shift_z(array, d):
    return send(array, lambda z, yl, x, yh, c: (z + d, yl, x, yh, c))


def shift_x(array, d):
    return send(array, lambda z, yl, x, yh, c: (z, yl, x + d, yh, c))


def silu_of_half(h):
    return h + h * jnp.tanh(h)


SMEM = pl.BlockSpec(memory_space=pltpu.SMEM)
VMEM = pl.BlockSpec(memory_space=pltpu.VMEM)


def call(kernel, scalars, arrays, outs, limit, scratch=()):
    arrays = [pltpu.with_memory_space_constraint(a, pltpu.VMEM) for a in arrays]
    return pl.pallas_call(
        kernel,
        in_specs=[SMEM] * len(scalars) + [VMEM] * len(arrays),
        out_specs=[VMEM] * len(outs),
        out_shape=[pltpu.VMEM(shape, dtype) for shape, dtype in outs],
        scratch_shapes=list(scratch),
        compiler_params=pltpu.CompilerParams(vmem_limit_bytes=limit << 20),
    )(*scalars, *arrays)


PIECE = 128


def project_rows(info, blocks, gain_ref, w_ref, put):
    gains = [gain_ref[pl.ds(info[3] ^ j, 1), :] for j in range(4)]

    def step(i, carry):
        for r in range(2):
            at = pl.ds(pl.multiple_of((2 * i + r) * PIECE, PIECE), PIECE)
            xs = [p[at, :].astype(F32) for p in blocks]
            total = sum(jnp.sum(v, axis=1, keepdims=True) for v in xs)
            mean = total * (1.0 / D)
            xs = [v - mean for v in xs]
            var = sum(jnp.sum(v * v, axis=1, keepdims=True) for v in xs) * (1.0 / D)
            inv = lax.rsqrt(var + EPS)
            acc = None
            for j, v in enumerate(xs):
                n = (v * inv * gains[j]).astype(BF)
                part = jnp.dot(n, w_ref[j * 256 : (j + 1) * 256, :], preferred_element_type=F32)
                acc = part if acc is None else acc + part
            put(at, silu_of_half(acc * 0.5).astype(BF))
        return carry

    lax.fori_loop(0, ROWS // PIECE // 2, step, 0)


def put_into(gate_ref, q_ref, kv_ref):
    def put(at, y):
        gate_ref[at, :] = y[:, :128]
        q_ref[at, :] = y[:, 256:384]
        kv_ref[at, :128] = y[:, 384:]
        kv_ref[at, 128:] = y[:, 128:256]

    return put


def other_kernel(info, *refs):
    blocks, gain_ref, w_ref = refs[:4], refs[4], refs[5]
    gate_ref, q_ref, kv_ref, w_out = refs[6:]
    for j in range(4):
        rows = pl.ds(pl.multiple_of((info[3] ^ j) * 256, 256), 256)
        for g in range(4):
            cols = pl.ds(pl.multiple_of(g * 256 + info[1] * HDIM, HDIM), HDIM)
            w_out[j * 256 : (j + 1) * 256, g * HDIM : (g + 1) * HDIM] = w_ref[rows, cols]
    project_rows(info, blocks, gain_ref, w_out, put_into(gate_ref, q_ref, kv_ref))


def own_kernel(info, *refs):
    blocks, gain_ref, w_ref, q_other = refs[:4], refs[4], refs[5], refs[6]
    gate_ref, kv_ref, q_refs, q_own = refs[7], refs[8], refs[9:13], refs[13]
    project_rows(info, blocks, gain_ref, w_ref, put_into(gate_ref, q_own, kv_ref))
    for i in range(4):
        source = (q_own, q_other)[i >> 1]
        shift = lax.rem((i ^ (2 * info[1])) - info[0] + 4, 4)
        for d in range(4):

            @pl.when(shift == d)
            def _():
                q_refs[d][...] = source[(i & 1) * SUB : ((i & 1) + 1) * SUB, :]


def project_other(info, blocks, gain, w):
    outs = [((ROWS, HDIM), BF), ((ROWS, HDIM), BF), ((ROWS, 2 * HDIM), BF), ((D, 4 * HDIM), BF)]
    return call(other_kernel, (info,), (*blocks, gain, w), outs, 8)


def project_own(info, blocks, gain, w, q_other):
    outs = [((ROWS, HDIM), BF), ((ROWS, 2 * HDIM), BF)] + [((SUB, HDIM), BF)] * 4
    scratch = [pltpu.VMEM((ROWS, HDIM), BF)]
    return call(own_kernel, (info,), (*blocks, gain, w, q_other), outs, 8, scratch)


LIST = 416


def plan_kernel(info, full_early, edge_early, full_late, edge_late):
    z, yl, x = info[0], info[1], info[2]
    far_z, far_x = lax.rem(z + 2, 4), lax.rem(x + 2, 4)

    def start_of(position):
        s = jnp.int32(0)
        for i in range(8):
            e = info[4 + i]
            s = jnp.maximum(s, jnp.where(e <= position, e, 0))
        return s

    def tiles_upto(position):
        t = position - x * ROWS
        m = lax.div(t, 4 * ROWS)
        r = lax.div(t - m * (4 * ROWS), KEYS)
        count = 3 * m + 1 + jnp.minimum(r, 2)
        return jnp.minimum(jnp.where(t < 0, 0, count), KEY_TILES)

    def list_queries(t, counts):
        first = query_first(info, t)
        begin_last = start_of(first + SUB - 1)
        low = tiles_upto(start_of(first) - KEYS)
        high = tiles_upto(first + SUB - 1)
        near = (t & 3) != far_x

        def list_keys(n, counts):
            fe, ee, fl, el = counts
            k = key_first(info, n)
            early = near & (lax.div(n, 6) != far_z)
            full = (k + KEYS - 1 <= first) & (k >= begin_last)
            entry = t * 32 + n
            full_early[fe] = entry
            edge_early[ee] = entry
            full_late[fl] = entry
            edge_late[el] = entry
            early, full = early.astype(jnp.int32), full.astype(jnp.int32)
            return (
                fe + early * full,
                ee + early * (1 - full),
                fl + (1 - early) * full,
                el + (1 - early) * (1 - full),
            )

        return lax.fori_loop(low, high, list_keys, counts)

    zero = jnp.int32(0)
    fe, ee, fl, el = lax.fori_loop(0, TILES, list_queries, (zero, zero, zero, zero))
    for fulls, nf, edges, ne in ((full_early, fe, edge_early, ee), (full_late, fl, edge_late, el)):
        groups = nf >> 2

        def move(i, ne):
            edges[ne] = fulls[i]
            return ne + 1

        ne = lax.fori_loop(groups * 4, nf, move, ne)
        edges[ne] = 512 + (z * 4 + x) * 32 + z * 6 + 3 * yl
        fulls[LIST - 1] = groups
        edges[LIST - 1] = (ne + 1) >> 1


def query_first(info, t):
    return ((t >> 2) * 8 + (info[0] >> 1) * 4 + (t & 3)) * ROWS + (info[0] & 1) * SUB


def key_first(info, n):
    m = lax.div(n, 3)
    return (m * 4 + info[2]) * ROWS + (n - 3 * m) * KEYS


def plan(info):
    return pl.pallas_call(
        plan_kernel,
        in_specs=[SMEM],
        out_specs=[SMEM] * 4,
        out_shape=[jax.ShapeDtypeStruct((LIST,), jnp.int32)] * 4,
        compiler_params=pltpu.CompilerParams(vmem_limit_bytes=1 << 20),
        name="plan",
    )(info)


def attend_kernel(info, *refs):
    lists, q_refs, kv_refs, out = refs[:4], refs[4:8], refs[8:16], refs[16]
    q, kv, acc, sem = refs[17:]
    z, yl, x = info[0], info[1], info[2]

    def load_queries(e, ref):
        copies = []
        for k in range(4):
            tile = lax.rem(z - k + 4, 4) * 4 + lax.rem(x - e + 4, 4)
            copies.append(
                pltpu.make_async_copy(
                    ref.at[pl.ds(k * SUB, SUB)],
                    q.at[pl.ds(pl.multiple_of(tile * SUB, SUB), SUB)],
                    sem.at[4 * e + k],
                )
            )
        return copies

    def load_keys(k, ref, d, rel):
        block = lax.rem(z - d + 4, 4) * 2 + (yl ^ rel)
        to = kv.at[pl.ds(pl.multiple_of(block * ROWS, ROWS), ROWS)]
        return [pltpu.make_async_copy(ref, to, sem.at[16 + k])]

    queries = [load_queries(e, ref) for e, ref in zip((0, 1, 3, 2), q_refs)]
    places = zip(kv_refs, (0, 0, 1, 1, 3, 3, 2, 2), (0, 1, 0, 1, 0, 1, 0, 1))
    keys = [load_keys(k, *place) for k, place in enumerate(places)]
    early, late = sum(keys[:6] + queries[:3], []), sum(keys[6:] + queries[3:], [])
    for c in early + late:
        c.start()
    acc[...] = jnp.zeros(acc.shape, F32)
    for c in early:
        c.wait()

    def scores(entry):
        t, n = (entry >> 5) & 15, entry & 31
        q_rows = pl.ds(pl.multiple_of(t * SUB, SUB), SUB)
        k_rows = pl.ds(pl.multiple_of(n * KEYS, KEYS), KEYS)
        s = lax.dot_general(
            q[q_rows, :], kv[k_rows, 0:HDIM], (((1,), (1,)), ((), ())), preferred_element_type=F32
        )
        return silu_of_half(s * HALF_SCALE), q_rows, k_rows, t, n

    def add(w, q_rows, k_rows):
        acc[q_rows, :] += jnp.dot(w.astype(BF), kv[k_rows, HDIM:], preferred_element_type=F32)

    def run(full_list, edge_list):
        def full_tiles(i, carry):
            for u in range(4):
                w, q_rows, k_rows, _, _ = scores(full_list[4 * i + u])
                add(w, q_rows, k_rows)
            return carry

        lax.fori_loop(0, full_list[LIST - 1], full_tiles, 0)

        def edge_tiles(i, carry):
            for u in range(2):
                entry = edge_list[2 * i + u]
                w, q_rows, k_rows, t, n = scores(entry)
                first = query_first(info, t)
                col = key_first(info, n) + lax.broadcasted_iota(jnp.int32, (1, KEYS), 1)
                ends = jnp.full((1, KEYS), FAR, jnp.int32)
                for j in range(8):
                    e = info[4 + j]
                    ends = jnp.minimum(ends, jnp.where(col < e, e, FAR))
                row = lax.broadcasted_iota(jnp.int32, (SUB, KEYS), 0)
                skip = (entry >> 9) * FAR
                allowed = (row >= col + (skip - first)) & (row < ends - first)
                add(jnp.where(allowed, w, 0.0), q_rows, k_rows)
            return carry

        lax.fori_loop(0, edge_list[LIST - 1], edge_tiles, 0)

    run(lists[0], lists[1])
    for c in late:
        c.wait()
    run(lists[2], lists[3])
    for t in range(TILES):
        out[t] = acc[t * SUB : (t + 1) * SUB, :].astype(BF)


def attend(info, lists, queries, keyvals):
    return call(
        attend_kernel,
        (info, *lists),
        (*queries, *keyvals),
        [((TILES, SUB, HDIM), BF)],
        limit=24,
        scratch=[
            pltpu.VMEM((TILES * SUB, HDIM), BF),
            pltpu.VMEM((TILES * SUB, 2 * HDIM), BF),
            pltpu.VMEM((TILES * SUB, HDIM), F32),
            pltpu.SemaphoreType.DMA((24,)),
        ],
    )[0]


def gate_kernel(info, part_ref, gate_own, gate_other, own_ref, other_ref):
    ones = jnp.ones((8, HDIM), BF)
    add_lanes = lambda v: lax.dot_general(ones, v, (((1,), (1,)), ((), ())), preferred_element_type=F32)
    for i in range(4):
        gate_ref, out, half = (gate_own, gate_other)[i >> 1], (own_ref, other_ref)[i >> 1], i & 1
        a = (i ^ (2 * info[1])) * 4
        total = part_ref[a].astype(F32)
        for b in range(1, 4):
            total = total + part_ref[a + b].astype(F32)
        at = slice(half * SUB, (half + 1) * SUB)
        out[at, :] = (total * gate_ref[at, :].astype(F32)).astype(BF)
        square = total * total
        top = square.astype(BF)
        sums = add_lanes(top) + add_lanes((square - top.astype(F32)).astype(BF))
        for c in range(SUB // HDIM):
            value = sums[:, c * HDIM : (c + 1) * HDIM]
            top = value.astype(BF)
            to = ROWS + TAIL * (3 * half + c)
            out[to : to + 8, :] = top
            out[to + 8 : to + 16, :] = (value - top.astype(F32)).astype(BF)


def gate_rows(info, parts, gate_own, gate_other):
    outs = [((ROWS + 6 * TAIL, HDIM), BF)] * 2
    return call(gate_kernel, (info,), (parts, gate_own, gate_other), outs, 8)


def mix_kernel(info, *refs):
    rows, w_here, w_there = refs[:4], refs[4], refs[5]
    mine_ref, theirs_ref, squares_ref = refs[6:]
    core = info[3] & 1
    for out, c in ((theirs_ref, 1 - core), (mine_ref, core)):
        cols = pl.ds(pl.multiple_of(c * 256, 256), 256)
        acc = None
        for r, w, flip in zip(rows, (w_here, w_here, w_there, w_there), (0, 1, 1, 0)):
            at = pl.ds(pl.multiple_of((info[1] ^ flip) * HDIM, HDIM), HDIM)
            part = jnp.dot(r[0:ROWS, :], w[at, cols], preferred_element_type=F32)
            acc = part if acc is None else acc + part
        out[0:ROWS, :] = acc
    tail = sum(r[ROWS:, :].astype(F32) for r in rows)
    lines = [tail[TAIL * c : TAIL * c + 1] + tail[TAIL * c + 8 : TAIL * c + 9] for c in range(6)]
    squares = jnp.concatenate(lines + [jnp.zeros((2, HDIM), F32)], axis=0)
    squares_ref[...] = squares
    theirs_ref[ROWS:, 0:HDIM] = squares
    theirs_ref[ROWS:, HDIM:] = squares


def mix(info, gated, w_here, w_there):
    outs = [((ROWS, 256), F32), ((ROWS + 8, 256), F32), ((8, HDIM), F32)]
    return call(mix_kernel, (info,), (*gated, w_here, w_there), outs, 12)


def finish_kernel(mine_ref, got_ref, squares_ref, ev_ref, out_ref, rows, sem):
    inv = lax.rsqrt((squares_ref[...] + got_ref[ROWS:, 0:HDIM]) * (1.0 / D) + EPS)
    eye = lax.broadcasted_iota(jnp.int32, (HDIM, HDIM), 0) == lax.broadcasted_iota(jnp.int32, (HDIM, HDIM), 1)
    copies = []
    for k in range(6):
        column = jnp.sum(jnp.where(eye, inv[k : k + 1, :], 0.0), axis=1, keepdims=True)
        at = slice(k * HDIM, (k + 1) * HDIM)
        total = mine_ref[at, :] + got_ref[at, :]
        rows[at, :] = (ev_ref[at, :].astype(F32) + total * column).astype(BF)
        copies.append(pltpu.make_async_copy(rows.at[at], out_ref.at[at], sem.at[k]))
        copies[-1].start()
    for c in copies:
        c.wait()


def finish(mine, got, squares, events):
    arrays = [pltpu.with_memory_space_constraint(a, pltpu.VMEM) for a in (mine, got, squares, events)]
    return pl.pallas_call(
        finish_kernel,
        in_specs=[VMEM] * 4,
        out_specs=pl.BlockSpec(memory_space=pl.ANY),
        out_shape=jax.ShapeDtypeStruct((ROWS, 256), BF),
        scratch_shapes=[pltpu.VMEM((ROWS, 256), BF), pltpu.SemaphoreType.DMA((6,))],
        compiler_params=pltpu.CompilerParams(vmem_limit_bytes=8 << 20),
        name="finish",
    )(*arrays)


def layer(events, norm_gain, w_uvqk, w_out, lengths):
    z, yl, x = (lax.axis_index(a).astype(jnp.int32) for a in ("z", "yl", "x"))
    yh = lax.axis_index("yh").astype(jnp.int32)
    o = yh * 2 + lax.axis_index("core").astype(jnp.int32)
    info = jnp.concatenate([jnp.stack([z, yl, x, o]), jnp.cumsum(lengths).astype(jnp.int32)])

    p1, p2, p3 = to_p1(events), to_p2(events), to_p3(events)
    c0 = flip_core(events)
    w_in = w_uvqk.reshape(D, 4 * 256)
    gain = norm_gain.reshape(4, 256)
    p1, w_in, info, gain = lax.optimization_barrier((p1, w_in, info, gain))
    c1, c2, c3 = flip_core(p1), flip_core(p2), flip_core(p3)

    gate_other, q_other, kv_other, w_in = project_other(info, (p1, c1, p2, c2), gain, w_in)
    gate_own, kv_own, *pieces = project_own(info, (events, c0, p3, c3), gain, w_in, q_other)

    pieces = [pieces[0]] + [shift_z(pieces[d], d) for d in (1, 2, 3)]
    up_other, down_other = shift_z(kv_other, 1), shift_z(kv_other, -1)
    up_own, down_own = shift_z(kv_own, 1), shift_z(kv_own, -1)

    q_mine = jnp.concatenate(pieces, axis=0)
    queries = [q_mine] + [shift_x(q_mine, e) for e in (1, 3, 2)]
    near, away = shift_z(up_own, 1), shift_z(down_other, -1)

    keyvals = [kv_own, kv_other, up_own, up_other, down_own, down_other, near, away]
    lists = plan(info)
    parts = attend(info, lists, queries, keyvals)

    w_here = lax.dynamic_slice_in_dim(w_out, yh * 512, 512, 1)
    w_away = lax.dynamic_slice_in_dim(w_out, (1 - yh) * 512, 512, 1)
    w_away, _ = lax.optimization_barrier((w_away, q_mine))
    w_there = to_p3(w_away)

    parts = lax.all_to_all(parts, ("z", "x"), 0, 0)
    own, other = gate_rows(info, parts, gate_own, gate_other)
    gated = [own, to_p1(other), to_p2(other), to_p3(own)]
    mine, theirs, squares = mix(info, gated, w_here, w_there)
    return finish(mine, flip_core(theirs), squares, events)


def solution(mesh):
    fine = Mesh(mesh.devices.reshape(SIZES), AXES)
    ctx, head = ("z", "yl", "x"), ("yh", "core")
    in_specs = (P(ctx, head), P(), P(None, None, head), P(head, None), P())
    return jax.shard_map(layer, mesh=fine, in_specs=in_specs, out_specs=P(ctx, head), check_vma=False)
```

time: 161 us -> 151 us (0.938)
  waiting for transfers between devices: 52.1 us -> 63.8 us
  Pallas kernels: 48.9 us -> 37.4 us
  local copies, waits for them, and re-layouts: 12.3 us -> 3.35 us
    pallas_call x7, Pallas kernels: 48.9 us -> 37.4 us  [the longest x5 32.7 us: call(): pl.pallas_call(kernel, in_specs=[SMEM] * len(scalars) + [VMEM] * len(arra...]
    ppermute x25 -> x24, waiting for transfers between devices: 38.6 us -> 49.7 us  [send(): return lax.ppermute(array, AXES, pairs)]
    unnamed x54 -> x10, local copies, waits for them, and re-layouts: 9.26 us -> 2.17 us
    ppermute x25 -> x24, starting transfers between devices: 41.9 us -> 41.4 us  [send(): return lax.ppermute(array, AXES, pairs)]
  transfers between devices with their start and end apart: 26 -> 25, of which waited for: 14 -> 12; matrix products, arithmetic and copies ran while one was open for 4% -> 2% of each run, Pallas kernels for 9% -> 5%
where the time goes in v2:
time: 151 us; the launch traced here: 150 us
  waiting for transfers between devices  63.8 us (42%)
  starting transfers between devices  45.1 us (30%)
  Pallas kernels  37.4 us (25%)
  local copies, waits for them, and re-layouts  3.35 us (2%)
    ppermute x24, waiting for transfers between devices, send(): return lax.ppermute(array, AXES, pairs)  49.7 us
    ppermute x24, starting transfers between devices, send(): return lax.ppermute(array, AXES, pairs)  41.4 us
    pallas_call x5, Pallas kernels, call(): pl.pallas_call(kernel, in_specs=[SMEM] * len(scalars) + [VMEM] * len(arra...  32.7 us
    all_to_all x1, waiting for transfers between devices, layer(): parts = lax.all_to_all(parts, ('z', 'x'), 0, 0)  14.1 us
    pallas_call x1, Pallas kernels, plan(): pl.pallas_call(plan_kernel, in_specs=[SMEM], out_specs=[SMEM] * 4, out_sh...  3.8 us
    all_to_all x1, starting transfers between devices, layer(): parts = lax.all_to_all(parts, ('z', 'x'), 0, 0)  3.72 us
  transfers between devices with their start and end apart: 25, of which 12 were waited for; matrix products, arithmetic and copies ran while one was open for 2% of the time, Pallas kernels for 5%

profile of v2, /device:TPU:1, one launch (start us, length us, event | category | flops | bytes accessed | tf_op | source)
XLA Modules:
  0.0 150.3 jit_solution(729922121281544888)
XLA Ops:
  0.0 2.1 %collective-permute-start = (bf16[768,256]{1,0:T(8,128)(2,1)}, bf16[768,256]{1,0:T(8,128)(2,1)S(1)}, u32[]{:S(2)}, u32[]{:S(2)}) collective-permute-start(bf16[768,256]{1,0:T(8,128)(2,1)} %ev_ref.1), channel_id=1, source_target_pairs={{0,16},{1,17},{2,18},{3,19},{4,20},{5,21},{6,22},{7,23},{8,24},{9,... | collective-permute-start | bytes 1179656 | tf_op jit(solution)/shard_map/ppermute | solution.py:34
  2.1 1.9 %collective-permute-start.5 = (bf16[768,256]{1,0:T(8,128)(2,1)}, bf16[768,256]{1,0:T(8,128)(2,1)}, u32[]{:S(2)}, u32[]{:S(2)}) collective-permute-start(bf16[768,256]{1,0:T(8,128)(2,1)} %ev_ref.1), channel_id=1, source_target_pairs={{0,18},{1,19},{2,16},{3,17},{4,22},{5,23},{6,20},{7,21},{8,26},{9,... | collective-permute-start | bytes 1179656 | tf_op jit(solution)/shard_map/ppermute | solution.py:34
  4.0 0.7 collective-permute-start.2
  4.7 2.1 %copy.6 = bf16[128,8,4,256]{3,1,2,0:T(8,128)(2,1)S(1)} copy(bf16[128,8,4,256]{3,2,1,0:T(4,128)(2,1)} %bitcast.9) | data formatting | bytes 4194304
  6.9 0.0 copy-done.1
  6.9 0.0 copy-done.2
  6.9 0.2 reduce-window.9
  7.1 0.1 concatenate.6.info
  7.2 3.7 %collective-permute-done.refs_0_ = bf16[768,256]{1,0:T(8,128)(2,1)S(1)} collective-permute-done((bf16[768,256]{1,0:T(8,128)(2,1)}, bf16[768,256]{1,0:T(8,128)(2,1)S(1)}, u32[]{:S(2)}, u32[]{:S(2)}) %collective-permute-start) | collective-permute-done | bytes 393248 | tf_op jit(solution)/shard_map/ppermute | solution.py:34
  10.9 2.7 %collective-permute-start.4 = (bf16[768,256]{1,0:T(8,128)(2,1)S(1)}, bf16[768,256]{1,0:T(8,128)(2,1)S(1)}, u32[]{:S(2)}, u32[]{:S(2)}) collective-permute-start(bf16[768,256]{1,0:T(8,128)(2,1)S(1)} %collective-permute-done.refs_0_), channel_id=1, source_target_pairs={{0,1},{1,0},{2,3},{3,2},{4,5},{5,4},{6,7},{7,6},{8,9},{9,8},{10,11... | collective-permute-start | bytes 1179656 | tf_op jit(solution)/shard_map/ppermute | solution.py:34
  13.6 6.6 %collective-permute-done.5.refs_2_ = bf16[768,256]{1,0:T(8,128)(2,1)} collective-permute-done((bf16[768,256]{1,0:T(8,128)(2,1)}, bf16[768,256]{1,0:T(8,128)(2,1)}, u32[]{:S(2)}, u32[]{:S(2)}) %collective-permute-start.5) | collective-permute-done | bytes 393248 | tf_op jit(solution)/shard_map/ppermute | solution.py:34
  20.1 2.0 %collective-permute-start.6 = (bf16[768,256]{1,0:T(8,128)(2,1)}, bf16[768,256]{1,0:T(8,128)(2,1)S(1)}, u32[]{:S(2)}, u32[]{:S(2)}) collective-permute-start(bf16[768,256]{1,0:T(8,128)(2,1)} %collective-permute-done.5.refs_2_), channel_id=1, source_target_pairs={{0,1},{1,0},{2,3},{3,2},{4,5},{5,4},{6,7},{7,6},{8,9},{9,8},{10,11... | collective-permute-start | bytes 1179656 | tf_op jit(solution)/shard_map/ppermute | solution.py:34
  22.1 0.0 copy-done
  22.1 0.0 collective-permute-start.1
  22.1 0.0 collective-permute-done.2.refs_2_
  22.1 1.4 collective-permute-start.3
  23.5 0.0 collective-permute-done.4.refs_1_
  23.5 0.2 collective-permute-done.6.refs_3_
  23.6 3.4 %shard_map.55 = (bf16[768,128]{1,0:T(8,128)(2,1)S(1)}, bf16[768,128]{1,0:T(8,128)(2,1)S(1)}, bf16[768,256]{1,0:T(8,128)(2,1)S(1)}, bf16[1024,512]{1,0:T(8,128)(2,1)S(1)}) custom-call(s32[12]{0:T(128)S(1)} %concatenate.6.info, bf16[768,256]{1,0:T(8,128)(2,1)S(1)} %collective-permute-done.refs_0_, bf16[768,256]{1,0:T(8,128)(2,1)S(1)} %collective-permute-done.4.refs_1_, ...), custom_call_target="tpu_custom_call" | custom-call | tf_op jit(solution)/shard_map/pallas_call | solution.py:71
  27.0 0.0 collective-permute-done.1.refs_1_
  27.0 0.0 collective-permute-done.3.refs_3_
  27.0 2.8 %shard_map.56 = (bf16[768,128]{1,0:T(8,128)(2,1)S(1)}, bf16[768,256]{1,0:T(8,128)(2,1)S(1)}, bf16[384,128]{1,0:T(8,128)(2,1)S(1)}, bf16[384,128]{1,0:T(8,128)(2,...) custom-call(s32[12]{0:T(128)S(1)} %concatenate.6.info, bf16[768,256]{1,0:T(8,128)(2,1)S(1)} %copy-done, ...), custom_call_target="tpu_custom_call" | custom-call | tf_op jit(solution)/shard_map/pallas_call | solution.py:71
  29.8 1.7 %collective-permute-start.13 = (bf16[768,256]{1,0:T(8,128)(2,1)S(1)}, bf16[768,256]{1,0:T(8,128)(2,1)S(1)}, u32[]{:S(2)}, u32[]{:S(2)}) collective-permute-start(bf16[768,256]{1,0:T(8,128)(2,1)S(1)} %get-tuple-element.43.refs_8_), channel_id=1, source_target_pairs={{0,32},{1,33},{2,34},{3,35},{4,36},{5,37},{6,38},{7,39},{8,40},{9,... | collective-permute-start | bytes 1179656 | tf_op jit(solution)/shard_map/ppermute | solution.py:34
  31.5 2.2 %collective-permute-start.15 = (bf16[768,256]{1,0:T(8,128)(2,1)S(1)}, bf16[768,256]{1,0:T(8,128)(2,1)S(1)}, u32[]{:S(2)}, u32[]{:S(2)}) collective-permute-start(bf16[768,256]{1,0:T(8,128)(2,1)S(1)} %get-tuple-element.43.refs_8_), channel_id=1, source_target_pairs={{0,96},{1,97},{2,98},{3,99},{4,100},{5,101},{6,102},{7,103},{8,104... | collective-permute-start | bytes 1179656 | tf_op jit(solution)/shard_map/ppermute | solution.py:34
  33.7 1.4 collective-permute-start.16
  35.1 0.1 collective-permute-start.14
  35.2 0.0 collective-permute-start.7
  35.2 18.1 %collective-permute-done.7 = bf16[384,128]{1,0:T(8,128)(2,1)S(1)} collective-permute-done((bf16[384,128]{1,0:T(8,128)(2,1)S(1)}, bf16[384,128]{1,0:T(8,128)(2,1)S(1)}, u32[]{:S(2)}, u32[]{:S(2)}) %collective-permute-start.7) | collective-permute-done | bytes 98336 | tf_op jit(solution)/shard_map/ppermute | solution.py:34
  53.3 1.0 collective-permute-start.8
  54.3 4.0 %collective-permute-done.8 = bf16[384,128]{1,0:T(8,128)(2,1)S(1)} collective-permute-done((bf16[384,128]{1,0:T(8,128)(2,1)S(1)}, bf16[384,128]{1,0:T(8,128)(2,1)S(1)}, u32[]{:S(2)}, u32[]{:S(2)}) %collective-permute-start.8) | collective-permute-done | bytes 98336 | tf_op jit(solution)/shard_map/ppermute | solution.py:34
  58.3 1.2 collective-permute-start.9
  59.5 2.3 %collective-permute-done.9 = bf16[384,128]{1,0:T(8,128)(2,1)S(1)} collective-permute-done((bf16[384,128]{1,0:T(8,128)(2,1)S(1)}, bf16[384,128]{1,0:T(8,128)(2,1)S(1)}, u32[]{:S(2)}, u32[]{:S(2)}) %collective-permute-start.9) | collective-permute-done | bytes 98336 | tf_op jit(solution)/shard_map/ppermute | solution.py:34
  61.7 1.3 collective-permute-start.10
  63.0 0.0 collective-permute-done.13.refs_10_
  63.0 1.5 collective-permute-start.11
  64.5 0.0 collective-permute-done.15.refs_12_
  64.5 1.5 %collective-permute-start.12 = (bf16[1536,128]{1,0:T(8,128)(2,1)S(1)}, bf16[1536,128]{1,0:T(8,128)(2,1)S(1)}, u32[]{:S(2)}, u32[]{:S(2)}) collective-permute-start(bf16[1536,128]{1,0:T(8,128)(2,1)S(1)} %constant_dynamic-update-slice_fusion.refs_4_), channel_id=1, source_target_pairs={{0,8},{1,9},{2,10},{3,11},{4,12},{5,13},{6,14},{7,15},{8,0},{9,1},... | collective-permute-start | bytes 1179656 | tf_op jit(solution)/shard_map/ppermute | solution.py:34
  66.0 0.0 collective-permute-done.16.refs_13_
  66.0 0.0 collective-permute-start.17
  66.0 0.0 collective-permute-done.14.refs_11_
  66.0 2.7 %collective-permute-start.18 = (bf16[768,256]{1,0:T(8,128)(2,1)S(1)}, bf16[768,256]{1,0:T(8,128)(2,1)S(1)}, u32[]{:S(2)}, u32[]{:S(2)}) collective-permute-start(bf16[768,256]{1,0:T(8,128)(2,1)S(1)} %collective-permute-done.16.refs_13_), channel_id=1, source_target_pairs={{0,96},{1,97},{2,98},{3,99},{4,100},{5,101},{6,102},{7,103},{8,104... | collective-permute-start | bytes 1179656 | tf_op jit(solution)/shard_map/ppermute | solution.py:34
  68.7 3.8 %plan.1 = (s32[416]{0:T(512)S(1)}, s32[416]{0:T(512)S(1)}, s32[416]{0:T(512)S(1)}, s32[416]{0:T(512)S(1)}) custom-call(s32[12]{0:T(128)S(1)} %concatenate.6.info), custom_call_target="tpu_custom_call" | custom-call | tf_op jit(solution)/shard_map/plan/pallas_call | solution.py:226
  72.5 0.0 collective-permute-done.10.refs_5_
  72.5 0.0 collective-permute-done.11.refs_6_
  72.5 7.4 %collective-permute-done.12.refs_7_ = bf16[1536,128]{1,0:T(8,128)(2,1)S(1)} collective-permute-done((bf16[1536,128]{1,0:T(8,128)(2,1)S(1)}, bf16[1536,128]{1,0:T(8,128)(2,1)S(1)}, u32[]{:S(2)}, u32[]{:S(2)}) %collective-permute-start.12) | collective-permute-done | bytes 393248 | tf_op jit(solution)/shard_map/ppermute | solution.py:34
  79.9 0.0 collective-permute-done.17.refs_14_
  79.9 0.0 collective-permute-done.18.refs_15_
  79.9 24.1 %shard_map.57 = bf16[16,384,128]{2,1,0:T(8,128)(2,1)} custom-call(s32[12]{0:T(128)S(1)} %concatenate.6.info, s32[416]{0:T(512)S(1)} %get-tuple-element.30.refs_0_, s32[416]{0:T(512)S(1)} %get-tuple-element.31.refs_1_, s32[416]{0:T(512)S(1)} %get-tuple-element.32.refs_2_, s32[416]{0:T(512)S(1)} %get-tuple-element.33.refs_3_, ...), custom_call_target="tpu_custom_call" | custom-call | tf_op jit(solution)/shard_map/pallas_call | solution.py:71
  104.0 3.7 %all-to-all-start = ((bf16[16,384,128]{2,1,0:T(8,128)(2,1)}), bf16[16,384,128]{2,1,0:T(8,128)(2,1)S(1)}, u32[]{:S(2)}, u32[]{:S(2)}) async-start(bf16[16,384,128]{2,1,0:T(8,128)(2,1)} %shard_map.57), calls=%async_computation | async-start | bytes 3145728 | tf_op jit(solution)/shard_map/all_to_all | solution.py:445
  107.7 1.1 constant_dynamic-slice_fusion
  108.8 3.2 %collective-permute-start.22 = (bf16[256,512]{1,0:T(8,128)(2,1)S(1)}, bf16[256,512]{1,0:T(8,128)(2,1)S(1)}, u32[]{:S(2)}, u32[]{:S(2)}) collective-permute-start(bf16[256,512]{1,0:T(8,128)(2,1)S(1)} %get-tuple-element.49), channel_id=1, source_target_pairs={{0,2},{1,3},{2,0},{3,1},{4,6},{5,7},{6,4},{7,5},{8,10},{9,11},{10,... | collective-permute-start | bytes 786440 | tf_op jit(solution)/shard_map/ppermute | solution.py:34
  111.9 14.1 %all-to-all-done.part_ref = bf16[16,384,128]{2,1,0:T(8,128)(2,1)S(1)} async-done(((bf16[16,384,128]{2,1,0:T(8,128)(2,1)}), bf16[16,384,128]{2,1,0:T(8,128)(2,1)S(1)}, u32[]{:S(2)}, u32[]{:S(2)}) %all-to-all-start) | async-done | bytes 1572896 | tf_op jit(solution)/shard_map/all_to_all | solution.py:445
  126.0 1.0 shard_map.58
  127.1 0.5 collective-permute-start.19
  127.5 3.1 %collective-permute-start.20 = (bf16[864,128]{1,0:T(8,128)(2,1)S(1)}, bf16[864,128]{1,0:T(8,128)(2,1)S(1)}, u32[]{:S(2)}, u32[]{:S(2)}) collective-permute-start(bf16[864,128]{1,0:T(8,128)(2,1)S(1)} %get-tuple-element.48), channel_id=1, source_target_pairs={{0,18},{1,19},{2,16},{3,17},{4,22},{5,23},{6,20},{7,21},{8,26},{9,... | collective-permute-start | bytes 663560 | tf_op jit(solution)/shard_map/ppermute | solution.py:34
  130.6 1.1 collective-permute-start.21
  131.7 0.0 collective-permute-done.22.refs_5_
  131.7 0.5 collective-permute-done.19.refs_1_
  132.2 3.7 %collective-permute-done.20.refs_2_ = bf16[864,128]{1,0:T(8,128)(2,1)S(1)} collective-permute-done((bf16[864,128]{1,0:T(8,128)(2,1)S(1)}, bf16[864,128]{1,0:T(8,128)(2,1)S(1)}, u32[]{:S(2)}, u32[]{:S(2)}) %collective-permute-start.20) | collective-permute-done | bytes 221216 | tf_op jit(solution)/shard_map/ppermute | solution.py:34
  135.9 1.5 %collective-permute-done.21.refs_3_ = bf16[864,128]{1,0:T(8,128)(2,1)S(1)} collective-permute-done((bf16[864,128]{1,0:T(8,128)(2,1)S(1)}, bf16[864,128]{1,0:T(8,128)(2,1)S(1)}, u32[]{:S(2)}, u32[]{:S(2)}) %collective-permute-start.21) | collective-permute-done | bytes 221216 | tf_op jit(solution)/shard_map/ppermute | solution.py:34
  137.4 1.5 %shard_map.59 = (f32[768,256]{1,0:T(8,128)S(1)}, f32[776,256]{1,0:T(8,128)S(1)}, f32[8,128]{1,0:T(8,128)S(1)}) custom-call(s32[12]{0:T(128)S(1)} %concatenate.6.info, bf16[864,128]{1,0:T(8,128)(2,1)S(1)} %get-tuple-element.47.refs_0_, bf16[864,128]{1,0:T(8,128)(2,1)S(1)} %collective-permute-done.19.refs_1_, ...), custom_call_target="tpu_custom_call" | custom-call | tf_op jit(solution)/shard_map/pallas_call | solution.py:71
  138.9 8.3 %collective-permute-start.23 = (f32[776,256]{1,0:T(8,128)S(1)}, f32[776,256]{1,0:T(8,128)S(1)}, u32[]{:S(2)}, u32[]{:S(2)}) collective-permute-start(f32[776,256]{1,0:T(8,128)S(1)} %get-tuple-element.51), channel_id=1, source_target_pairs={{0,1},{1,0},{2,3},{3,2},{4,5},{5,4},{6,7},{7,6},{8,9},{9,8},{10,11... | collective-permute-start | bytes 2383880 | tf_op jit(solution)/shard_map/ppermute | solution.py:34
  147.3 1.9 %collective-permute-done.23.got_ref = f32[776,256]{1,0:T(8,128)S(1)} collective-permute-done((f32[776,256]{1,0:T(8,128)S(1)}, f32[776,256]{1,0:T(8,128)S(1)}, u32[]{:S(2)}, u32[]{:S(2)}) %collective-permute-start.23) | collective-permute-done | bytes 794656 | tf_op jit(solution)/shard_map/ppermute | solution.py:34
  149.2 0.9 finish.1
  (8 shorter events, 0.1 us)
Async XLA Ops:
  0.0 10.9 %collective-permute-start = (bf16[768,256]{1,0:T(8,128)(2,1)}, bf16[768,256]{1,0:T(8,128)(2,1)S(1)}, u32[]{:S(2)}, u32[]{:S(2)}) collective-permute-start(bf16[768,256]{1,0:T(8,128)(2,1)} %ev_ref.1), channel_id=1, source_target_pairs={{0,16},{1,17},{2,18},{3,19},{4,20},{5,21},{6,22},{7,23},{8,24},{9,... | collective-permute-start | bytes 1179656 | tf_op jit(solution)/shard_map/ppermute | solution.py:34
  2.1 18.0 %collective-permute-start.5 = (bf16[768,256]{1,0:T(8,128)(2,1)}, bf16[768,256]{1,0:T(8,128)(2,1)}, u32[]{:S(2)}, u32[]{:S(2)}) collective-permute-start(bf16[768,256]{1,0:T(8,128)(2,1)} %ev_ref.1), channel_id=1, source_target_pairs={{0,18},{1,19},{2,16},{3,17},{4,22},{5,23},{6,20},{7,21},{8,26},{9,... | collective-permute-start | bytes 1179656 | tf_op jit(solution)/shard_map/ppermute | solution.py:34
  4.0 18.1 %collective-permute-start.2 = (bf16[768,256]{1,0:T(8,128)(2,1)}, bf16[768,256]{1,0:T(8,128)(2,1)S(1)}, u32[]{:S(2)}, u32[]{:S(2)}) collective-permute-start(bf16[768,256]{1,0:T(8,128)(2,1)} %ev_ref.1), channel_id=1, source_target_pairs={{0,2},{1,3},{2,0},{3,1},{4,6},{5,7},{6,4},{7,5},{8,10},{9,11},{10,... | collective-permute-start | bytes 1179656 | tf_op jit(solution)/shard_map/ppermute | solution.py:34
  4.7 2.1 %copy-start.1 = (f32[1024]{0:T(1024)S(1)}, f32[1024]{0:T(1024)}, u32[]{:S(2)}) copy-start(f32[1024]{0:T(1024)} %param.6) | copy-start | bytes 12292
  4.7 2.2 %copy-start.2 = (s32[8]{0:T(128)S(1)}, s32[8]{0:T(128)}, u32[]{:S(2)}) copy-start(s32[8]{0:T(128)} %param.9) | copy-start | bytes 100
  4.7 17.3 %copy-start = (bf16[768,256]{1,0:T(8,128)(2,1)S(1)}, bf16[768,256]{1,0:T(8,128)(2,1)}, u32[]{:S(2)}) copy-start(bf16[768,256]{1,0:T(8,128)(2,1)} %ev_ref.1) | copy-start | bytes 1179652
  10.9 12.6 %collective-permute-start.4 = (bf16[768,256]{1,0:T(8,128)(2,1)S(1)}, bf16[768,256]{1,0:T(8,128)(2,1)S(1)}, u32[]{:S(2)}, u32[]{:S(2)}) collective-permute-start(bf16[768,256]{1,0:T(8,128)(2,1)S(1)} %collective-permute-done.refs_0_), channel_id=1, source_target_pairs={{0,1},{1,0},{2,3},{3,2},{4,5},{5,4},{6,7},{7,6},{8,9},{9,8},{10,11... | collective-permute-start | bytes 1179656 | tf_op jit(solution)/shard_map/ppermute | solution.py:34
  20.1 3.5 %collective-permute-start.6 = (bf16[768,256]{1,0:T(8,128)(2,1)}, bf16[768,256]{1,0:T(8,128)(2,1)S(1)}, u32[]{:S(2)}, u32[]{:S(2)}) collective-permute-start(bf16[768,256]{1,0:T(8,128)(2,1)} %collective-permute-done.5.refs_2_), channel_id=1, source_target_pairs={{0,1},{1,0},{2,3},{3,2},{4,5},{5,4},{6,7},{7,6},{8,9},{9,8},{10,11... | collective-permute-start | bytes 1179656 | tf_op jit(solution)/shard_map/ppermute | solution.py:34
  22.1 4.9 %collective-permute-start.1 = (bf16[768,256]{1,0:T(8,128)(2,1)S(1)}, bf16[768,256]{1,0:T(8,128)(2,1)S(1)}, u32[]{:S(2)}, u32[]{:S(2)}) collective-permute-start(bf16[768,256]{1,0:T(8,128)(2,1)S(1)} %copy-done), channel_id=1, source_target_pairs={{0,1},{1,0},{2,3},{3,2},{4,5},{5,4},{6,7},{7,6},{8,9},{9,8},{10,11... | collective-permute-start | bytes 1179656 | tf_op jit(solution)/shard_map/ppermute | solution.py:34
  22.1 4.9 %collective-permute-start.3 = (bf16[768,256]{1,0:T(8,128)(2,1)S(1)}, bf16[768,256]{1,0:T(8,128)(2,1)S(1)}, u32[]{:S(2)}, u32[]{:S(2)}) collective-permute-start(bf16[768,256]{1,0:T(8,128)(2,1)S(1)} %collective-permute-done.2.refs_2_), channel_id=1, source_target_pairs={{0,1},{1,0},{2,3},{3,2},{4,5},{5,4},{6,7},{7,6},{8,9},{9,8},{10,11... | collective-permute-start | bytes 1179656 | tf_op jit(solution)/shard_map/ppermute | solution.py:34
  29.8 33.2 %collective-permute-start.13 = (bf16[768,256]{1,0:T(8,128)(2,1)S(1)}, bf16[768,256]{1,0:T(8,128)(2,1)S(1)}, u32[]{:S(2)}, u32[]{:S(2)}) collective-permute-start(bf16[768,256]{1,0:T(8,128)(2,1)S(1)} %get-tuple-element.43.refs_8_), channel_id=1, source_target_pairs={{0,32},{1,33},{2,34},{3,35},{4,36},{5,37},{6,38},{7,39},{8,40},{9,... | collective-permute-start | bytes 1179656 | tf_op jit(solution)/shard_map/ppermute | solution.py:34
  31.5 33.0 %collective-permute-start.15 = (bf16[768,256]{1,0:T(8,128)(2,1)S(1)}, bf16[768,256]{1,0:T(8,128)(2,1)S(1)}, u32[]{:S(2)}, u32[]{:S(2)}) collective-permute-start(bf16[768,256]{1,0:T(8,128)(2,1)S(1)} %get-tuple-element.43.refs_8_), channel_id=1, source_target_pairs={{0,96},{1,97},{2,98},{3,99},{4,100},{5,101},{6,102},{7,103},{8,104... | collective-permute-start | bytes 1179656 | tf_op jit(solution)/shard_map/ppermute | solution.py:34
  33.7 32.3 %collective-permute-start.16 = (bf16[768,256]{1,0:T(8,128)(2,1)S(1)}, bf16[768,256]{1,0:T(8,128)(2,1)S(1)}, u32[]{:S(2)}, u32[]{:S(2)}) collective-permute-start(bf16[768,256]{1,0:T(8,128)(2,1)S(1)} %get-tuple-element.44.refs_9_), channel_id=1, source_target_pairs={{0,96},{1,97},{2,98},{3,99},{4,100},{5,101},{6,102},{7,103},{8,104... | collective-permute-start | bytes 1179656 | tf_op jit(solution)/shard_map/ppermute | solution.py:34
  35.1 30.9 %collective-permute-start.14 = (bf16[768,256]{1,0:T(8,128)(2,1)S(1)}, bf16[768,256]{1,0:T(8,128)(2,1)S(1)}, u32[]{:S(2)}, u32[]{:S(2)}) collective-permute-start(bf16[768,256]{1,0:T(8,128)(2,1)S(1)} %get-tuple-element.44.refs_9_), channel_id=1, source_target_pairs={{0,32},{1,33},{2,34},{3,35},{4,36},{5,37},{6,38},{7,39},{8,40},{9,... | collective-permute-start | bytes 1179656 | tf_op jit(solution)/shard_map/ppermute | solution.py:34
  35.2 18.1 %collective-permute-start.7 = (bf16[384,128]{1,0:T(8,128)(2,1)S(1)}, bf16[384,128]{1,0:T(8,128)(2,1)S(1)}, u32[]{:S(2)}, u32[]{:S(2)}) collective-permute-start(bf16[384,128]{1,0:T(8,128)(2,1)S(1)} %get-tuple-element.40), channel_id=1, source_target_pairs={{0,32},{1,33},{2,34},{3,35},{4,36},{5,37},{6,38},{7,39},{8,40},{9,... | collective-permute-start | bytes 294920 | tf_op jit(solution)/shard_map/ppermute | solution.py:34
  53.3 5.0 %collective-permute-start.8 = (bf16[384,128]{1,0:T(8,128)(2,1)S(1)}, bf16[384,128]{1,0:T(8,128)(2,1)S(1)}, u32[]{:S(2)}, u32[]{:S(2)}) collective-permute-start(bf16[384,128]{1,0:T(8,128)(2,1)S(1)} %get-tuple-element.41), channel_id=1, source_target_pairs={{0,64},{1,65},{2,66},{3,67},{4,68},{5,69},{6,70},{7,71},{8,72},{9,... | collective-permute-start | bytes 294920 | tf_op jit(solution)/shard_map/ppermute | solution.py:34
  58.3 3.5 %collective-permute-start.9 = (bf16[384,128]{1,0:T(8,128)(2,1)S(1)}, bf16[384,128]{1,0:T(8,128)(2,1)S(1)}, u32[]{:S(2)}, u32[]{:S(2)}) collective-permute-start(bf16[384,128]{1,0:T(8,128)(2,1)S(1)} %get-tuple-element.42), channel_id=1, source_target_pairs={{0,96},{1,97},{2,98},{3,99},{4,100},{5,101},{6,102},{7,103},{8,104... | collective-permute-start | bytes 294920 | tf_op jit(solution)/shard_map/ppermute | solution.py:34
  61.7 10.8 %collective-permute-start.10 = (bf16[1536,128]{1,0:T(8,128)(2,1)S(1)}, bf16[1536,128]{1,0:T(8,128)(2,1)S(1)}, u32[]{:S(2)}, u32[]{:S(2)}) collective-permute-start(bf16[1536,128]{1,0:T(8,128)(2,1)S(1)} %constant_dynamic-update-slice_fusion.refs_4_), channel_id=1, source_target_pairs={{0,4},{1,5},{2,6},{3,7},{4,8},{5,9},{6,10},{7,11},{8,12},{9,13},{1... | collective-permute-start | bytes 1179656 | tf_op jit(solution)/shard_map/ppermute | solution.py:34
  63.0 9.5 %collective-permute-start.11 = (bf16[1536,128]{1,0:T(8,128)(2,1)S(1)}, bf16[1536,128]{1,0:T(8,128)(2,1)S(1)}, u32[]{:S(2)}, u32[]{:S(2)}) collective-permute-start(bf16[1536,128]{1,0:T(8,128)(2,1)S(1)} %constant_dynamic-update-slice_fusion.refs_4_), channel_id=1, source_target_pairs={{0,12},{1,13},{2,14},{3,15},{4,0},{5,1},{6,2},{7,3},{8,4},{9,5},{1... | collective-permute-start | bytes 1179656 | tf_op jit(solution)/shard_map/ppermute | solution.py:34
  64.5 15.4 %collective-permute-start.12 = (bf16[1536,128]{1,0:T(8,128)(2,1)S(1)}, bf16[1536,128]{1,0:T(8,128)(2,1)S(1)}, u32[]{:S(2)}, u32[]{:S(2)}) collective-permute-start(bf16[1536,128]{1,0:T(8,128)(2,1)S(1)} %constant_dynamic-update-slice_fusion.refs_4_), channel_id=1, source_target_pairs={{0,8},{1,9},{2,10},{3,11},{4,12},{5,13},{6,14},{7,15},{8,0},{9,1},... | collective-permute-start | bytes 1179656 | tf_op jit(solution)/shard_map/ppermute | solution.py:34
  66.0 13.9 %collective-permute-start.17 = (bf16[768,256]{1,0:T(8,128)(2,1)S(1)}, bf16[768,256]{1,0:T(8,128)(2,1)S(1)}, u32[]{:S(2)}, u32[]{:S(2)}) collective-permute-start(bf16[768,256]{1,0:T(8,128)(2,1)S(1)} %collective-permute-done.13.refs_10_), channel_id=1, source_target_pairs={{0,32},{1,33},{2,34},{3,35},{4,36},{5,37},{6,38},{7,39},{8,40},{9,... | collective-permute-start | bytes 1179656 | tf_op jit(solution)/shard_map/ppermute | solution.py:34
  66.0 13.9 %collective-permute-start.18 = (bf16[768,256]{1,0:T(8,128)(2,1)S(1)}, bf16[768,256]{1,0:T(8,128)(2,1)S(1)}, u32[]{:S(2)}, u32[]{:S(2)}) collective-permute-start(bf16[768,256]{1,0:T(8,128)(2,1)S(1)} %collective-permute-done.16.refs_13_), channel_id=1, source_target_pairs={{0,96},{1,97},{2,98},{3,99},{4,100},{5,101},{6,102},{7,103},{8,104... | collective-permute-start | bytes 1179656 | tf_op jit(solution)/shard_map/ppermute | solution.py:34
  104.0 22.1 %all-to-all-start = ((bf16[16,384,128]{2,1,0:T(8,128)(2,1)}), bf16[16,384,128]{2,1,0:T(8,128)(2,1)S(1)}, u32[]{:S(2)}, u32[]{:S(2)}) async-start(bf16[16,384,128]{2,1,0:T(8,128)(2,1)} %shard_map.57), calls=%async_computation | async-start | bytes 3145728 | tf_op jit(solution)/shard_map/all_to_all | solution.py:445
  108.8 23.0 %collective-permute-start.22 = (bf16[256,512]{1,0:T(8,128)(2,1)S(1)}, bf16[256,512]{1,0:T(8,128)(2,1)S(1)}, u32[]{:S(2)}, u32[]{:S(2)}) collective-permute-start(bf16[256,512]{1,0:T(8,128)(2,1)S(1)} %get-tuple-element.49), channel_id=1, source_target_pairs={{0,2},{1,3},{2,0},{3,1},{4,6},{5,7},{6,4},{7,5},{8,10},{9,11},{10,... | collective-permute-start | bytes 786440 | tf_op jit(solution)/shard_map/ppermute | solution.py:34
  127.1 5.2 %collective-permute-start.19 = (bf16[864,128]{1,0:T(8,128)(2,1)S(1)}, bf16[864,128]{1,0:T(8,128)(2,1)S(1)}, u32[]{:S(2)}, u32[]{:S(2)}) collective-permute-start(bf16[864,128]{1,0:T(8,128)(2,1)S(1)} %get-tuple-element.48), channel_id=1, source_target_pairs={{0,16},{1,17},{2,18},{3,19},{4,20},{5,21},{6,22},{7,23},{8,24},{9,... | collective-permute-start | bytes 663560 | tf_op jit(solution)/shard_map/ppermute | solution.py:34
  127.5 8.4 %collective-permute-start.20 = (bf16[864,128]{1,0:T(8,128)(2,1)S(1)}, bf16[864,128]{1,0:T(8,128)(2,1)S(1)}, u32[]{:S(2)}, u32[]{:S(2)}) collective-permute-start(bf16[864,128]{1,0:T(8,128)(2,1)S(1)} %get-tuple-element.48), channel_id=1, source_target_pairs={{0,18},{1,19},{2,16},{3,17},{4,22},{5,23},{6,20},{7,21},{8,26},{9,... | collective-permute-start | bytes 663560 | tf_op jit(solution)/shard_map/ppermute | solution.py:34
  130.6 6.8 %collective-permute-start.21 = (bf16[864,128]{1,0:T(8,128)(2,1)S(1)}, bf16[864,128]{1,0:T(8,128)(2,1)S(1)}, u32[]{:S(2)}, u32[]{:S(2)}) collective-permute-start(bf16[864,128]{1,0:T(8,128)(2,1)S(1)} %get-tuple-element.47.refs_0_), channel_id=1, source_target_pairs={{0,2},{1,3},{2,0},{3,1},{4,6},{5,7},{6,4},{7,5},{8,10},{9,11},{10,... | collective-permute-start | bytes 663560 | tf_op jit(solution)/shard_map/ppermute | solution.py:34
  138.9 10.3 %collective-permute-start.23 = (f32[776,256]{1,0:T(8,128)S(1)}, f32[776,256]{1,0:T(8,128)S(1)}, u32[]{:S(2)}, u32[]{:S(2)}) collective-permute-start(f32[776,256]{1,0:T(8,128)S(1)} %get-tuple-element.51), channel_id=1, source_target_pairs={{0,1},{1,0},{2,3},{3,2},{4,5},{5,4},{6,7},{7,6},{8,9},{9,8},{10,11... | collective-permute-start | bytes 2383880 | tf_op jit(solution)/shard_map/ppermute | solution.py:34

commit v3 on v2

--- a/solution.py
+++ b/solution.py
@@ -66,7 +66,7 @@
 VMEM = pl.BlockSpec(memory_space=pltpu.VMEM)
 
 
-def call(kernel, scalars, arrays, outs, limit, scratch=()):
+def call(kernel, scalars, arrays, outs, limit, scratch=(), aliases={}):
     arrays = [pltpu.with_memory_space_constraint(a, pltpu.VMEM) for a in arrays]
     return pl.pallas_call(
         kernel,
@@ -74,20 +74,23 @@
         out_specs=[VMEM] * len(outs),
         out_shape=[pltpu.VMEM(shape, dtype) for shape, dtype in outs],
         scratch_shapes=list(scratch),
+        input_output_aliases=aliases,
         compiler_params=pltpu.CompilerParams(vmem_limit_bytes=limit << 20),
     )(*scalars, *arrays)
 
 
 PIECE = 128
-
-
-def project_rows(info, blocks, gain_ref, w_ref, put):
+PER = 3
+
+
+def project_rows(info, blocks, gain_ref, w_ref, put, offset=0, rows=ROWS):
     gains = [gain_ref[pl.ds(info[3] ^ j, 1), :] for j in range(4)]
 
     def step(i, carry):
-        for r in range(2):
-            at = pl.ds(pl.multiple_of((2 * i + r) * PIECE, PIECE), PIECE)
-            xs = [p[at, :].astype(F32) for p in blocks]
+        for r in range(PER):
+            here = (PER * i + r) * PIECE + offset
+            at = pl.ds(pl.multiple_of(here, PIECE), PIECE)
+            xs = [p[pl.ds(pl.multiple_of(here - f, PIECE), PIECE), :].astype(F32) for p, f in blocks]
             total = sum(jnp.sum(v, axis=1, keepdims=True) for v in xs)
             mean = total * (1.0 / D)
             xs = [v - mean for v in xs]
@@ -101,7 +104,7 @@
             put(at, silu_of_half(acc * 0.5).astype(BF))
         return carry
 
-    lax.fori_loop(0, ROWS // PIECE // 2, step, 0)
+    lax.fori_loop(0, rows // PIECE // PER, step, 0)
 
 
 def put_into(gate_ref, q_ref, kv_ref):
@@ -122,13 +125,18 @@
         for g in range(4):
             cols = pl.ds(pl.multiple_of(g * 256 + info[1] * HDIM, HDIM), HDIM)
             w_out[j * 256 : (j + 1) * 256, g * HDIM : (g + 1) * HDIM] = w_ref[rows, cols]
-    project_rows(info, blocks, gain_ref, w_out, put_into(gate_ref, q_ref, kv_ref))
+    project_rows(info, [(b, 0) for b in blocks], gain_ref, w_out, put_into(gate_ref, q_ref, kv_ref))
 
 
 def own_kernel(info, *refs):
-    blocks, gain_ref, w_ref, q_other = refs[:4], refs[4], refs[5], refs[6]
-    gate_ref, kv_ref, q_refs, q_own = refs[7], refs[8], refs[9:13], refs[13]
-    project_rows(info, blocks, gain_ref, w_ref, put_into(gate_ref, q_own, kv_ref))
+    here, core, far, far_core = refs[0], refs[1], refs[2:4], refs[4:6]
+    gain_ref, w_ref, q_other = refs[6:9]
+    gate_ref, kv_ref, q_refs, q_own = refs[9], refs[10], refs[11:15], refs[15]
+    put = put_into(gate_ref, q_own, kv_ref)
+    for half in range(2):
+        at = half * SUB
+        blocks = [(here, 0), (core, 0), (far[half], at), (far_core[half], at)]
+        project_rows(info, blocks, gain_ref, w_ref, put, at, SUB)
     for i in range(4):
         source = (q_own, q_other)[i >> 1]
         shift = lax.rem((i ^ (2 * info[1])) - info[0] + 4, 4)
@@ -233,39 +241,23 @@
     )(info)
 
 
-def attend_kernel(info, *refs):
-    lists, q_refs, kv_refs, out = refs[:4], refs[4:8], refs[8:16], refs[16]
-    q, kv, acc, sem = refs[17:]
-    z, yl, x = info[0], info[1], info[2]
-
-    def load_queries(e, ref):
-        copies = []
-        for k in range(4):
-            tile = lax.rem(z - k + 4, 4) * 4 + lax.rem(x - e + 4, 4)
-            copies.append(
-                pltpu.make_async_copy(
-                    ref.at[pl.ds(k * SUB, SUB)],
-                    q.at[pl.ds(pl.multiple_of(tile * SUB, SUB), SUB)],
-                    sem.at[4 * e + k],
-                )
-            )
-        return copies
-
-    def load_keys(k, ref, d, rel):
-        block = lax.rem(z - d + 4, 4) * 2 + (yl ^ rel)
-        to = kv.at[pl.ds(pl.multiple_of(block * ROWS, ROWS), ROWS)]
-        return [pltpu.make_async_copy(ref, to, sem.at[16 + k])]
-
-    queries = [load_queries(e, ref) for e, ref in zip((0, 1, 3, 2), q_refs)]
-    places = zip(kv_refs, (0, 0, 1, 1, 3, 3, 2, 2), (0, 1, 0, 1, 0, 1, 0, 1))
-    keys = [load_keys(k, *place) for k, place in enumerate(places)]
-    early, late = sum(keys[:6] + queries[:3], []), sum(keys[6:] + queries[3:], [])
-    for c in early + late:
-        c.start()
-    acc[...] = jnp.zeros(acc.shape, F32)
-    for c in early:
-        c.wait()
-
+def load_queries(info, e, ref, q, sem):
+    z, x = info[0], info[2]
+    copies = []
+    for k in range(4):
+        tile = lax.rem(z - k + 4, 4) * 4 + lax.rem(x - e + 4, 4)
+        to = q.at[pl.ds(pl.multiple_of(tile * SUB, SUB), SUB)]
+        copies.append(pltpu.make_async_copy(ref.at[pl.ds(k * SUB, SUB)], to, sem.at[4 * e + k]))
+    return copies
+
+
+def load_keys(info, d, rel, ref, kv, sem):
+    block = lax.rem(info[0] - d + 4, 4) * 2 + (info[1] ^ rel)
+    to = kv.at[pl.ds(pl.multiple_of(block * ROWS, ROWS), ROWS)]
+    return [pltpu.make_async_copy(ref, to, sem.at[16 + 2 * d + rel])]
+
+
+def add_tiles(info, full_list, edge_list, q, kv, acc):
     def scores(entry):
         t, n = (entry >> 5) & 15, entry & 31
         q_rows = pl.ds(pl.multiple_of(t * SUB, SUB), SUB)
@@ -278,81 +270,99 @@
     def add(w, q_rows, k_rows):
         acc[q_rows, :] += jnp.dot(w.astype(BF), kv[k_rows, HDIM:], preferred_element_type=F32)
 
-    def run(full_list, edge_list):
-        def full_tiles(i, carry):
-            for u in range(4):
-                w, q_rows, k_rows, _, _ = scores(full_list[4 * i + u])
-                add(w, q_rows, k_rows)
-            return carry
-
-        lax.fori_loop(0, full_list[LIST - 1], full_tiles, 0)
-
-        def edge_tiles(i, carry):
-            for u in range(2):
-                entry = edge_list[2 * i + u]
-                w, q_rows, k_rows, t, n = scores(entry)
-                first = query_first(info, t)
-                col = key_first(info, n) + lax.broadcasted_iota(jnp.int32, (1, KEYS), 1)
-                ends = jnp.full((1, KEYS), FAR, jnp.int32)
-                for j in range(8):
-                    e = info[4 + j]
-                    ends = jnp.minimum(ends, jnp.where(col < e, e, FAR))
-                row = lax.broadcasted_iota(jnp.int32, (SUB, KEYS), 0)
-                skip = (entry >> 9) * FAR
-                allowed = (row >= col + (skip - first)) & (row < ends - first)
-                add(jnp.where(allowed, w, 0.0), q_rows, k_rows)
-            return carry
-
-        lax.fori_loop(0, edge_list[LIST - 1], edge_tiles, 0)
-
-    run(lists[0], lists[1])
-    for c in late:
+    def full_tiles(i, carry):
+        for u in range(4):
+            w, q_rows, k_rows, _, _ = scores(full_list[4 * i + u])
+            add(w, q_rows, k_rows)
+        return carry
+
+    lax.fori_loop(0, full_list[LIST - 1], full_tiles, 0)
+
+    def edge_tiles(i, carry):
+        for u in range(2):
+            entry = edge_list[2 * i + u]
+            w, q_rows, k_rows, t, n = scores(entry)
+            first = query_first(info, t)
+            col = key_first(info, n) + lax.broadcasted_iota(jnp.int32, (1, KEYS), 1)
+            ends = jnp.full((1, KEYS), FAR, jnp.int32)
+            for j in range(8):
+                e = info[4 + j]
+                ends = jnp.minimum(ends, jnp.where(col < e, e, FAR))
+            row = lax.broadcasted_iota(jnp.int32, (SUB, KEYS), 0)
+            skip = (entry >> 9) * FAR
+            allowed = (row >= col + (skip - first)) & (row < ends - first)
+            add(jnp.where(allowed, w, 0.0), q_rows, k_rows)
+        return carry
+
+    lax.fori_loop(0, edge_list[LIST - 1], edge_tiles, 0)
+
+
+def early_kernel(info, full_list, edge_list, *refs):
+    q_refs, kv_refs = refs[:3], refs[3:9]
+    acc, q, kv, sem = refs[9:]
+    copies = sum([load_queries(info, e, ref, q, sem) for e, ref in zip((0, 1, 3), q_refs)], [])
+    for i, ref in enumerate(kv_refs):
+        copies += load_keys(info, (0, 1, 3)[i >> 1], i & 1, ref, kv, sem)
+    for c in copies:
+        c.start()
+    acc[...] = jnp.zeros(acc.shape, F32)
+    for c in copies:
         c.wait()
-    run(lists[2], lists[3])
+    add_tiles(info, full_list, edge_list, q, kv, acc)
+
+
+HELD = (((TILES * SUB, HDIM), F32), ((TILES * SUB, HDIM), BF), ((TILES * SUB, 2 * HDIM), BF))
+
+
+def attend_early(info, lists, queries, keyvals):
+    scratch = [pltpu.SemaphoreType.DMA((24,))]
+    return call(early_kernel, (info, *lists), (*queries, *keyvals), HELD, 4, scratch)
+
+
+def late_kernel(info, full_list, edge_list, acc_in, q_in, kv_in, far_q, near, away, out, acc, q, kv, sem):
+    copies = load_queries(info, 2, far_q, q, sem)
+    copies += load_keys(info, 2, 0, near, kv, sem) + load_keys(info, 2, 1, away, kv, sem)
+    for c in copies:
+        c.start()
+    for c in copies:
+        c.wait()
+    add_tiles(info, full_list, edge_list, q, kv, acc)
     for t in range(TILES):
         out[t] = acc[t * SUB : (t + 1) * SUB, :].astype(BF)
 
 
-def attend(info, lists, queries, keyvals):
-    return call(
-        attend_kernel,
-        (info, *lists),
-        (*queries, *keyvals),
-        [((TILES, SUB, HDIM), BF)],
-        limit=24,
-        scratch=[
-            pltpu.VMEM((TILES * SUB, HDIM), BF),
-            pltpu.VMEM((TILES * SUB, 2 * HDIM), BF),
-            pltpu.VMEM((TILES * SUB, HDIM), F32),
-            pltpu.SemaphoreType.DMA((24,)),
-        ],
-    )[0]
+def attend_late(info, lists, held, far_q, near, away):
+    scratch = [pltpu.SemaphoreType.DMA((24,))]
+    outs = (((TILES, SUB, HDIM), BF), *HELD)
+    aliases = {3: 1, 4: 2, 5: 3}
+    return call(late_kernel, (info, *lists), (*held, far_q, near, away), outs, 4, scratch, aliases)[0]
 
 
 def gate_kernel(info, part_ref, gate_own, gate_other, own_ref, other_ref):
     ones = jnp.ones((8, HDIM), BF)
     add_lanes = lambda v: lax.dot_general(ones, v, (((1,), (1,)), ((), ())), preferred_element_type=F32)
-    for i in range(4):
-        gate_ref, out, half = (gate_own, gate_other)[i >> 1], (own_ref, other_ref)[i >> 1], i & 1
-        a = (i ^ (2 * info[1])) * 4
-        total = part_ref[a].astype(F32)
-        for b in range(1, 4):
-            total = total + part_ref[a + b].astype(F32)
-        at = slice(half * SUB, (half + 1) * SUB)
-        out[at, :] = (total * gate_ref[at, :].astype(F32)).astype(BF)
-        square = total * total
-        top = square.astype(BF)
-        sums = add_lanes(top) + add_lanes((square - top.astype(F32)).astype(BF))
-        for c in range(SUB // HDIM):
-            value = sums[:, c * HDIM : (c + 1) * HDIM]
-            top = value.astype(BF)
-            to = ROWS + TAIL * (3 * half + c)
-            out[to : to + 8, :] = top
-            out[to + 8 : to + 16, :] = (value - top.astype(F32)).astype(BF)
+    for gate_ref, out, rel in ((gate_own, own_ref, 0), (gate_other, other_ref, 1)):
+        high, low = [], []
+        for half in range(2):
+            a = ((2 * rel + half) ^ (2 * info[1])) * 4
+            total = part_ref[a].astype(F32)
+            for b in range(1, 4):
+                total = total + part_ref[a + b].astype(F32)
+            at = slice(half * SUB, (half + 1) * SUB)
+            out[at, :] = (total * gate_ref[at, :].astype(F32)).astype(BF)
+            square = total * total
+            top = square.astype(BF)
+            sums = add_lanes(top) + add_lanes((square - top.astype(F32)).astype(BF))
+            for c in range(SUB // HDIM):
+                value = sums[0:1, c * HDIM : (c + 1) * HDIM]
+                top = value.astype(BF).astype(F32)
+                high.append(top)
+                low.append(value - top)
+        out[ROWS:, :] = jnp.concatenate(high + low + [jnp.zeros((4, HDIM), F32)], axis=0).astype(BF)
 
 
 def gate_rows(info, parts, gate_own, gate_other):
-    outs = [((ROWS + 6 * TAIL, HDIM), BF)] * 2
+    outs = [((ROWS + TAIL, HDIM), BF)] * 2
     return call(gate_kernel, (info,), (parts, gate_own, gate_other), outs, 8)
 
 
@@ -369,8 +379,7 @@
             acc = part if acc is None else acc + part
         out[0:ROWS, :] = acc
     tail = sum(r[ROWS:, :].astype(F32) for r in rows)
-    lines = [tail[TAIL * c : TAIL * c + 1] + tail[TAIL * c + 8 : TAIL * c + 9] for c in range(6)]
-    squares = jnp.concatenate(lines + [jnp.zeros((2, HDIM), F32)], axis=0)
+    squares = jnp.concatenate([tail[0:6] + tail[6:12], jnp.zeros((2, HDIM), F32)], axis=0)
     squares_ref[...] = squares
     theirs_ref[ROWS:, 0:HDIM] = squares
     theirs_ref[ROWS:, HDIM:] = squares
@@ -415,15 +424,17 @@
     o = yh * 2 + lax.axis_index("core").astype(jnp.int32)
     info = jnp.concatenate([jnp.stack([z, yl, x, o]), jnp.cumsum(lengths).astype(jnp.int32)])
 
-    p1, p2, p3 = to_p1(events), to_p2(events), to_p3(events)
+    p1, p2 = to_p1(events), to_p2(events)
     c0 = flip_core(events)
     w_in = w_uvqk.reshape(D, 4 * 256)
     gain = norm_gain.reshape(4, 256)
     p1, w_in, info, gain = lax.optimization_barrier((p1, w_in, info, gain))
-    c1, c2, c3 = flip_core(p1), flip_core(p2), flip_core(p3)
+    far = [to_p2(p1[:SUB]), to_p1(p2[SUB:])]
+    c1, c2 = flip_core(p1), flip_core(p2)
+    far_core = [flip_core(far[0]), flip_core(far[1])]
 
     gate_other, q_other, kv_other, w_in = project_other(info, (p1, c1, p2, c2), gain, w_in)
-    gate_own, kv_own, *pieces = project_own(info, (events, c0, p3, c3), gain, w_in, q_other)
+    gate_own, kv_own, *pieces = project_own(info, (events, c0, *far, *far_core), gain, w_in, q_other)
 
     pieces = [pieces[0]] + [shift_z(pieces[d], d) for d in (1, 2, 3)]
     up_other, down_other = shift_z(kv_other, 1), shift_z(kv_other, -1)
@@ -433,9 +444,10 @@
     queries = [q_mine] + [shift_x(q_mine, e) for e in (1, 3, 2)]
     near, away = shift_z(up_own, 1), shift_z(down_other, -1)
 
-    keyvals = [kv_own, kv_other, up_own, up_other, down_own, down_other, near, away]
+    keyvals = [kv_own, kv_other, up_own, up_other, down_own, down_other]
     lists = plan(info)
-    parts = attend(info, lists, queries, keyvals)
+    held = attend_early(info, lists[:2], queries[:3], keyvals)
+    parts = attend_late(info, lists[2:], held, queries[3], near, away)
 
     w_here = lax.dynamic_slice_in_dim(w_out, yh * 512, 512, 1)
     w_away = lax.dynamic_slice_in_dim(w_out, (1 - yh) * 512, 512, 1)

time: 151 us -> 147 us (0.974)
  waiting for transfers between devices: 63.8 us -> 57.8 us
  starting transfers between devices: 45.1 us -> 48.8 us
    ppermute x24 -> x26, waiting for transfers between devices: 49.7 us -> 42.3 us  [send(): return lax.ppermute(array, AXES, pairs)]
    ppermute x24 -> x26, starting transfers between devices: 41.4 us -> 44.9 us  [send(): return lax.ppermute(array, AXES, pairs)]
    pallas_call x5 -> x6, Pallas kernels: 32.7 us -> 32.7 us  [call(): pl.pallas_call(kernel, in_specs=[SMEM] * len(scalars) + [VMEM] * len(arra...]
  transfers between devices with their start and end apart: 25 -> 27, of which waited for: 12 -> 10; matrix products, arithmetic and copies ran while one was open for 2% -> 2% of each run, Pallas kernels for 5% -> 14%
where the time goes in v3:
time: 147 us
  waiting for transfers between devices  57.8 us (39%)
  starting transfers between devices  48.8 us (33%)
  Pallas kernels  37.5 us (26%)
  local copies, waits for them, and re-layouts  2.36 us (2%)
    ppermute x26, starting transfers between devices, send(): return lax.ppermute(array, AXES, pairs)  44.9 us
    ppermute x26, waiting for transfers between devices, send(): return lax.ppermute(array, AXES, pairs)  42.3 us
    pallas_call x6, Pallas kernels, call(): pl.pallas_call(kernel, in_specs=[SMEM] * len(scalars) + [VMEM] * len(arra...  32.7 us
    all_to_all x1, waiting for transfers between devices, layer(): parts = lax.all_to_all(parts, ('z', 'x'), 0, 0)  15.5 us
    all_to_all x1, starting transfers between devices, layer(): parts = lax.all_to_all(parts, ('z', 'x'), 0, 0)  3.85 us
    pallas_call x1, Pallas kernels, plan(): pl.pallas_call(plan_kernel, in_specs=[SMEM], out_specs=[SMEM] * 4, out_sh...  3.8 us
  transfers between devices with their start and end apart: 27, of which 10 were waited for; matrix products, arithmetic and copies ran while one was open for 2% of the time, Pallas kernels for 14%

profile of v3, /device:TPU:1, one launch (start us, length us, event | category | flops | bytes accessed | tf_op | source)
XLA Modules:
  0.0 147.0 jit_solution(9563379821562577284)
XLA Ops:
  0.0 2.1 %collective-permute-start = (bf16[768,256]{1,0:T(8,128)(2,1)}, bf16[768,256]{1,0:T(8,128)(2,1)S(1)}, u32[]{:S(2)}, u32[]{:S(2)}) collective-permute-start(bf16[768,256]{1,0:T(8,128)(2,1)} %ev_ref.1), channel_id=1, source_target_pairs={{0,16},{1,17},{2,18},{3,19},{4,20},{5,21},{6,22},{7,23},{8,24},{9,... | collective-permute-start | bytes 1179656 | tf_op jit(solution)/shard_map/ppermute | solution.py:34
  2.1 1.9 %collective-permute-start.3 = (bf16[768,256]{1,0:T(8,128)(2,1)}, bf16[768,256]{1,0:T(8,128)(2,1)S(1)}, u32[]{:S(2)}, u32[]{:S(2)}) collective-permute-start(bf16[768,256]{1,0:T(8,128)(2,1)} %ev_ref.1), channel_id=1, source_target_pairs={{0,18},{1,19},{2,16},{3,17},{4,22},{5,23},{6,20},{7,21},{8,26},{9,... | collective-permute-start | bytes 1179656 | tf_op jit(solution)/shard_map/ppermute | solution.py:34
  4.0 2.1 %copy.9 = bf16[128,8,4,256]{3,1,2,0:T(8,128)(2,1)S(1)} copy(bf16[128,8,4,256]{3,2,1,0:T(4,128)(2,1)} %bitcast.9) | data formatting | bytes 4194304
  6.2 0.2 reduce-window.9
  6.4 0.1 concatenate.6.info
  6.5 4.3 %collective-permute-done.refs_0_ = bf16[768,256]{1,0:T(8,128)(2,1)S(1)} collective-permute-done((bf16[768,256]{1,0:T(8,128)(2,1)}, bf16[768,256]{1,0:T(8,128)(2,1)S(1)}, u32[]{:S(2)}, u32[]{:S(2)}) %collective-permute-start) | collective-permute-done | bytes 393248 | tf_op jit(solution)/shard_map/ppermute | solution.py:34
  10.8 1.6 %collective-permute-start.7 = (bf16[768,256]{1,0:T(8,128)(2,1)S(1)}, bf16[768,256]{1,0:T(8,128)(2,1)S(1)}, u32[]{:S(2)}, u32[]{:S(2)}) collective-permute-start(bf16[768,256]{1,0:T(8,128)(2,1)S(1)} %collective-permute-done.refs_0_), channel_id=1, source_target_pairs={{0,1},{1,0},{2,3},{3,2},{4,5},{5,4},{6,7},{7,6},{8,9},{9,8},{10,11... | collective-permute-start | bytes 1179656 | tf_op jit(solution)/shard_map/ppermute | solution.py:34
  12.4 0.9 collective-permute-done.3.refs_2_
  13.3 1.8 %collective-permute-start.8 = (bf16[768,256]{1,0:T(8,128)(2,1)S(1)}, bf16[768,256]{1,0:T(8,128)(2,1)S(1)}, u32[]{:S(2)}, u32[]{:S(2)}) collective-permute-start(bf16[768,256]{1,0:T(8,128)(2,1)S(1)} %collective-permute-done.3.refs_2_), channel_id=1, source_target_pairs={{0,1},{1,0},{2,3},{3,2},{4,5},{5,4},{6,7},{7,6},{8,9},{9,8},{10,11... | collective-permute-start | bytes 1179656 | tf_op jit(solution)/shard_map/ppermute | solution.py:34
  15.1 0.0 collective-permute-start.1
  15.1 2.0 %collective-permute-start.2 = (bf16[384,256]{1,0:T(8,128)(2,1)S(1)}, bf16[384,256]{1,0:T(8,128)(2,1)S(1)}, u32[]{:S(2)}, u32[]{:S(2)}) collective-permute-start(bf16[384,256]{1,0:T(8,128)(2,1)S(1)} %slice.6), channel_id=1, source_target_pairs={{0,18},{1,19},{2,16},{3,17},{4,22},{5,23},{6,20},{7,21},{8,26},{9,... | collective-permute-start | bytes 589832 | tf_op jit(solution)/shard_map/ppermute | solution.py:34
  17.1 0.1 collective-permute-start.4
  17.2 5.2 %collective-permute-done.2.refs_2_ = bf16[384,256]{1,0:T(8,128)(2,1)S(1)} collective-permute-done((bf16[384,256]{1,0:T(8,128)(2,1)S(1)}, bf16[384,256]{1,0:T(8,128)(2,1)S(1)}, u32[]{:S(2)}, u32[]{:S(2)}) %collective-permute-start.2) | collective-permute-done | bytes 196640 | tf_op jit(solution)/shard_map/ppermute | solution.py:34
  22.3 1.4 collective-permute-start.5
  23.7 0.0 collective-permute-done.4.refs_3_
  23.7 0.8 collective-permute-start.6
  24.5 0.0 collective-permute-done.7.refs_1_
  24.5 0.0 collective-permute-done.8.refs_3_
  24.5 2.8 %shard_map.55 = (bf16[768,128]{1,0:T(8,128)(2,1)S(1)}, bf16[768,128]{1,0:T(8,128)(2,1)S(1)}, bf16[768,256]{1,0:T(8,128)(2,1)S(1)}, bf16[1024,512]{1,0:T(8,128)(2,1)S(1)}) custom-call(s32[12]{0:T(128)S(1)} %concatenate.6.info, bf16[768,256]{1,0:T(8,128)(2,1)S(1)} %collective-permute-done.refs_0_, bf16[768,256]{1,0:T(8,128)(2,1)S(1)} %collective-permute-done.7.refs_1_, ...), custom_call_target="tpu_custom_call" | custom-call | tf_op jit(solution)/shard_map/pallas_call | solution.py:71
  27.3 0.0 collective-permute-done.1.refs_1_
  27.3 0.0 collective-permute-done.5.refs_4_
  27.3 0.0 collective-permute-done.6.refs_5_
  27.3 2.5 %shard_map.56 = (bf16[768,128]{1,0:T(8,128)(2,1)S(1)}, bf16[768,256]{1,0:T(8,128)(2,1)S(1)}, bf16[384,128]{1,0:T(8,128)(2,1)S(1)}, bf16[384,128]{1,0:T(8,128)(2,...) custom-call(s32[12]{0:T(128)S(1)} %concatenate.6.info, bf16[768,256]{1,0:T(8,128)(2,1)S(1)} %copy-done, ...), custom_call_target="tpu_custom_call" | custom-call | tf_op jit(solution)/shard_map/pallas_call | solution.py:71
  29.8 1.7 %collective-permute-start.14 = (bf16[768,256]{1,0:T(8,128)(2,1)S(1)}, bf16[768,256]{1,0:T(8,128)(2,1)S(1)}, u32[]{:S(2)}, u32[]{:S(2)}) collective-permute-start(bf16[768,256]{1,0:T(8,128)(2,1)S(1)} %get-tuple-element.47.refs_3_), channel_id=1, source_target_pairs={{0,32},{1,33},{2,34},{3,35},{4,36},{5,37},{6,38},{7,39},{8,40},{9,... | collective-permute-start | bytes 1179656 | tf_op jit(solution)/shard_map/ppermute | solution.py:34
  31.5 2.2 %collective-permute-start.16 = (bf16[768,256]{1,0:T(8,128)(2,1)S(1)}, bf16[768,256]{1,0:T(8,128)(2,1)S(1)}, u32[]{:S(2)}, u32[]{:S(2)}) collective-permute-start(bf16[768,256]{1,0:T(8,128)(2,1)S(1)} %get-tuple-element.47.refs_3_), channel_id=1, source_target_pairs={{0,96},{1,97},{2,98},{3,99},{4,100},{5,101},{6,102},{7,103},{8,104... | collective-permute-start | bytes 1179656 | tf_op jit(solution)/shard_map/ppermute | solution.py:34
  33.7 1.4 collective-permute-start.17
  35.1 0.1 collective-permute-start.15
  35.2 0.0 collective-permute-start.9
  35.2 18.4 %collective-permute-done.9 = bf16[384,128]{1,0:T(8,128)(2,1)S(1)} collective-permute-done((bf16[384,128]{1,0:T(8,128)(2,1)S(1)}, bf16[384,128]{1,0:T(8,128)(2,1)S(1)}, u32[]{:S(2)}, u32[]{:S(2)}) %collective-permute-start.9) | collective-permute-done | bytes 98336 | tf_op jit(solution)/shard_map/ppermute | solution.py:34
  53.7 1.0 collective-permute-start.10
  54.7 4.2 %collective-permute-done.10 = bf16[384,128]{1,0:T(8,128)(2,1)S(1)} collective-permute-done((bf16[384,128]{1,0:T(8,128)(2,1)S(1)}, bf16[384,128]{1,0:T(8,128)(2,1)S(1)}, u32[]{:S(2)}, u32[]{:S(2)}) %collective-permute-start.10) | collective-permute-done | bytes 98336 | tf_op jit(solution)/shard_map/ppermute | solution.py:34
  58.9 0.9 collective-permute-start.11
  59.8 2.6 %collective-permute-done.11 = bf16[384,128]{1,0:T(8,128)(2,1)S(1)} collective-permute-done((bf16[384,128]{1,0:T(8,128)(2,1)S(1)}, bf16[384,128]{1,0:T(8,128)(2,1)S(1)}, u32[]{:S(2)}, u32[]{:S(2)}) %collective-permute-start.11) | collective-permute-done | bytes 98336 | tf_op jit(solution)/shard_map/ppermute | solution.py:34
  62.4 1.3 collective-permute-start.12
  63.7 0.0 collective-permute-done.14.refs_5_
  63.7 1.5 collective-permute-start.13
  65.2 0.0 collective-permute-done.16.refs_7_
  65.2 1.5 %collective-permute-start.18 = (bf16[1536,128]{1,0:T(8,128)(2,1)S(1)}, bf16[1536,128]{1,0:T(8,128)(2,1)S(1)}, u32[]{:S(2)}, u32[]{:S(2)}) collective-permute-start(bf16[1536,128]{1,0:T(8,128)(2,1)S(1)} %constant_dynamic-update-slice_fusion.refs_0_), channel_id=1, source_target_pairs={{0,8},{1,9},{2,10},{3,11},{4,12},{5,13},{6,14},{7,15},{8,0},{9,1},... | collective-permute-start | bytes 1179656 | tf_op jit(solution)/shard_map/ppermute | solution.py:34
  66.7 0.0 collective-permute-done.17.refs_8_
  66.7 0.0 collective-permute-start.19
  66.7 0.0 collective-permute-done.15.refs_6_
  66.7 2.7 %collective-permute-start.20 = (bf16[768,256]{1,0:T(8,128)(2,1)S(1)}, bf16[768,256]{1,0:T(8,128)(2,1)S(1)}, u32[]{:S(2)}, u32[]{:S(2)}) collective-permute-start(bf16[768,256]{1,0:T(8,128)(2,1)S(1)} %collective-permute-done.17.refs_8_), channel_id=1, source_target_pairs={{0,96},{1,97},{2,98},{3,99},{4,100},{5,101},{6,102},{7,103},{8,104... | collective-permute-start | bytes 1179656 | tf_op jit(solution)/shard_map/ppermute | solution.py:34
  69.4 3.8 %plan.1 = (s32[416]{0:T(512)S(1)}, s32[416]{0:T(512)S(1)}, s32[416]{0:T(512)S(1)}, s32[416]{0:T(512)S(1)}) custom-call(s32[12]{0:T(128)S(1)} %concatenate.6.info), custom_call_target="tpu_custom_call" | custom-call | tf_op jit(solution)/shard_map/plan/pallas_call | solution.py:234
  73.2 0.0 collective-permute-done.12.refs_1_
  73.2 0.0 collective-permute-done.13.refs_2_
  73.2 12.2 %shard_map.57 = (f32[6144,128]{1,0:T(8,128)S(1)}, bf16[6144,128]{1,0:T(8,128)(2,1)S(1)}, bf16[6144,256]{1,0:T(8,128)(2,1)S(1)}) custom-call(s32[12]{0:T(128)S(1)} %concatenate.6.info, s32[416]{0:T(512)S(1)} %get-tuple-element.36.full_list, s32[416]{0:T(512)S(1)} %get-tuple-element.37.edge_list, ...), custom_call_target="tpu_custom_call" | custom-call | tf_op jit(solution)/shard_map/pallas_call | solution.py:71
  85.5 0.0 collective-permute-done.18.far_q
  85.5 0.0 collective-permute-done.19.near
  85.5 12.7 %shard_map.58 = (bf16[16,384,128]{2,1,0:T(8,128)(2,1)}, f32[6144,128]{1,0:T(8,128)S(1)}, bf16[6144,128]{1,0:T(8,128)(2,1)S(1)}, bf16[6144,256]{1,0:T(8,128)(2,1)S(1)}) custom-call(s32[12]{0:T(128)S(1)} %concatenate.6.info, s32[416]{0:T(512)S(1)} %get-tuple-element.34.full_list, ...), custom_call_target="tpu_custom_call", output_to_operand_aliasing={{1}: (3, {}), {2}: (4, {}), {3}: (5, {})} | custom-call | tf_op jit(solution)/shard_map/pallas_call | solution.py:71
  98.2 0.0 copy-start.1
  98.2 3.9 %all-to-all-start = ((bf16[16,384,128]{2,1,0:T(8,128)(2,1)}), bf16[16,384,128]{2,1,0:T(8,128)(2,1)S(1)}, u32[]{:S(2)}, u32[]{:S(2)}) async-start(bf16[16,384,128]{2,1,0:T(8,128)(2,1)} %get-tuple-element.52), calls=%async_computation | async-start | bytes 3145728 | tf_op jit(solution)/shard_map/all_to_all | solution.py:457
  102.1 0.6 collective-permute-start.24
  102.7 15.5 %all-to-all-done.part_ref = bf16[16,384,128]{2,1,0:T(8,128)(2,1)S(1)} async-done(((bf16[16,384,128]{2,1,0:T(8,128)(2,1)}), bf16[16,384,128]{2,1,0:T(8,128)(2,1)S(1)}, u32[]{:S(2)}, u32[]{:S(2)}) %all-to-all-start) | async-done | bytes 1572896 | tf_op jit(solution)/shard_map/all_to_all | solution.py:457
  118.2 1.0 shard_map.59
  119.2 0.1 collective-permute-start.21
  119.3 0.8 collective-permute-start.22
  120.1 2.5 %collective-permute-start.23 = (bf16[784,128]{1,0:T(8,128)(2,1)S(1)}, bf16[784,128]{1,0:T(8,128)(2,1)S(1)}, u32[]{:S(2)}, u32[]{:S(2)}) collective-permute-start(bf16[784,128]{1,0:T(8,128)(2,1)S(1)} %get-tuple-element.55.refs_0_), channel_id=1, source_target_pairs={{0,2},{1,3},{2,0},{3,1},{4,6},{5,7},{6,4},{7,5},{8,10},{9,11},{10,... | collective-permute-start | bytes 602120 | tf_op jit(solution)/shard_map/ppermute | solution.py:34
  122.6 0.0 collective-permute-done.24.refs_5_
  122.6 1.6 %collective-permute-done.21.refs_1_ = bf16[784,128]{1,0:T(8,128)(2,1)S(1)} collective-permute-done((bf16[784,128]{1,0:T(8,128)(2,1)S(1)}, bf16[784,128]{1,0:T(8,128)(2,1)S(1)}, u32[]{:S(2)}, u32[]{:S(2)}) %collective-permute-start.21) | collective-permute-done | bytes 200736 | tf_op jit(solution)/shard_map/ppermute | solution.py:34
  124.2 3.2 %collective-permute-done.22.refs_2_ = bf16[784,128]{1,0:T(8,128)(2,1)S(1)} collective-permute-done((bf16[784,128]{1,0:T(8,128)(2,1)S(1)}, bf16[784,128]{1,0:T(8,128)(2,1)S(1)}, u32[]{:S(2)}, u32[]{:S(2)}) %collective-permute-start.22) | collective-permute-done | bytes 200736 | tf_op jit(solution)/shard_map/ppermute | solution.py:34
  127.3 1.5 %shard_map.60 = (f32[768,256]{1,0:T(8,128)S(1)}, f32[776,256]{1,0:T(8,128)S(1)}, f32[8,128]{1,0:T(8,128)S(1)}) custom-call(s32[12]{0:T(128)S(1)} %concatenate.6.info, bf16[784,128]{1,0:T(8,128)(2,1)S(1)} %get-tuple-element.55.refs_0_, bf16[784,128]{1,0:T(8,128)(2,1)S(1)} %collective-permute-done.21.refs_1_, ...), custom_call_target="tpu_custom_call" | custom-call | tf_op jit(solution)/shard_map/pallas_call | solution.py:71
  128.8 15.1 %collective-permute-start.25 = (f32[776,256]{1,0:T(8,128)S(1)}, f32[776,256]{1,0:T(8,128)S(1)}, u32[]{:S(2)}, u32[]{:S(2)}) collective-permute-start(f32[776,256]{1,0:T(8,128)S(1)} %get-tuple-element.59), channel_id=1, source_target_pairs={{0,1},{1,0},{2,3},{3,2},{4,5},{5,4},{6,7},{7,6},{8,9},{9,8},{10,11... | collective-permute-start | bytes 2383880 | tf_op jit(solution)/shard_map/ppermute | solution.py:34
  144.0 1.9 %collective-permute-done.25.got_ref = f32[776,256]{1,0:T(8,128)S(1)} collective-permute-done((f32[776,256]{1,0:T(8,128)S(1)}, f32[776,256]{1,0:T(8,128)S(1)}, u32[]{:S(2)}, u32[]{:S(2)}) %collective-permute-start.25) | collective-permute-done | bytes 794656 | tf_op jit(solution)/shard_map/ppermute | solution.py:34
  145.9 0.9 finish.1
  (17 shorter events, 0.1 us)
Async XLA Ops:
  0.0 10.8 %collective-permute-start = (bf16[768,256]{1,0:T(8,128)(2,1)}, bf16[768,256]{1,0:T(8,128)(2,1)S(1)}, u32[]{:S(2)}, u32[]{:S(2)}) collective-permute-start(bf16[768,256]{1,0:T(8,128)(2,1)} %ev_ref.1), channel_id=1, source_target_pairs={{0,16},{1,17},{2,18},{3,19},{4,20},{5,21},{6,22},{7,23},{8,24},{9,... | collective-permute-start | bytes 1179656 | tf_op jit(solution)/shard_map/ppermute | solution.py:34
  2.1 11.1 %collective-permute-start.3 = (bf16[768,256]{1,0:T(8,128)(2,1)}, bf16[768,256]{1,0:T(8,128)(2,1)S(1)}, u32[]{:S(2)}, u32[]{:S(2)}) collective-permute-start(bf16[768,256]{1,0:T(8,128)(2,1)} %ev_ref.1), channel_id=1, source_target_pairs={{0,18},{1,19},{2,16},{3,17},{4,22},{5,23},{6,20},{7,21},{8,26},{9,... | collective-permute-start | bytes 1179656 | tf_op jit(solution)/shard_map/ppermute | solution.py:34
  4.0 2.1 %copy-start.2 = (f32[1024]{0:T(1024)S(1)}, f32[1024]{0:T(1024)}, u32[]{:S(2)}) copy-start(f32[1024]{0:T(1024)} %param.6) | copy-start | bytes 12292
  4.0 2.2 %copy-start.3 = (s32[8]{0:T(128)S(1)}, s32[8]{0:T(128)}, u32[]{:S(2)}) copy-start(s32[8]{0:T(128)} %param.9) | copy-start | bytes 100
  4.0 11.0 %copy-start = (bf16[768,256]{1,0:T(8,128)(2,1)S(1)}, bf16[768,256]{1,0:T(8,128)(2,1)}, u32[]{:S(2)}) copy-start(bf16[768,256]{1,0:T(8,128)(2,1)} %ev_ref.1) | copy-start | bytes 1179652
  10.8 13.7 %collective-permute-start.7 = (bf16[768,256]{1,0:T(8,128)(2,1)S(1)}, bf16[768,256]{1,0:T(8,128)(2,1)S(1)}, u32[]{:S(2)}, u32[]{:S(2)}) collective-permute-start(bf16[768,256]{1,0:T(8,128)(2,1)S(1)} %collective-permute-done.refs_0_), channel_id=1, source_target_pairs={{0,1},{1,0},{2,3},{3,2},{4,5},{5,4},{6,7},{7,6},{8,9},{9,8},{10,11... | collective-permute-start | bytes 1179656 | tf_op jit(solution)/shard_map/ppermute | solution.py:34
  13.3 11.2 %collective-permute-start.8 = (bf16[768,256]{1,0:T(8,128)(2,1)S(1)}, bf16[768,256]{1,0:T(8,128)(2,1)S(1)}, u32[]{:S(2)}, u32[]{:S(2)}) collective-permute-start(bf16[768,256]{1,0:T(8,128)(2,1)S(1)} %collective-permute-done.3.refs_2_), channel_id=1, source_target_pairs={{0,1},{1,0},{2,3},{3,2},{4,5},{5,4},{6,7},{7,6},{8,9},{9,8},{10,11... | collective-permute-start | bytes 1179656 | tf_op jit(solution)/shard_map/ppermute | solution.py:34
  15.1 12.2 %collective-permute-start.1 = (bf16[768,256]{1,0:T(8,128)(2,1)S(1)}, bf16[768,256]{1,0:T(8,128)(2,1)S(1)}, u32[]{:S(2)}, u32[]{:S(2)}) collective-permute-start(bf16[768,256]{1,0:T(8,128)(2,1)S(1)} %copy-done), channel_id=1, source_target_pairs={{0,1},{1,0},{2,3},{3,2},{4,5},{5,4},{6,7},{7,6},{8,9},{9,8},{10,11... | collective-permute-start | bytes 1179656 | tf_op jit(solution)/shard_map/ppermute | solution.py:34
  15.1 7.2 %collective-permute-start.2 = (bf16[384,256]{1,0:T(8,128)(2,1)S(1)}, bf16[384,256]{1,0:T(8,128)(2,1)S(1)}, u32[]{:S(2)}, u32[]{:S(2)}) collective-permute-start(bf16[384,256]{1,0:T(8,128)(2,1)S(1)} %slice.6), channel_id=1, source_target_pairs={{0,18},{1,19},{2,16},{3,17},{4,22},{5,23},{6,20},{7,21},{8,26},{9,... | collective-permute-start | bytes 589832 | tf_op jit(solution)/shard_map/ppermute | solution.py:34
  17.1 6.6 %collective-permute-start.4 = (bf16[384,256]{1,0:T(8,128)(2,1)S(1)}, bf16[384,256]{1,0:T(8,128)(2,1)S(1)}, u32[]{:S(2)}, u32[]{:S(2)}) collective-permute-start(bf16[384,256]{1,0:T(8,128)(2,1)S(1)} %slice.8), channel_id=1, source_target_pairs={{0,16},{1,17},{2,18},{3,19},{4,20},{5,21},{6,22},{7,23},{8,24},{9,... | collective-permute-start | bytes 589832 | tf_op jit(solution)/shard_map/ppermute | solution.py:34
  22.3 5.0 %collective-permute-start.5 = (bf16[384,256]{1,0:T(8,128)(2,1)S(1)}, bf16[384,256]{1,0:T(8,128)(2,1)S(1)}, u32[]{:S(2)}, u32[]{:S(2)}) collective-permute-start(bf16[384,256]{1,0:T(8,128)(2,1)S(1)} %collective-permute-done.2.refs_2_), channel_id=1, source_target_pairs={{0,1},{1,0},{2,3},{3,2},{4,5},{5,4},{6,7},{7,6},{8,9},{9,8},{10,11... | collective-permute-start | bytes 589832 | tf_op jit(solution)/shard_map/ppermute | solution.py:34
  23.7 3.6 %collective-permute-start.6 = (bf16[384,256]{1,0:T(8,128)(2,1)S(1)}, bf16[384,256]{1,0:T(8,128)(2,1)S(1)}, u32[]{:S(2)}, u32[]{:S(2)}) collective-permute-start(bf16[384,256]{1,0:T(8,128)(2,1)S(1)} %collective-permute-done.4.refs_3_), channel_id=1, source_target_pairs={{0,1},{1,0},{2,3},{3,2},{4,5},{5,4},{6,7},{7,6},{8,9},{9,8},{10,11... | collective-permute-start | bytes 589832 | tf_op jit(solution)/shard_map/ppermute | solution.py:34
  29.8 33.9 %collective-permute-start.14 = (bf16[768,256]{1,0:T(8,128)(2,1)S(1)}, bf16[768,256]{1,0:T(8,128)(2,1)S(1)}, u32[]{:S(2)}, u32[]{:S(2)}) collective-permute-start(bf16[768,256]{1,0:T(8,128)(2,1)S(1)} %get-tuple-element.47.refs_3_), channel_id=1, source_target_pairs={{0,32},{1,33},{2,34},{3,35},{4,36},{5,37},{6,38},{7,39},{8,40},{9,... | collective-permute-start | bytes 1179656 | tf_op jit(solution)/shard_map/ppermute | solution.py:34
  31.5 33.6 %collective-permute-start.16 = (bf16[768,256]{1,0:T(8,128)(2,1)S(1)}, bf16[768,256]{1,0:T(8,128)(2,1)S(1)}, u32[]{:S(2)}, u32[]{:S(2)}) collective-permute-start(bf16[768,256]{1,0:T(8,128)(2,1)S(1)} %get-tuple-element.47.refs_3_), channel_id=1, source_target_pairs={{0,96},{1,97},{2,98},{3,99},{4,100},{5,101},{6,102},{7,103},{8,104... | collective-permute-start | bytes 1179656 | tf_op jit(solution)/shard_map/ppermute | solution.py:34
  33.7 33.0 %collective-permute-start.17 = (bf16[768,256]{1,0:T(8,128)(2,1)S(1)}, bf16[768,256]{1,0:T(8,128)(2,1)S(1)}, u32[]{:S(2)}, u32[]{:S(2)}) collective-permute-start(bf16[768,256]{1,0:T(8,128)(2,1)S(1)} %get-tuple-element.48.refs_4_), channel_id=1, source_target_pairs={{0,96},{1,97},{2,98},{3,99},{4,100},{5,101},{6,102},{7,103},{8,104... | collective-permute-start | bytes 1179656 | tf_op jit(solution)/shard_map/ppermute | solution.py:34
  35.1 31.6 %collective-permute-start.15 = (bf16[768,256]{1,0:T(8,128)(2,1)S(1)}, bf16[768,256]{1,0:T(8,128)(2,1)S(1)}, u32[]{:S(2)}, u32[]{:S(2)}) collective-permute-start(bf16[768,256]{1,0:T(8,128)(2,1)S(1)} %get-tuple-element.48.refs_4_), channel_id=1, source_target_pairs={{0,32},{1,33},{2,34},{3,35},{4,36},{5,37},{6,38},{7,39},{8,40},{9,... | collective-permute-start | bytes 1179656 | tf_op jit(solution)/shard_map/ppermute | solution.py:34
  35.2 18.5 %collective-permute-start.9 = (bf16[384,128]{1,0:T(8,128)(2,1)S(1)}, bf16[384,128]{1,0:T(8,128)(2,1)S(1)}, u32[]{:S(2)}, u32[]{:S(2)}) collective-permute-start(bf16[384,128]{1,0:T(8,128)(2,1)S(1)} %get-tuple-element.44), channel_id=1, source_target_pairs={{0,32},{1,33},{2,34},{3,35},{4,36},{5,37},{6,38},{7,39},{8,40},{9,... | collective-permute-start | bytes 294920 | tf_op jit(solution)/shard_map/ppermute | solution.py:34
  53.7 5.3 %collective-permute-start.10 = (bf16[384,128]{1,0:T(8,128)(2,1)S(1)}, bf16[384,128]{1,0:T(8,128)(2,1)S(1)}, u32[]{:S(2)}, u32[]{:S(2)}) collective-permute-start(bf16[384,128]{1,0:T(8,128)(2,1)S(1)} %get-tuple-element.45), channel_id=1, source_target_pairs={{0,64},{1,65},{2,66},{3,67},{4,68},{5,69},{6,70},{7,71},{8,72},{9,... | collective-permute-start | bytes 294920 | tf_op jit(solution)/shard_map/ppermute | solution.py:34
  58.9 3.5 %collective-permute-start.11 = (bf16[384,128]{1,0:T(8,128)(2,1)S(1)}, bf16[384,128]{1,0:T(8,128)(2,1)S(1)}, u32[]{:S(2)}, u32[]{:S(2)}) collective-permute-start(bf16[384,128]{1,0:T(8,128)(2,1)S(1)} %get-tuple-element.46), channel_id=1, source_target_pairs={{0,96},{1,97},{2,98},{3,99},{4,100},{5,101},{6,102},{7,103},{8,104... | collective-permute-start | bytes 294920 | tf_op jit(solution)/shard_map/ppermute | solution.py:34
  62.4 10.8 %collective-permute-start.12 = (bf16[1536,128]{1,0:T(8,128)(2,1)S(1)}, bf16[1536,128]{1,0:T(8,128)(2,1)S(1)}, u32[]{:S(2)}, u32[]{:S(2)}) collective-permute-start(bf16[1536,128]{1,0:T(8,128)(2,1)S(1)} %constant_dynamic-update-slice_fusion.refs_0_), channel_id=1, source_target_pairs={{0,4},{1,5},{2,6},{3,7},{4,8},{5,9},{6,10},{7,11},{8,12},{9,13},{1... | collective-permute-start | bytes 1179656 | tf_op jit(solution)/shard_map/ppermute | solution.py:34
  63.7 9.5 %collective-permute-start.13 = (bf16[1536,128]{1,0:T(8,128)(2,1)S(1)}, bf16[1536,128]{1,0:T(8,128)(2,1)S(1)}, u32[]{:S(2)}, u32[]{:S(2)}) collective-permute-start(bf16[1536,128]{1,0:T(8,128)(2,1)S(1)} %constant_dynamic-update-slice_fusion.refs_0_), channel_id=1, source_target_pairs={{0,12},{1,13},{2,14},{3,15},{4,0},{5,1},{6,2},{7,3},{8,4},{9,5},{1... | collective-permute-start | bytes 1179656 | tf_op jit(solution)/shard_map/ppermute | solution.py:34
  65.2 20.3 %collective-permute-start.18 = (bf16[1536,128]{1,0:T(8,128)(2,1)S(1)}, bf16[1536,128]{1,0:T(8,128)(2,1)S(1)}, u32[]{:S(2)}, u32[]{:S(2)}) collective-permute-start(bf16[1536,128]{1,0:T(8,128)(2,1)S(1)} %constant_dynamic-update-slice_fusion.refs_0_), channel_id=1, source_target_pairs={{0,8},{1,9},{2,10},{3,11},{4,12},{5,13},{6,14},{7,15},{8,0},{9,1},... | collective-permute-start | bytes 1179656 | tf_op jit(solution)/shard_map/ppermute | solution.py:34
  66.7 18.8 %collective-permute-start.19 = (bf16[768,256]{1,0:T(8,128)(2,1)S(1)}, bf16[768,256]{1,0:T(8,128)(2,1)S(1)}, u32[]{:S(2)}, u32[]{:S(2)}) collective-permute-start(bf16[768,256]{1,0:T(8,128)(2,1)S(1)} %collective-permute-done.14.refs_5_), channel_id=1, source_target_pairs={{0,32},{1,33},{2,34},{3,35},{4,36},{5,37},{6,38},{7,39},{8,40},{9,... | collective-permute-start | bytes 1179656 | tf_op jit(solution)/shard_map/ppermute | solution.py:34
  66.7 18.8 %collective-permute-start.20 = (bf16[768,256]{1,0:T(8,128)(2,1)S(1)}, bf16[768,256]{1,0:T(8,128)(2,1)S(1)}, u32[]{:S(2)}, u32[]{:S(2)}) collective-permute-start(bf16[768,256]{1,0:T(8,128)(2,1)S(1)} %collective-permute-done.17.refs_8_), channel_id=1, source_target_pairs={{0,96},{1,97},{2,98},{3,99},{4,100},{5,101},{6,102},{7,103},{8,104... | collective-permute-start | bytes 1179656 | tf_op jit(solution)/shard_map/ppermute | solution.py:34
  98.2 3.9 %copy-start.1 = (bf16[256,1024]{1,0:T(8,128)(2,1)S(1)}, bf16[256,1024]{1,0:T(8,128)(2,1)}, u32[]{:S(2)}) copy-start(bf16[256,1024]{1,0:T(8,128)(2,1)} %param.8) | copy-start | bytes 1572868
  98.2 20.0 %all-to-all-start = ((bf16[16,384,128]{2,1,0:T(8,128)(2,1)}), bf16[16,384,128]{2,1,0:T(8,128)(2,1)S(1)}, u32[]{:S(2)}, u32[]{:S(2)}) async-start(bf16[16,384,128]{2,1,0:T(8,128)(2,1)} %get-tuple-element.52), calls=%async_computation | async-start | bytes 3145728 | tf_op jit(solution)/shard_map/all_to_all | solution.py:457
  102.1 20.5 %collective-permute-start.24 = (bf16[256,512]{1,0:T(8,128)(2,1)S(1)}, bf16[256,512]{1,0:T(8,128)(2,1)S(1)}, u32[]{:S(2)}, u32[]{:S(2)}) collective-permute-start(bf16[256,512]{1,0:T(8,128)(2,1)S(1)} %get-tuple-element.57), channel_id=1, source_target_pairs={{0,2},{1,3},{2,0},{3,1},{4,6},{5,7},{6,4},{7,5},{8,10},{9,11},{10,... | collective-permute-start | bytes 786440 | tf_op jit(solution)/shard_map/ppermute | solution.py:34
  119.2 4.9 %collective-permute-start.21 = (bf16[784,128]{1,0:T(8,128)(2,1)S(1)}, bf16[784,128]{1,0:T(8,128)(2,1)S(1)}, u32[]{:S(2)}, u32[]{:S(2)}) collective-permute-start(bf16[784,128]{1,0:T(8,128)(2,1)S(1)} %get-tuple-element.56), channel_id=1, source_target_pairs={{0,16},{1,17},{2,18},{3,19},{4,20},{5,21},{6,22},{7,23},{8,24},{9,... | collective-permute-start | bytes 602120 | tf_op jit(solution)/shard_map/ppermute | solution.py:34
  119.3 8.0 %collective-permute-start.22 = (bf16[784,128]{1,0:T(8,128)(2,1)S(1)}, bf16[784,128]{1,0:T(8,128)(2,1)S(1)}, u32[]{:S(2)}, u32[]{:S(2)}) collective-permute-start(bf16[784,128]{1,0:T(8,128)(2,1)S(1)} %get-tuple-element.56), channel_id=1, source_target_pairs={{0,18},{1,19},{2,16},{3,17},{4,22},{5,23},{6,20},{7,21},{8,26},{9,... | collective-permute-start | bytes 602120 | tf_op jit(solution)/shard_map/ppermute | solution.py:34
  120.1 7.2 %collective-permute-start.23 = (bf16[784,128]{1,0:T(8,128)(2,1)S(1)}, bf16[784,128]{1,0:T(8,128)(2,1)S(1)}, u32[]{:S(2)}, u32[]{:S(2)}) collective-permute-start(bf16[784,128]{1,0:T(8,128)(2,1)S(1)} %get-tuple-element.55.refs_0_), channel_id=1, source_target_pairs={{0,2},{1,3},{2,0},{3,1},{4,6},{5,7},{6,4},{7,5},{8,10},{9,11},{10,... | collective-permute-start | bytes 602120 | tf_op jit(solution)/shard_map/ppermute | solution.py:34
  128.8 17.1 %collective-permute-start.25 = (f32[776,256]{1,0:T(8,128)S(1)}, f32[776,256]{1,0:T(8,128)S(1)}, u32[]{:S(2)}, u32[]{:S(2)}) collective-permute-start(f32[776,256]{1,0:T(8,128)S(1)} %get-tuple-element.59), channel_id=1, source_target_pairs={{0,1},{1,0},{2,3},{3,2},{4,5},{5,4},{6,7},{7,6},{8,9},{9,8},{10,11... | collective-permute-start | bytes 2383880 | tf_op jit(solution)/shard_map/ppermute | solution.py:34

commit v4 on v3

--- a/solution.py
+++ b/solution.py
@@ -241,20 +241,15 @@
     )(info)
 
 
-def load_queries(info, e, ref, q, sem):
-    z, x = info[0], info[2]
-    copies = []
+def place_queries(info, e, ref, q):
     for k in range(4):
-        tile = lax.rem(z - k + 4, 4) * 4 + lax.rem(x - e + 4, 4)
-        to = q.at[pl.ds(pl.multiple_of(tile * SUB, SUB), SUB)]
-        copies.append(pltpu.make_async_copy(ref.at[pl.ds(k * SUB, SUB)], to, sem.at[4 * e + k]))
-    return copies
-
-
-def load_keys(info, d, rel, ref, kv, sem):
+        tile = lax.rem(info[0] - k + 4, 4) * 4 + lax.rem(info[2] - e + 4, 4)
+        q[pl.ds(pl.multiple_of(tile * SUB, SUB), SUB), :] = ref[k * SUB : (k + 1) * SUB, :]
+
+
+def place_keys(info, d, rel, ref, kv):
     block = lax.rem(info[0] - d + 4, 4) * 2 + (info[1] ^ rel)
-    to = kv.at[pl.ds(pl.multiple_of(block * ROWS, ROWS), ROWS)]
-    return [pltpu.make_async_copy(ref, to, sem.at[16 + 2 * d + rel])]
+    kv[pl.ds(pl.multiple_of(block * ROWS, ROWS), ROWS), :] = ref[...]
 
 
 def add_tiles(info, full_list, edge_list, q, kv, acc):
@@ -299,15 +294,12 @@
 
 def early_kernel(info, full_list, edge_list, *refs):
     q_refs, kv_refs = refs[:3], refs[3:9]
-    acc, q, kv, sem = refs[9:]
-    copies = sum([load_queries(info, e, ref, q, sem) for e, ref in zip((0, 1, 3), q_refs)], [])
+    acc, q, kv = refs[9:]
+    for e, ref in zip((0, 1, 3), q_refs):
+        place_queries(info, e, ref, q)
     for i, ref in enumerate(kv_refs):
-        copies += load_keys(info, (0, 1, 3)[i >> 1], i & 1, ref, kv, sem)
-    for c in copies:
-        c.start()
+        place_keys(info, (0, 1, 3)[i >> 1], i & 1, ref, kv)
     acc[...] = jnp.zeros(acc.shape, F32)
-    for c in copies:
-        c.wait()
     add_tiles(info, full_list, edge_list, q, kv, acc)
 
 
@@ -315,27 +307,22 @@
 
 
 def attend_early(info, lists, queries, keyvals):
-    scratch = [pltpu.SemaphoreType.DMA((24,))]
-    return call(early_kernel, (info, *lists), (*queries, *keyvals), HELD, 4, scratch)
-
-
-def late_kernel(info, full_list, edge_list, acc_in, q_in, kv_in, far_q, near, away, out, acc, q, kv, sem):
-    copies = load_queries(info, 2, far_q, q, sem)
-    copies += load_keys(info, 2, 0, near, kv, sem) + load_keys(info, 2, 1, away, kv, sem)
-    for c in copies:
-        c.start()
-    for c in copies:
-        c.wait()
+    return call(early_kernel, (info, *lists), (*queries, *keyvals), HELD, 4)
+
+
+def late_kernel(info, full_list, edge_list, acc_in, q_in, kv_in, far_q, near, away, out, acc, q, kv):
+    place_queries(info, 2, far_q, q)
+    place_keys(info, 2, 0, near, kv)
+    place_keys(info, 2, 1, away, kv)
     add_tiles(info, full_list, edge_list, q, kv, acc)
     for t in range(TILES):
         out[t] = acc[t * SUB : (t + 1) * SUB, :].astype(BF)
 
 
 def attend_late(info, lists, held, far_q, near, away):
-    scratch = [pltpu.SemaphoreType.DMA((24,))]
     outs = (((TILES, SUB, HDIM), BF), *HELD)
-    aliases = {3: 1, 4: 2, 5: 3}
-    return call(late_kernel, (info, *lists), (*held, far_q, near, away), outs, 4, scratch, aliases)[0]
+    arrays = (*held, far_q, near, away)
+    return call(late_kernel, (info, *lists), arrays, outs, 4, aliases={3: 1, 4: 2, 5: 3})[0]
 
 
 def gate_kernel(info, part_ref, gate_own, gate_other, own_ref, other_ref):
@@ -377,27 +364,30 @@
             at = pl.ds(pl.multiple_of((info[1] ^ flip) * HDIM, HDIM), HDIM)
             part = jnp.dot(r[0:ROWS, :], w[at, cols], preferred_element_type=F32)
             acc = part if acc is None else acc + part
-        out[0:ROWS, :] = acc
+        out[0:ROWS, :] = acc.astype(out.dtype)
     tail = sum(r[ROWS:, :].astype(F32) for r in rows)
     squares = jnp.concatenate([tail[0:6] + tail[6:12], jnp.zeros((2, HDIM), F32)], axis=0)
     squares_ref[...] = squares
-    theirs_ref[ROWS:, 0:HDIM] = squares
-    theirs_ref[ROWS:, HDIM:] = squares
+    top = squares.astype(BF)
+    theirs_ref[ROWS : ROWS + 8, 0:HDIM] = top
+    theirs_ref[ROWS : ROWS + 8, HDIM:] = (squares - top.astype(F32)).astype(BF)
+    theirs_ref[ROWS + 8 :, :] = jnp.zeros((8, 256), BF)
 
 
 def mix(info, gated, w_here, w_there):
-    outs = [((ROWS, 256), F32), ((ROWS + 8, 256), F32), ((8, HDIM), F32)]
+    outs = [((ROWS, 256), F32), ((ROWS + TAIL, 256), BF), ((8, HDIM), F32)]
     return call(mix_kernel, (info,), (*gated, w_here, w_there), outs, 12)
 
 
 def finish_kernel(mine_ref, got_ref, squares_ref, ev_ref, out_ref, rows, sem):
-    inv = lax.rsqrt((squares_ref[...] + got_ref[ROWS:, 0:HDIM]) * (1.0 / D) + EPS)
+    tail = got_ref[ROWS : ROWS + 8, :].astype(F32)
+    inv = lax.rsqrt((squares_ref[...] + tail[:, 0:HDIM] + tail[:, HDIM:]) * (1.0 / D) + EPS)
     eye = lax.broadcasted_iota(jnp.int32, (HDIM, HDIM), 0) == lax.broadcasted_iota(jnp.int32, (HDIM, HDIM), 1)
     copies = []
     for k in range(6):
         column = jnp.sum(jnp.where(eye, inv[k : k + 1, :], 0.0), axis=1, keepdims=True)
         at = slice(k * HDIM, (k + 1) * HDIM)
-        total = mine_ref[at, :] + got_ref[at, :]
+        total = mine_ref[at, :] + got_ref[at, :].astype(F32)
         rows[at, :] = (ev_ref[at, :].astype(F32) + total * column).astype(BF)
         copies.append(pltpu.make_async_copy(rows.at[at], out_ref.at[at], sem.at[k]))
         copies[-1].start()
@@ -428,7 +418,9 @@
     c0 = flip_core(events)
     w_in = w_uvqk.reshape(D, 4 * 256)
     gain = norm_gain.reshape(4, 256)
-    p1, w_in, info, gain = lax.optimization_barrier((p1, w_in, info, gain))
+    w_here = lax.dynamic_slice_in_dim(w_out, yh * 512, 512, 1)
+    w_away = lax.dynamic_slice_in_dim(w_out, (1 - yh) * 512, 512, 1)
+    p1, w_in, info, gain, w_here, w_away = lax.optimization_barrier((p1, w_in, info, gain, w_here, w_away))
     far = [to_p2(p1[:SUB]), to_p1(p2[SUB:])]
     c1, c2 = flip_core(p1), flip_core(p2)
     far_core = [flip_core(far[0]), flip_core(far[1])]
@@ -449,9 +441,6 @@
     held = attend_early(info, lists[:2], queries[:3], keyvals)
     parts = attend_late(info, lists[2:], held, queries[3], near, away)
 
-    w_here = lax.dynamic_slice_in_dim(w_out, yh * 512, 512, 1)
-    w_away = lax.dynamic_slice_in_dim(w_out, (1 - yh) * 512, 512, 1)
-    w_away, _ = lax.optimization_barrier((w_away, q_mine))
     w_there = to_p3(w_away)
 
     parts = lax.all_to_all(parts, ("z", "x"), 0, 0)

time: 147 us -> 145 us (0.986)
  Pallas kernels: 37.5 us -> 33.6 us
  local copies, waits for them, and re-layouts: 2.36 us -> 5.45 us
  starting transfers between devices: 48.8 us -> 45.8 us
  waiting for transfers between devices: 57.8 us -> 59.3 us
    pallas_call x6, Pallas kernels: 32.7 us -> 28.9 us  [call(): pl.pallas_call(kernel, in_specs=[SMEM] * len(scalars) + [VMEM] * len(arra...]
    ppermute x26, starting transfers between devices: 44.9 us -> 41.9 us  [send(): return lax.ppermute(array, AXES, pairs)]
    ppermute x26, waiting for transfers between devices: 42.3 us -> 45.1 us  [send(): return lax.ppermute(array, AXES, pairs)]
    dynamic_slice x1, local copies, waits for them, and re-layouts: 0.04 us -> 1.77 us  [layer(): w_away = lax.dynamic_slice_in_dim(w_out, (1 - yh) * 512, 512, 1)]
  transfers between devices with their start and end apart: 27 -> 27, of which waited for: 10 -> 12; matrix products, arithmetic and copies ran while one was open for 2% -> 4% of each run, Pallas kernels for 14% -> 12%
where the time goes in v4:
time: 145 us
  waiting for transfers between devices  59.3 us (41%)
  starting transfers between devices  45.8 us (32%)
  Pallas kernels  33.6 us (23%)
  local copies, waits for them, and re-layouts  5.45 us (4%)
    ppermute x26, waiting for transfers between devices, send(): return lax.ppermute(array, AXES, pairs)  45.1 us
    ppermute x26, starting transfers between devices, send(): return lax.ppermute(array, AXES, pairs)  41.9 us
    pallas_call x6, Pallas kernels, call(): pl.pallas_call(kernel, in_specs=[SMEM] * len(scalars) + [VMEM] * len(arra...  28.9 us
    all_to_all x1, waiting for transfers between devices, layer(): parts = lax.all_to_all(parts, ('z', 'x'), 0, 0)  14.2 us
    all_to_all x1, starting transfers between devices, layer(): parts = lax.all_to_all(parts, ('z', 'x'), 0, 0)  3.84 us
    pallas_call x1, Pallas kernels, plan(): pl.pallas_call(plan_kernel, in_specs=[SMEM], out_specs=[SMEM] * 4, out_sh...  3.8 us
  transfers between devices with their start and end apart: 27, of which 12 were waited for; matrix products, arithmetic and copies ran while one was open for 4% of the time, Pallas kernels for 12%

profile of v4, /device:TPU:1, one launch (start us, length us, event | category | flops | bytes accessed | tf_op | source)
XLA Modules:
  0.0 145.2 jit_solution(2080079298648681569)
XLA Ops:
  0.0 2.1 %collective-permute-start = (bf16[768,256]{1,0:T(8,128)(2,1)}, bf16[768,256]{1,0:T(8,128)(2,1)S(1)}, u32[]{:S(2)}, u32[]{:S(2)}) collective-permute-start(bf16[768,256]{1,0:T(8,128)(2,1)} %ev_ref.1), channel_id=1, source_target_pairs={{0,16},{1,17},{2,18},{3,19},{4,20},{5,21},{6,22},{7,23},{8,24},{9,... | collective-permute-start | bytes 1179656 | tf_op jit(solution)/shard_map/ppermute | solution.py:34
  2.1 1.9 %collective-permute-start.3 = (bf16[768,256]{1,0:T(8,128)(2,1)}, bf16[768,256]{1,0:T(8,128)(2,1)S(1)}, u32[]{:S(2)}, u32[]{:S(2)}) collective-permute-start(bf16[768,256]{1,0:T(8,128)(2,1)} %ev_ref.1), channel_id=1, source_target_pairs={{0,18},{1,19},{2,16},{3,17},{4,22},{5,23},{6,20},{7,21},{8,26},{9,... | collective-permute-start | bytes 1179656 | tf_op jit(solution)/shard_map/ppermute | solution.py:34
  4.0 0.8 reduce-window.9
  4.8 0.7 reshape.35.refs_4_.refs_6_
  5.5 2.1 %copy.9 = bf16[128,8,4,256]{3,1,2,0:T(8,128)(2,1)S(1)} copy(bf16[128,8,4,256]{3,2,1,0:T(4,128)(2,1)} %bitcast.9) | data formatting | bytes 4194304
  7.7 0.1 concatenate.6.info
  7.8 1.8 %constant_dynamic-slice_fusion = (bf16[256,512]{1,0:T(8,128)(2,1)}, bf16[256,512]{1,0:T(8,128)(2,1)S(1)}) fusion(bf16[256,1024]{1,0:T(8,128)(2,1)} %param.8, s32[]{:T(128)S(6)} %select_n.7, s32[]{:T(128)S(6)} %select_n.6), kind=kLoop, calls=%fused_computation.4 | loop fusion | bytes 1048584 | tf_op jit(solution)/shard_map/dynamic_slice | solution.py:422
  9.5 1.3 collective-permute-done.refs_0_
  10.8 2.5 %collective-permute-done.3.refs_2_ = bf16[768,256]{1,0:T(8,128)(2,1)S(1)} collective-permute-done((bf16[768,256]{1,0:T(8,128)(2,1)}, bf16[768,256]{1,0:T(8,128)(2,1)S(1)}, u32[]{:S(2)}, u32[]{:S(2)}) %collective-permute-start.3) | collective-permute-done | bytes 393248 | tf_op jit(solution)/shard_map/ppermute | solution.py:34
  13.3 1.8 %collective-permute-start.8 = (bf16[768,256]{1,0:T(8,128)(2,1)S(1)}, bf16[768,256]{1,0:T(8,128)(2,1)S(1)}, u32[]{:S(2)}, u32[]{:S(2)}) collective-permute-start(bf16[768,256]{1,0:T(8,128)(2,1)S(1)} %collective-permute-done.3.refs_2_), channel_id=1, source_target_pairs={{0,1},{1,0},{2,3},{3,2},{4,5},{5,4},{6,7},{7,6},{8,9},{9,8},{10,11... | collective-permute-start | bytes 1179656 | tf_op jit(solution)/shard_map/ppermute | solution.py:34
  15.1 0.0 collective-permute-start.7
  15.1 0.5 collective-permute-start.1
  15.6 0.1 collective-permute-start.4
  15.7 2.0 %collective-permute-start.2 = (bf16[384,256]{1,0:T(8,128)(2,1)S(1)}, bf16[384,256]{1,0:T(8,128)(2,1)S(1)}, u32[]{:S(2)}, u32[]{:S(2)}) collective-permute-start(bf16[384,256]{1,0:T(8,128)(2,1)S(1)} %slice.6), channel_id=1, source_target_pairs={{0,18},{1,19},{2,16},{3,17},{4,22},{5,23},{6,20},{7,21},{8,26},{9,... | collective-permute-start | bytes 589832 | tf_op jit(solution)/shard_map/ppermute | solution.py:34
  17.7 4.4 %collective-permute-done.4.refs_3_ = bf16[384,256]{1,0:T(8,128)(2,1)S(1)} collective-permute-done((bf16[384,256]{1,0:T(8,128)(2,1)S(1)}, bf16[384,256]{1,0:T(8,128)(2,1)S(1)}, u32[]{:S(2)}, u32[]{:S(2)}) %collective-permute-start.4) | collective-permute-done | bytes 196640 | tf_op jit(solution)/shard_map/ppermute | solution.py:34
  22.1 0.9 collective-permute-start.6
  23.0 0.5 collective-permute-done.2.refs_2_
  23.5 0.9 collective-permute-start.5
  24.3 0.0 collective-permute-done.8.refs_3_
  24.3 0.0 collective-permute-done.7.refs_1_
  24.3 2.9 %shard_map.55 = (bf16[768,128]{1,0:T(8,128)(2,1)S(1)}, bf16[768,128]{1,0:T(8,128)(2,1)S(1)}, bf16[768,256]{1,0:T(8,128)(2,1)S(1)}, bf16[1024,512]{1,0:T(8,128)(2,1)S(1)}) custom-call(s32[12]{0:T(128)S(1)} %concatenate.6.info, bf16[768,256]{1,0:T(8,128)(2,1)S(1)} %collective-permute-done.refs_0_, bf16[768,256]{1,0:T(8,128)(2,1)S(1)} %collective-permute-done.7.refs_1_, ...), custom_call_target="tpu_custom_call" | custom-call | tf_op jit(solution)/shard_map/pallas_call | solution.py:71
  27.2 0.7 copy-done.1
  27.9 0.0 collective-permute-done.1.refs_1_
  27.9 0.0 collective-permute-done.6.refs_5_
  27.9 0.0 collective-permute-done.5.refs_4_
  27.9 2.6 %shard_map.56 = (bf16[768,128]{1,0:T(8,128)(2,1)S(1)}, bf16[768,256]{1,0:T(8,128)(2,1)S(1)}, bf16[384,128]{1,0:T(8,128)(2,1)S(1)}, bf16[384,128]{1,0:T(8,128)(2,...) custom-call(s32[12]{0:T(128)S(1)} %concatenate.6.info, bf16[768,256]{1,0:T(8,128)(2,1)S(1)} %copy-done, ...), custom_call_target="tpu_custom_call" | custom-call | tf_op jit(solution)/shard_map/pallas_call | solution.py:71
  30.6 3.8 %collective-permute-start.16 = (bf16[768,256]{1,0:T(8,128)(2,1)S(1)}, bf16[768,256]{1,0:T(8,128)(2,1)S(1)}, u32[]{:S(2)}, u32[]{:S(2)}) collective-permute-start(bf16[768,256]{1,0:T(8,128)(2,1)S(1)} %get-tuple-element.48.refs_3_), channel_id=1, source_target_pairs={{0,96},{1,97},{2,98},{3,99},{4,100},{5,101},{6,102},{7,103},{8,104... | collective-permute-start | bytes 1179656 | tf_op jit(solution)/shard_map/ppermute | solution.py:34
  34.4 0.0 collective-permute-start.14
  34.4 2.7 %collective-permute-start.17 = (bf16[768,256]{1,0:T(8,128)(2,1)S(1)}, bf16[768,256]{1,0:T(8,128)(2,1)S(1)}, u32[]{:S(2)}, u32[]{:S(2)}) collective-permute-start(bf16[768,256]{1,0:T(8,128)(2,1)S(1)} %get-tuple-element.49.refs_4_), channel_id=1, source_target_pairs={{0,96},{1,97},{2,98},{3,99},{4,100},{5,101},{6,102},{7,103},{8,104... | collective-permute-start | bytes 1179656 | tf_op jit(solution)/shard_map/ppermute | solution.py:34
  37.1 0.0 collective-permute-start.15
  37.1 19.4 %collective-permute-done.9 = bf16[384,128]{1,0:T(8,128)(2,1)S(1)} collective-permute-done((bf16[384,128]{1,0:T(8,128)(2,1)S(1)}, bf16[384,128]{1,0:T(8,128)(2,1)S(1)}, u32[]{:S(2)}, u32[]{:S(2)}) %collective-permute-start.9) | collective-permute-done | bytes 98336 | tf_op jit(solution)/shard_map/ppermute | solution.py:34
  56.5 0.0 collective-permute-start.10
  56.5 5.0 %collective-permute-done.10 = bf16[384,128]{1,0:T(8,128)(2,1)S(1)} collective-permute-done((bf16[384,128]{1,0:T(8,128)(2,1)S(1)}, bf16[384,128]{1,0:T(8,128)(2,1)S(1)}, u32[]{:S(2)}, u32[]{:S(2)}) %collective-permute-start.10) | collective-permute-done | bytes 98336 | tf_op jit(solution)/shard_map/ppermute | solution.py:34
  61.5 0.0 collective-permute-start.11
  61.5 3.4 %collective-permute-done.11 = bf16[384,128]{1,0:T(8,128)(2,1)S(1)} collective-permute-done((bf16[384,128]{1,0:T(8,128)(2,1)S(1)}, bf16[384,128]{1,0:T(8,128)(2,1)S(1)}, u32[]{:S(2)}, u32[]{:S(2)}) %collective-permute-start.11) | collective-permute-done | bytes 98336 | tf_op jit(solution)/shard_map/ppermute | solution.py:34
  65.0 2.5 %collective-permute-start.13 = (bf16[1536,128]{1,0:T(8,128)(2,1)S(1)}, bf16[1536,128]{1,0:T(8,128)(2,1)S(1)}, u32[]{:S(2)}, u32[]{:S(2)}) collective-permute-start(bf16[1536,128]{1,0:T(8,128)(2,1)S(1)} %constant_dynamic-update-slice_fusion.refs_0_), channel_id=1, source_target_pairs={{0,12},{1,13},{2,14},{3,15},{4,0},{5,1},{6,2},{7,3},{8,4},{9,5},{1... | collective-permute-start | bytes 1179656 | tf_op jit(solution)/shard_map/ppermute | solution.py:34
  67.5 0.0 collective-permute-done.16.refs_7_
  67.5 0.0 collective-permute-start.12
  67.5 1.7 %collective-permute-start.18 = (bf16[1536,128]{1,0:T(8,128)(2,1)S(1)}, bf16[1536,128]{1,0:T(8,128)(2,1)S(1)}, u32[]{:S(2)}, u32[]{:S(2)}) collective-permute-start(bf16[1536,128]{1,0:T(8,128)(2,1)S(1)} %constant_dynamic-update-slice_fusion.refs_0_), channel_id=1, source_target_pairs={{0,8},{1,9},{2,10},{3,11},{4,12},{5,13},{6,14},{7,15},{8,0},{9,1},... | collective-permute-start | bytes 1179656 | tf_op jit(solution)/shard_map/ppermute | solution.py:34
  69.3 0.0 collective-permute-done.17.refs_8_
  69.3 0.0 collective-permute-start.19
  69.3 0.0 collective-permute-done.15.refs_6_
  69.3 2.7 %collective-permute-start.20 = (bf16[768,256]{1,0:T(8,128)(2,1)S(1)}, bf16[768,256]{1,0:T(8,128)(2,1)S(1)}, u32[]{:S(2)}, u32[]{:S(2)}) collective-permute-start(bf16[768,256]{1,0:T(8,128)(2,1)S(1)} %collective-permute-done.17.refs_8_), channel_id=1, source_target_pairs={{0,96},{1,97},{2,98},{3,99},{4,100},{5,101},{6,102},{7,103},{8,104... | collective-permute-start | bytes 1179656 | tf_op jit(solution)/shard_map/ppermute | solution.py:34
  72.0 3.8 %plan.1 = (s32[416]{0:T(512)S(1)}, s32[416]{0:T(512)S(1)}, s32[416]{0:T(512)S(1)}, s32[416]{0:T(512)S(1)}) custom-call(s32[12]{0:T(128)S(1)} %concatenate.6.info), custom_call_target="tpu_custom_call" | custom-call | tf_op jit(solution)/shard_map/plan/pallas_call | solution.py:234
  75.8 0.0 collective-permute-done.13.refs_2_
  75.8 1.7 %collective-permute-done.12.refs_1_ = bf16[1536,128]{1,0:T(8,128)(2,1)S(1)} collective-permute-done((bf16[1536,128]{1,0:T(8,128)(2,1)S(1)}, bf16[1536,128]{1,0:T(8,128)(2,1)S(1)}, u32[]{:S(2)}, u32[]{:S(2)}) %collective-permute-start.12) | collective-permute-done | bytes 393248 | tf_op jit(solution)/shard_map/ppermute | solution.py:34
  77.4 9.2 %shard_map.57 = (f32[6144,128]{1,0:T(8,128)S(1)}, bf16[6144,128]{1,0:T(8,128)(2,1)S(1)}, bf16[6144,256]{1,0:T(8,128)(2,1)S(1)}) custom-call(s32[12]{0:T(128)S(1)} %concatenate.6.info, s32[416]{0:T(512)S(1)} %get-tuple-element.37.full_list, s32[416]{0:T(512)S(1)} %get-tuple-element.38.edge_list, ...), custom_call_target="tpu_custom_call" | custom-call | tf_op jit(solution)/shard_map/pallas_call | solution.py:71
  86.7 0.0 collective-permute-done.19.near
  86.7 11.6 %shard_map.58 = (bf16[16,384,128]{2,1,0:T(8,128)(2,1)}, f32[6144,128]{1,0:T(8,128)S(1)}, bf16[6144,128]{1,0:T(8,128)(2,1)S(1)}, bf16[6144,256]{1,0:T(8,128)(2,1)S(1)}) custom-call(s32[12]{0:T(128)S(1)} %concatenate.6.info, s32[416]{0:T(512)S(1)} %get-tuple-element.35.full_list, ...), custom_call_target="tpu_custom_call", output_to_operand_aliasing={{1}: (3, {}), {2}: (4, {}), {3}: (5, {})} | custom-call | tf_op jit(solution)/shard_map/pallas_call | solution.py:71
  98.3 3.8 %all-to-all-start = ((bf16[16,384,128]{2,1,0:T(8,128)(2,1)}), bf16[16,384,128]{2,1,0:T(8,128)(2,1)S(1)}, u32[]{:S(2)}, u32[]{:S(2)}) async-start(bf16[16,384,128]{2,1,0:T(8,128)(2,1)} %get-tuple-element.53), calls=%async_computation | async-start | bytes 3145728 | tf_op jit(solution)/shard_map/all_to_all | solution.py:446
  102.1 2.0 %collective-permute-start.24 = (bf16[256,512]{1,0:T(8,128)(2,1)S(1)}, bf16[256,512]{1,0:T(8,128)(2,1)S(1)}, u32[]{:S(2)}, u32[]{:S(2)}) collective-permute-start(bf16[256,512]{1,0:T(8,128)(2,1)S(1)} %copy-done.3), channel_id=1, source_target_pairs={{0,2},{1,3},{2,0},{3,1},{4,6},{5,7},{6,4},{7,5},{8,10},{9,11},{10,... | collective-permute-start | bytes 786440 | tf_op jit(solution)/shard_map/ppermute | solution.py:34
  104.2 14.2 %all-to-all-done.part_ref = bf16[16,384,128]{2,1,0:T(8,128)(2,1)S(1)} async-done(((bf16[16,384,128]{2,1,0:T(8,128)(2,1)}), bf16[16,384,128]{2,1,0:T(8,128)(2,1)S(1)}, u32[]{:S(2)}, u32[]{:S(2)}) %all-to-all-start) | async-done | bytes 1572896 | tf_op jit(solution)/shard_map/all_to_all | solution.py:446
  118.3 1.0 shard_map.59
  119.4 2.0 %collective-permute-start.23 = (bf16[784,128]{1,0:T(8,128)(2,1)S(1)}, bf16[784,128]{1,0:T(8,128)(2,1)S(1)}, u32[]{:S(2)}, u32[]{:S(2)}) collective-permute-start(bf16[784,128]{1,0:T(8,128)(2,1)S(1)} %get-tuple-element.56.refs_0_), channel_id=1, source_target_pairs={{0,2},{1,3},{2,0},{3,1},{4,6},{5,7},{6,4},{7,5},{8,10},{9,11},{10,... | collective-permute-start | bytes 602120 | tf_op jit(solution)/shard_map/ppermute | solution.py:34
  121.4 0.7 collective-permute-start.22
  122.1 0.0 collective-permute-start.21
  122.1 0.0 collective-permute-done.24.refs_5_
  122.1 3.7 %collective-permute-done.23.refs_3_ = bf16[784,128]{1,0:T(8,128)(2,1)S(1)} collective-permute-done((bf16[784,128]{1,0:T(8,128)(2,1)S(1)}, bf16[784,128]{1,0:T(8,128)(2,1)S(1)}, u32[]{:S(2)}, u32[]{:S(2)}) %collective-permute-start.23) | collective-permute-done | bytes 200736 | tf_op jit(solution)/shard_map/ppermute | solution.py:34
  125.8 1.9 %collective-permute-done.22.refs_2_ = bf16[784,128]{1,0:T(8,128)(2,1)S(1)} collective-permute-done((bf16[784,128]{1,0:T(8,128)(2,1)S(1)}, bf16[784,128]{1,0:T(8,128)(2,1)S(1)}, u32[]{:S(2)}, u32[]{:S(2)}) %collective-permute-start.22) | collective-permute-done | bytes 200736 | tf_op jit(solution)/shard_map/ppermute | solution.py:34
  127.7 0.0 collective-permute-done.21.refs_1_
  127.7 1.5 %shard_map.60 = (f32[768,256]{1,0:T(8,128)S(1)}, bf16[784,256]{1,0:T(8,128)(2,1)S(1)}, f32[8,128]{1,0:T(8,128)S(1)}) custom-call(s32[12]{0:T(128)S(1)} %concatenate.6.info, bf16[784,128]{1,0:T(8,128)(2,1)S(1)} %get-tuple-element.56.refs_0_, bf16[784,128]{1,0:T(8,128)(2,1)S(1)} %collective-permute-done.21.refs_1_, ...), custom_call_target="tpu_custom_call" | custom-call | tf_op jit(solution)/shard_map/pallas_call | solution.py:71
  129.2 13.6 %collective-permute-start.25 = (bf16[784,256]{1,0:T(8,128)(2,1)S(1)}, bf16[784,256]{1,0:T(8,128)(2,1)S(1)}, u32[]{:S(2)}, u32[]{:S(2)}) collective-permute-start(bf16[784,256]{1,0:T(8,128)(2,1)S(1)} %get-tuple-element.61), channel_id=1, source_target_pairs={{0,1},{1,0},{2,3},{3,2},{4,5},{5,4},{6,7},{7,6},{8,9},{9,8},{10,11... | collective-permute-start | bytes 1204232 | tf_op jit(solution)/shard_map/ppermute | solution.py:34
  142.8 1.4 collective-permute-done.25.got_ref
  144.1 0.9 finish.1
  (17 shorter events, 0.1 us)
Async XLA Ops:
  0.0 10.8 %collective-permute-start = (bf16[768,256]{1,0:T(8,128)(2,1)}, bf16[768,256]{1,0:T(8,128)(2,1)S(1)}, u32[]{:S(2)}, u32[]{:S(2)}) collective-permute-start(bf16[768,256]{1,0:T(8,128)(2,1)} %ev_ref.1), channel_id=1, source_target_pairs={{0,16},{1,17},{2,18},{3,19},{4,20},{5,21},{6,22},{7,23},{8,24},{9,... | collective-permute-start | bytes 1179656 | tf_op jit(solution)/shard_map/ppermute | solution.py:34
  2.1 11.1 %collective-permute-start.3 = (bf16[768,256]{1,0:T(8,128)(2,1)}, bf16[768,256]{1,0:T(8,128)(2,1)S(1)}, u32[]{:S(2)}, u32[]{:S(2)}) collective-permute-start(bf16[768,256]{1,0:T(8,128)(2,1)} %ev_ref.1), channel_id=1, source_target_pairs={{0,18},{1,19},{2,16},{3,17},{4,22},{5,23},{6,20},{7,21},{8,26},{9,... | collective-permute-start | bytes 1179656 | tf_op jit(solution)/shard_map/ppermute | solution.py:34
  5.5 9.5 %copy-start = (bf16[768,256]{1,0:T(8,128)(2,1)S(1)}, bf16[768,256]{1,0:T(8,128)(2,1)}, u32[]{:S(2)}) copy-start(bf16[768,256]{1,0:T(8,128)(2,1)} %ev_ref.1) | copy-start | bytes 1179652
  13.3 11.1 %collective-permute-start.8 = (bf16[768,256]{1,0:T(8,128)(2,1)S(1)}, bf16[768,256]{1,0:T(8,128)(2,1)S(1)}, u32[]{:S(2)}, u32[]{:S(2)}) collective-permute-start(bf16[768,256]{1,0:T(8,128)(2,1)S(1)} %collective-permute-done.3.refs_2_), channel_id=1, source_target_pairs={{0,1},{1,0},{2,3},{3,2},{4,5},{5,4},{6,7},{7,6},{8,9},{9,8},{10,11... | collective-permute-start | bytes 1179656 | tf_op jit(solution)/shard_map/ppermute | solution.py:34
  15.1 9.3 %collective-permute-start.7 = (bf16[768,256]{1,0:T(8,128)(2,1)S(1)}, bf16[768,256]{1,0:T(8,128)(2,1)S(1)}, u32[]{:S(2)}, u32[]{:S(2)}) collective-permute-start(bf16[768,256]{1,0:T(8,128)(2,1)S(1)} %collective-permute-done.refs_0_), channel_id=1, source_target_pairs={{0,1},{1,0},{2,3},{3,2},{4,5},{5,4},{6,7},{7,6},{8,9},{9,8},{10,11... | collective-permute-start | bytes 1179656 | tf_op jit(solution)/shard_map/ppermute | solution.py:34
  15.1 12.8 %collective-permute-start.1 = (bf16[768,256]{1,0:T(8,128)(2,1)S(1)}, bf16[768,256]{1,0:T(8,128)(2,1)S(1)}, u32[]{:S(2)}, u32[]{:S(2)}) collective-permute-start(bf16[768,256]{1,0:T(8,128)(2,1)S(1)} %copy-done), channel_id=1, source_target_pairs={{0,1},{1,0},{2,3},{3,2},{4,5},{5,4},{6,7},{7,6},{8,9},{9,8},{10,11... | collective-permute-start | bytes 1179656 | tf_op jit(solution)/shard_map/ppermute | solution.py:34
  15.6 6.5 %collective-permute-start.4 = (bf16[384,256]{1,0:T(8,128)(2,1)S(1)}, bf16[384,256]{1,0:T(8,128)(2,1)S(1)}, u32[]{:S(2)}, u32[]{:S(2)}) collective-permute-start(bf16[384,256]{1,0:T(8,128)(2,1)S(1)} %slice.8), channel_id=1, source_target_pairs={{0,16},{1,17},{2,18},{3,19},{4,20},{5,21},{6,22},{7,23},{8,24},{9,... | collective-permute-start | bytes 589832 | tf_op jit(solution)/shard_map/ppermute | solution.py:34
  15.7 7.7 %collective-permute-start.2 = (bf16[384,256]{1,0:T(8,128)(2,1)S(1)}, bf16[384,256]{1,0:T(8,128)(2,1)S(1)}, u32[]{:S(2)}, u32[]{:S(2)}) collective-permute-start(bf16[384,256]{1,0:T(8,128)(2,1)S(1)} %slice.6), channel_id=1, source_target_pairs={{0,18},{1,19},{2,16},{3,17},{4,22},{5,23},{6,20},{7,21},{8,26},{9,... | collective-permute-start | bytes 589832 | tf_op jit(solution)/shard_map/ppermute | solution.py:34
  22.1 5.8 %collective-permute-start.6 = (bf16[384,256]{1,0:T(8,128)(2,1)S(1)}, bf16[384,256]{1,0:T(8,128)(2,1)S(1)}, u32[]{:S(2)}, u32[]{:S(2)}) collective-permute-start(bf16[384,256]{1,0:T(8,128)(2,1)S(1)} %collective-permute-done.4.refs_3_), channel_id=1, source_target_pairs={{0,1},{1,0},{2,3},{3,2},{4,5},{5,4},{6,7},{7,6},{8,9},{9,8},{10,11... | collective-permute-start | bytes 589832 | tf_op jit(solution)/shard_map/ppermute | solution.py:34
  23.5 4.5 %collective-permute-start.5 = (bf16[384,256]{1,0:T(8,128)(2,1)S(1)}, bf16[384,256]{1,0:T(8,128)(2,1)S(1)}, u32[]{:S(2)}, u32[]{:S(2)}) collective-permute-start(bf16[384,256]{1,0:T(8,128)(2,1)S(1)} %collective-permute-done.2.refs_2_), channel_id=1, source_target_pairs={{0,1},{1,0},{2,3},{3,2},{4,5},{5,4},{6,7},{7,6},{8,9},{9,8},{10,11... | collective-permute-start | bytes 589832 | tf_op jit(solution)/shard_map/ppermute | solution.py:34
  27.2 0.7 copy-start.1
  30.6 37.0 %collective-permute-start.16 = (bf16[768,256]{1,0:T(8,128)(2,1)S(1)}, bf16[768,256]{1,0:T(8,128)(2,1)S(1)}, u32[]{:S(2)}, u32[]{:S(2)}) collective-permute-start(bf16[768,256]{1,0:T(8,128)(2,1)S(1)} %get-tuple-element.48.refs_3_), channel_id=1, source_target_pairs={{0,96},{1,97},{2,98},{3,99},{4,100},{5,101},{6,102},{7,103},{8,104... | collective-permute-start | bytes 1179656 | tf_op jit(solution)/shard_map/ppermute | solution.py:34
  34.4 33.1 %collective-permute-start.14 = (bf16[768,256]{1,0:T(8,128)(2,1)S(1)}, bf16[768,256]{1,0:T(8,128)(2,1)S(1)}, u32[]{:S(2)}, u32[]{:S(2)}) collective-permute-start(bf16[768,256]{1,0:T(8,128)(2,1)S(1)} %get-tuple-element.48.refs_3_), channel_id=1, source_target_pairs={{0,32},{1,33},{2,34},{3,35},{4,36},{5,37},{6,38},{7,39},{8,40},{9,... | collective-permute-start | bytes 1179656 | tf_op jit(solution)/shard_map/ppermute | solution.py:34
  34.4 34.9 %collective-permute-start.17 = (bf16[768,256]{1,0:T(8,128)(2,1)S(1)}, bf16[768,256]{1,0:T(8,128)(2,1)S(1)}, u32[]{:S(2)}, u32[]{:S(2)}) collective-permute-start(bf16[768,256]{1,0:T(8,128)(2,1)S(1)} %get-tuple-element.49.refs_4_), channel_id=1, source_target_pairs={{0,96},{1,97},{2,98},{3,99},{4,100},{5,101},{6,102},{7,103},{8,104... | collective-permute-start | bytes 1179656 | tf_op jit(solution)/shard_map/ppermute | solution.py:34
  37.1 32.2 %collective-permute-start.15 = (bf16[768,256]{1,0:T(8,128)(2,1)S(1)}, bf16[768,256]{1,0:T(8,128)(2,1)S(1)}, u32[]{:S(2)}, u32[]{:S(2)}) collective-permute-start(bf16[768,256]{1,0:T(8,128)(2,1)S(1)} %get-tuple-element.49.refs_4_), channel_id=1, source_target_pairs={{0,32},{1,33},{2,34},{3,35},{4,36},{5,37},{6,38},{7,39},{8,40},{9,... | collective-permute-start | bytes 1179656 | tf_op jit(solution)/shard_map/ppermute | solution.py:34
  37.1 19.5 %collective-permute-start.9 = (bf16[384,128]{1,0:T(8,128)(2,1)S(1)}, bf16[384,128]{1,0:T(8,128)(2,1)S(1)}, u32[]{:S(2)}, u32[]{:S(2)}) collective-permute-start(bf16[384,128]{1,0:T(8,128)(2,1)S(1)} %get-tuple-element.45), channel_id=1, source_target_pairs={{0,32},{1,33},{2,34},{3,35},{4,36},{5,37},{6,38},{7,39},{8,40},{9,... | collective-permute-start | bytes 294920 | tf_op jit(solution)/shard_map/ppermute | solution.py:34
  56.5 5.0 %collective-permute-start.10 = (bf16[384,128]{1,0:T(8,128)(2,1)S(1)}, bf16[384,128]{1,0:T(8,128)(2,1)S(1)}, u32[]{:S(2)}, u32[]{:S(2)}) collective-permute-start(bf16[384,128]{1,0:T(8,128)(2,1)S(1)} %get-tuple-element.46), channel_id=1, source_target_pairs={{0,64},{1,65},{2,66},{3,67},{4,68},{5,69},{6,70},{7,71},{8,72},{9,... | collective-permute-start | bytes 294920 | tf_op jit(solution)/shard_map/ppermute | solution.py:34
  61.5 3.5 %collective-permute-start.11 = (bf16[384,128]{1,0:T(8,128)(2,1)S(1)}, bf16[384,128]{1,0:T(8,128)(2,1)S(1)}, u32[]{:S(2)}, u32[]{:S(2)}) collective-permute-start(bf16[384,128]{1,0:T(8,128)(2,1)S(1)} %get-tuple-element.47), channel_id=1, source_target_pairs={{0,96},{1,97},{2,98},{3,99},{4,100},{5,101},{6,102},{7,103},{8,104... | collective-permute-start | bytes 294920 | tf_op jit(solution)/shard_map/ppermute | solution.py:34
  65.0 10.8 %collective-permute-start.13 = (bf16[1536,128]{1,0:T(8,128)(2,1)S(1)}, bf16[1536,128]{1,0:T(8,128)(2,1)S(1)}, u32[]{:S(2)}, u32[]{:S(2)}) collective-permute-start(bf16[1536,128]{1,0:T(8,128)(2,1)S(1)} %constant_dynamic-update-slice_fusion.refs_0_), channel_id=1, source_target_pairs={{0,12},{1,13},{2,14},{3,15},{4,0},{5,1},{6,2},{7,3},{8,4},{9,5},{1... | collective-permute-start | bytes 1179656 | tf_op jit(solution)/shard_map/ppermute | solution.py:34
  67.5 9.9 %collective-permute-start.12 = (bf16[1536,128]{1,0:T(8,128)(2,1)S(1)}, bf16[1536,128]{1,0:T(8,128)(2,1)S(1)}, u32[]{:S(2)}, u32[]{:S(2)}) collective-permute-start(bf16[1536,128]{1,0:T(8,128)(2,1)S(1)} %constant_dynamic-update-slice_fusion.refs_0_), channel_id=1, source_target_pairs={{0,4},{1,5},{2,6},{3,7},{4,8},{5,9},{6,10},{7,11},{8,12},{9,13},{1... | collective-permute-start | bytes 1179656 | tf_op jit(solution)/shard_map/ppermute | solution.py:34
  67.5 19.1 %collective-permute-start.18 = (bf16[1536,128]{1,0:T(8,128)(2,1)S(1)}, bf16[1536,128]{1,0:T(8,128)(2,1)S(1)}, u32[]{:S(2)}, u32[]{:S(2)}) collective-permute-start(bf16[1536,128]{1,0:T(8,128)(2,1)S(1)} %constant_dynamic-update-slice_fusion.refs_0_), channel_id=1, source_target_pairs={{0,8},{1,9},{2,10},{3,11},{4,12},{5,13},{6,14},{7,15},{8,0},{9,1},... | collective-permute-start | bytes 1179656 | tf_op jit(solution)/shard_map/ppermute | solution.py:34
  69.3 17.4 %collective-permute-start.19 = (bf16[768,256]{1,0:T(8,128)(2,1)S(1)}, bf16[768,256]{1,0:T(8,128)(2,1)S(1)}, u32[]{:S(2)}, u32[]{:S(2)}) collective-permute-start(bf16[768,256]{1,0:T(8,128)(2,1)S(1)} %collective-permute-done.14.refs_5_), channel_id=1, source_target_pairs={{0,32},{1,33},{2,34},{3,35},{4,36},{5,37},{6,38},{7,39},{8,40},{9,... | collective-permute-start | bytes 1179656 | tf_op jit(solution)/shard_map/ppermute | solution.py:34
  69.3 17.4 %collective-permute-start.20 = (bf16[768,256]{1,0:T(8,128)(2,1)S(1)}, bf16[768,256]{1,0:T(8,128)(2,1)S(1)}, u32[]{:S(2)}, u32[]{:S(2)}) collective-permute-start(bf16[768,256]{1,0:T(8,128)(2,1)S(1)} %collective-permute-done.17.refs_8_), channel_id=1, source_target_pairs={{0,96},{1,97},{2,98},{3,99},{4,100},{5,101},{6,102},{7,103},{8,104... | collective-permute-start | bytes 1179656 | tf_op jit(solution)/shard_map/ppermute | solution.py:34
  98.3 3.9 %copy-start.3 = (bf16[256,512]{1,0:T(8,128)(2,1)S(1)}, bf16[256,512]{1,0:T(8,128)(2,1)}, u32[]{:S(2)}) copy-start(bf16[256,512]{1,0:T(8,128)(2,1)} %get-tuple-element.59) | copy-start | bytes 786436
  98.3 20.1 %copy-start.2 = (bf16[768,128]{1,0:T(8,128)(2,1)S(1)}, bf16[768,128]{1,0:T(8,128)(2,1)}, u32[]{:S(2)}) copy-start(bf16[768,128]{1,0:T(8,128)(2,1)} %copy-done.1) | copy-start | bytes 589828
  98.3 20.0 %all-to-all-start = ((bf16[16,384,128]{2,1,0:T(8,128)(2,1)}), bf16[16,384,128]{2,1,0:T(8,128)(2,1)S(1)}, u32[]{:S(2)}, u32[]{:S(2)}) async-start(bf16[16,384,128]{2,1,0:T(8,128)(2,1)} %get-tuple-element.53), calls=%async_computation | async-start | bytes 3145728 | tf_op jit(solution)/shard_map/all_to_all | solution.py:446
  102.1 20.0 %collective-permute-start.24 = (bf16[256,512]{1,0:T(8,128)(2,1)S(1)}, bf16[256,512]{1,0:T(8,128)(2,1)S(1)}, u32[]{:S(2)}, u32[]{:S(2)}) collective-permute-start(bf16[256,512]{1,0:T(8,128)(2,1)S(1)} %copy-done.3), channel_id=1, source_target_pairs={{0,2},{1,3},{2,0},{3,1},{4,6},{5,7},{6,4},{7,5},{8,10},{9,11},{10,... | collective-permute-start | bytes 786440 | tf_op jit(solution)/shard_map/ppermute | solution.py:34
  119.4 6.4 %collective-permute-start.23 = (bf16[784,128]{1,0:T(8,128)(2,1)S(1)}, bf16[784,128]{1,0:T(8,128)(2,1)S(1)}, u32[]{:S(2)}, u32[]{:S(2)}) collective-permute-start(bf16[784,128]{1,0:T(8,128)(2,1)S(1)} %get-tuple-element.56.refs_0_), channel_id=1, source_target_pairs={{0,2},{1,3},{2,0},{3,1},{4,6},{5,7},{6,4},{7,5},{8,10},{9,11},{10,... | collective-permute-start | bytes 602120 | tf_op jit(solution)/shard_map/ppermute | solution.py:34
  121.4 6.3 %collective-permute-start.22 = (bf16[784,128]{1,0:T(8,128)(2,1)S(1)}, bf16[784,128]{1,0:T(8,128)(2,1)S(1)}, u32[]{:S(2)}, u32[]{:S(2)}) collective-permute-start(bf16[784,128]{1,0:T(8,128)(2,1)S(1)} %get-tuple-element.57), channel_id=1, source_target_pairs={{0,18},{1,19},{2,16},{3,17},{4,22},{5,23},{6,20},{7,21},{8,26},{9,... | collective-permute-start | bytes 602120 | tf_op jit(solution)/shard_map/ppermute | solution.py:34
  122.1 5.6 %collective-permute-start.21 = (bf16[784,128]{1,0:T(8,128)(2,1)S(1)}, bf16[784,128]{1,0:T(8,128)(2,1)S(1)}, u32[]{:S(2)}, u32[]{:S(2)}) collective-permute-start(bf16[784,128]{1,0:T(8,128)(2,1)S(1)} %get-tuple-element.57), channel_id=1, source_target_pairs={{0,16},{1,17},{2,18},{3,19},{4,20},{5,21},{6,22},{7,23},{8,24},{9,... | collective-permute-start | bytes 602120 | tf_op jit(solution)/shard_map/ppermute | solution.py:34
  129.2 14.9 %collective-permute-start.25 = (bf16[784,256]{1,0:T(8,128)(2,1)S(1)}, bf16[784,256]{1,0:T(8,128)(2,1)S(1)}, u32[]{:S(2)}, u32[]{:S(2)}) collective-permute-start(bf16[784,256]{1,0:T(8,128)(2,1)S(1)} %get-tuple-element.61), channel_id=1, source_target_pairs={{0,1},{1,0},{2,3},{3,2},{4,5},{5,4},{6,7},{7,6},{8,9},{9,8},{10,11... | collective-permute-start | bytes 1204232 | tf_op jit(solution)/shard_map/ppermute | solution.py:34

commit v5 on v4

--- a/solution.py
+++ b/solution.py
@@ -209,16 +209,17 @@
     zero = jnp.int32(0)
     fe, ee, fl, el = lax.fori_loop(0, TILES, list_queries, (zero, zero, zero, zero))
     for fulls, nf, edges, ne in ((full_early, fe, edge_early, ee), (full_late, fl, edge_late, el)):
-        groups = nf >> 2
+        groups = nf >> 3
 
         def move(i, ne):
             edges[ne] = fulls[i]
             return ne + 1
 
-        ne = lax.fori_loop(groups * 4, nf, move, ne)
-        edges[ne] = 512 + (z * 4 + x) * 32 + z * 6 + 3 * yl
+        ne = lax.fori_loop(groups * 8, nf, move, ne)
+        for pad in range(2):
+            edges[ne + pad] = 512 + (z * 4 + x) * 32 + z * 6 + 3 * yl
         fulls[LIST - 1] = groups
-        edges[LIST - 1] = (ne + 1) >> 1
+        edges[LIST - 1] = lax.div(ne + 2, 3)
 
 
 def query_first(info, t):
@@ -266,16 +267,16 @@
         acc[q_rows, :] += jnp.dot(w.astype(BF), kv[k_rows, HDIM:], preferred_element_type=F32)
 
     def full_tiles(i, carry):
-        for u in range(4):
-            w, q_rows, k_rows, _, _ = scores(full_list[4 * i + u])
+        for u in range(8):
+            w, q_rows, k_rows, _, _ = scores(full_list[8 * i + u])
             add(w, q_rows, k_rows)
         return carry
 
     lax.fori_loop(0, full_list[LIST - 1], full_tiles, 0)
 
     def edge_tiles(i, carry):
-        for u in range(2):
-            entry = edge_list[2 * i + u]
+        for u in range(3):
+            entry = edge_list[3 * i + u]
             w, q_rows, k_rows, t, n = scores(entry)
             first = query_first(info, t)
             col = key_first(info, n) + lax.broadcasted_iota(jnp.int32, (1, KEYS), 1)

time: 145 us -> 143 us (0.986)
  Pallas kernels: 33.6 us -> 30.9 us
    pallas_call x6, Pallas kernels: 28.9 us -> 26.2 us  [call(): pl.pallas_call(kernel, in_specs=[SMEM] * len(scalars) + [VMEM] * len(arra...]
  transfers between devices with their start and end apart: 27 -> 27, of which waited for: 12 -> 12; matrix products, arithmetic and copies ran while one was open for 4% -> 4% of each run, Pallas kernels for 12% -> 11%
where the time goes in v5:
time: 143 us
  waiting for transfers between devices  59.2 us (41%)
  starting transfers between devices  45.7 us (32%)
  Pallas kernels  30.9 us (22%)
  local copies, waits for them, and re-layouts  5.45 us (4%)
    ppermute x26, waiting for transfers between devices, send(): return lax.ppermute(array, AXES, pairs)  45.1 us
    ppermute x26, starting transfers between devices, send(): return lax.ppermute(array, AXES, pairs)  41.9 us
    pallas_call x6, Pallas kernels, call(): pl.pallas_call(kernel, in_specs=[SMEM] * len(scalars) + [VMEM] * len(arra...  26.2 us
    all_to_all x1, waiting for transfers between devices, layer(): parts = lax.all_to_all(parts, ('z', 'x'), 0, 0)  14.2 us
    all_to_all x1, starting transfers between devices, layer(): parts = lax.all_to_all(parts, ('z', 'x'), 0, 0)  3.84 us
    pallas_call x1, Pallas kernels, plan(): pl.pallas_call(plan_kernel, in_specs=[SMEM], out_specs=[SMEM] * 4, out_sh...  3.83 us
    unnamed x12, local copies, waits for them, and re-layouts  2.86 us
  transfers between devices with their start and end apart: 27, of which 12 were waited for; matrix products, arithmetic and copies ran while one was open for 4% of the time, Pallas kernels for 11%

profile of v5, /device:TPU:1, one launch (start us, length us, event | category | flops | bytes accessed | tf_op | source)
XLA Modules:
  0.0 142.5 jit_solution(10023019399083227163)
XLA Ops:
  0.0 2.1 %collective-permute-start = (bf16[768,256]{1,0:T(8,128)(2,1)}, bf16[768,256]{1,0:T(8,128)(2,1)S(1)}, u32[]{:S(2)}, u32[]{:S(2)}) collective-permute-start(bf16[768,256]{1,0:T(8,128)(2,1)} %ev_ref.1), channel_id=1, source_target_pairs={{0,16},{1,17},{2,18},{3,19},{4,20},{5,21},{6,22},{7,23},{8,24},{9,... | collective-permute-start | bytes 1179656 | tf_op jit(solution)/shard_map/ppermute | solution.py:34
  2.1 1.9 %collective-permute-start.3 = (bf16[768,256]{1,0:T(8,128)(2,1)}, bf16[768,256]{1,0:T(8,128)(2,1)S(1)}, u32[]{:S(2)}, u32[]{:S(2)}) collective-permute-start(bf16[768,256]{1,0:T(8,128)(2,1)} %ev_ref.1), channel_id=1, source_target_pairs={{0,18},{1,19},{2,16},{3,17},{4,22},{5,23},{6,20},{7,21},{8,26},{9,... | collective-permute-start | bytes 1179656 | tf_op jit(solution)/shard_map/ppermute | solution.py:34
  4.0 0.8 reduce-window.9
  4.8 0.7 reshape.35.refs_4_.refs_6_
  5.5 2.1 %copy.9 = bf16[128,8,4,256]{3,1,2,0:T(8,128)(2,1)S(1)} copy(bf16[128,8,4,256]{3,2,1,0:T(4,128)(2,1)} %bitcast.9) | data formatting | bytes 4194304
  7.7 0.1 concatenate.6.info
  7.8 1.8 %constant_dynamic-slice_fusion = (bf16[256,512]{1,0:T(8,128)(2,1)}, bf16[256,512]{1,0:T(8,128)(2,1)S(1)}) fusion(bf16[256,1024]{1,0:T(8,128)(2,1)} %param.8, s32[]{:T(128)S(6)} %select_n.7, s32[]{:T(128)S(6)} %select_n.6), kind=kLoop, calls=%fused_computation.4 | loop fusion | bytes 1048584 | tf_op jit(solution)/shard_map/dynamic_slice | solution.py:423
  9.5 1.3 collective-permute-done.refs_0_
  10.8 2.5 %collective-permute-done.3.refs_2_ = bf16[768,256]{1,0:T(8,128)(2,1)S(1)} collective-permute-done((bf16[768,256]{1,0:T(8,128)(2,1)}, bf16[768,256]{1,0:T(8,128)(2,1)S(1)}, u32[]{:S(2)}, u32[]{:S(2)}) %collective-permute-start.3) | collective-permute-done | bytes 393248 | tf_op jit(solution)/shard_map/ppermute | solution.py:34
  13.3 1.8 %collective-permute-start.8 = (bf16[768,256]{1,0:T(8,128)(2,1)S(1)}, bf16[768,256]{1,0:T(8,128)(2,1)S(1)}, u32[]{:S(2)}, u32[]{:S(2)}) collective-permute-start(bf16[768,256]{1,0:T(8,128)(2,1)S(1)} %collective-permute-done.3.refs_2_), channel_id=1, source_target_pairs={{0,1},{1,0},{2,3},{3,2},{4,5},{5,4},{6,7},{7,6},{8,9},{9,8},{10,11... | collective-permute-start | bytes 1179656 | tf_op jit(solution)/shard_map/ppermute | solution.py:34
  15.1 0.0 collective-permute-start.7
  15.1 0.5 collective-permute-start.1
  15.6 0.1 collective-permute-start.4
  15.7 2.0 %collective-permute-start.2 = (bf16[384,256]{1,0:T(8,128)(2,1)S(1)}, bf16[384,256]{1,0:T(8,128)(2,1)S(1)}, u32[]{:S(2)}, u32[]{:S(2)}) collective-permute-start(bf16[384,256]{1,0:T(8,128)(2,1)S(1)} %slice.6), channel_id=1, source_target_pairs={{0,18},{1,19},{2,16},{3,17},{4,22},{5,23},{6,20},{7,21},{8,26},{9,... | collective-permute-start | bytes 589832 | tf_op jit(solution)/shard_map/ppermute | solution.py:34
  17.7 4.4 %collective-permute-done.4.refs_3_ = bf16[384,256]{1,0:T(8,128)(2,1)S(1)} collective-permute-done((bf16[384,256]{1,0:T(8,128)(2,1)S(1)}, bf16[384,256]{1,0:T(8,128)(2,1)S(1)}, u32[]{:S(2)}, u32[]{:S(2)}) %collective-permute-start.4) | collective-permute-done | bytes 196640 | tf_op jit(solution)/shard_map/ppermute | solution.py:34
  22.1 0.9 collective-permute-start.6
  23.0 0.5 collective-permute-done.2.refs_2_
  23.5 0.9 collective-permute-start.5
  24.3 0.0 collective-permute-done.8.refs_3_
  24.3 0.0 collective-permute-done.7.refs_1_
  24.3 2.9 %shard_map.55 = (bf16[768,128]{1,0:T(8,128)(2,1)S(1)}, bf16[768,128]{1,0:T(8,128)(2,1)S(1)}, bf16[768,256]{1,0:T(8,128)(2,1)S(1)}, bf16[1024,512]{1,0:T(8,128)(2,1)S(1)}) custom-call(s32[12]{0:T(128)S(1)} %concatenate.6.info, bf16[768,256]{1,0:T(8,128)(2,1)S(1)} %collective-permute-done.refs_0_, bf16[768,256]{1,0:T(8,128)(2,1)S(1)} %collective-permute-done.7.refs_1_, ...), custom_call_target="tpu_custom_call" | custom-call | tf_op jit(solution)/shard_map/pallas_call | solution.py:71
  27.2 0.7 copy-done.1
  27.9 0.0 collective-permute-done.1.refs_1_
  27.9 0.0 collective-permute-done.6.refs_5_
  27.9 0.0 collective-permute-done.5.refs_4_
  27.9 2.6 %shard_map.56 = (bf16[768,128]{1,0:T(8,128)(2,1)S(1)}, bf16[768,256]{1,0:T(8,128)(2,1)S(1)}, bf16[384,128]{1,0:T(8,128)(2,1)S(1)}, bf16[384,128]{1,0:T(8,128)(2,...) custom-call(s32[12]{0:T(128)S(1)} %concatenate.6.info, bf16[768,256]{1,0:T(8,128)(2,1)S(1)} %copy-done, ...), custom_call_target="tpu_custom_call" | custom-call | tf_op jit(solution)/shard_map/pallas_call | solution.py:71
  30.6 3.8 %collective-permute-start.16 = (bf16[768,256]{1,0:T(8,128)(2,1)S(1)}, bf16[768,256]{1,0:T(8,128)(2,1)S(1)}, u32[]{:S(2)}, u32[]{:S(2)}) collective-permute-start(bf16[768,256]{1,0:T(8,128)(2,1)S(1)} %get-tuple-element.48.refs_3_), channel_id=1, source_target_pairs={{0,96},{1,97},{2,98},{3,99},{4,100},{5,101},{6,102},{7,103},{8,104... | collective-permute-start | bytes 1179656 | tf_op jit(solution)/shard_map/ppermute | solution.py:34
  34.4 0.0 collective-permute-start.14
  34.4 2.7 %collective-permute-start.17 = (bf16[768,256]{1,0:T(8,128)(2,1)S(1)}, bf16[768,256]{1,0:T(8,128)(2,1)S(1)}, u32[]{:S(2)}, u32[]{:S(2)}) collective-permute-start(bf16[768,256]{1,0:T(8,128)(2,1)S(1)} %get-tuple-element.49.refs_4_), channel_id=1, source_target_pairs={{0,96},{1,97},{2,98},{3,99},{4,100},{5,101},{6,102},{7,103},{8,104... | collective-permute-start | bytes 1179656 | tf_op jit(solution)/shard_map/ppermute | solution.py:34
  37.1 19.4 %collective-permute-done.9 = bf16[384,128]{1,0:T(8,128)(2,1)S(1)} collective-permute-done((bf16[384,128]{1,0:T(8,128)(2,1)S(1)}, bf16[384,128]{1,0:T(8,128)(2,1)S(1)}, u32[]{:S(2)}, u32[]{:S(2)}) %collective-permute-start.9) | collective-permute-done | bytes 98336 | tf_op jit(solution)/shard_map/ppermute | solution.py:34
  56.5 0.0 collective-permute-start.10
  56.5 5.0 %collective-permute-done.10 = bf16[384,128]{1,0:T(8,128)(2,1)S(1)} collective-permute-done((bf16[384,128]{1,0:T(8,128)(2,1)S(1)}, bf16[384,128]{1,0:T(8,128)(2,1)S(1)}, u32[]{:S(2)}, u32[]{:S(2)}) %collective-permute-start.10) | collective-permute-done | bytes 98336 | tf_op jit(solution)/shard_map/ppermute | solution.py:34
  61.5 0.0 collective-permute-start.11
  61.5 3.4 %collective-permute-done.11 = bf16[384,128]{1,0:T(8,128)(2,1)S(1)} collective-permute-done((bf16[384,128]{1,0:T(8,128)(2,1)S(1)}, bf16[384,128]{1,0:T(8,128)(2,1)S(1)}, u32[]{:S(2)}, u32[]{:S(2)}) %collective-permute-start.11) | collective-permute-done | bytes 98336 | tf_op jit(solution)/shard_map/ppermute | solution.py:34
  65.0 2.5 %collective-permute-start.13 = (bf16[1536,128]{1,0:T(8,128)(2,1)S(1)}, bf16[1536,128]{1,0:T(8,128)(2,1)S(1)}, u32[]{:S(2)}, u32[]{:S(2)}) collective-permute-start(bf16[1536,128]{1,0:T(8,128)(2,1)S(1)} %constant_dynamic-update-slice_fusion.refs_0_), channel_id=1, source_target_pairs={{0,12},{1,13},{2,14},{3,15},{4,0},{5,1},{6,2},{7,3},{8,4},{9,5},{1... | collective-permute-start | bytes 1179656 | tf_op jit(solution)/shard_map/ppermute | solution.py:34
  67.5 0.0 collective-permute-done.16.refs_7_
  67.5 0.0 collective-permute-start.12
  67.5 1.7 %collective-permute-start.18 = (bf16[1536,128]{1,0:T(8,128)(2,1)S(1)}, bf16[1536,128]{1,0:T(8,128)(2,1)S(1)}, u32[]{:S(2)}, u32[]{:S(2)}) collective-permute-start(bf16[1536,128]{1,0:T(8,128)(2,1)S(1)} %constant_dynamic-update-slice_fusion.refs_0_), channel_id=1, source_target_pairs={{0,8},{1,9},{2,10},{3,11},{4,12},{5,13},{6,14},{7,15},{8,0},{9,1},... | collective-permute-start | bytes 1179656 | tf_op jit(solution)/shard_map/ppermute | solution.py:34
  69.3 0.0 collective-permute-done.17.refs_8_
  69.3 0.0 collective-permute-start.19
  69.3 0.0 collective-permute-done.15.refs_6_
  69.3 2.7 %collective-permute-start.20 = (bf16[768,256]{1,0:T(8,128)(2,1)S(1)}, bf16[768,256]{1,0:T(8,128)(2,1)S(1)}, u32[]{:S(2)}, u32[]{:S(2)}) collective-permute-start(bf16[768,256]{1,0:T(8,128)(2,1)S(1)} %collective-permute-done.17.refs_8_), channel_id=1, source_target_pairs={{0,96},{1,97},{2,98},{3,99},{4,100},{5,101},{6,102},{7,103},{8,104... | collective-permute-start | bytes 1179656 | tf_op jit(solution)/shard_map/ppermute | solution.py:34
  72.0 3.8 %plan.1 = (s32[416]{0:T(512)S(1)}, s32[416]{0:T(512)S(1)}, s32[416]{0:T(512)S(1)}, s32[416]{0:T(512)S(1)}) custom-call(s32[12]{0:T(128)S(1)} %concatenate.6.info), custom_call_target="tpu_custom_call" | custom-call | tf_op jit(solution)/shard_map/plan/pallas_call | solution.py:235
  75.8 0.0 collective-permute-done.13.refs_2_
  75.8 1.6 %collective-permute-done.12.refs_1_ = bf16[1536,128]{1,0:T(8,128)(2,1)S(1)} collective-permute-done((bf16[1536,128]{1,0:T(8,128)(2,1)S(1)}, bf16[1536,128]{1,0:T(8,128)(2,1)S(1)}, u32[]{:S(2)}, u32[]{:S(2)}) %collective-permute-start.12) | collective-permute-done | bytes 393248 | tf_op jit(solution)/shard_map/ppermute | solution.py:34
  77.4 8.1 %shard_map.57 = (f32[6144,128]{1,0:T(8,128)S(1)}, bf16[6144,128]{1,0:T(8,128)(2,1)S(1)}, bf16[6144,256]{1,0:T(8,128)(2,1)S(1)}) custom-call(s32[12]{0:T(128)S(1)} %concatenate.6.info, s32[416]{0:T(512)S(1)} %get-tuple-element.37.full_list, s32[416]{0:T(512)S(1)} %get-tuple-element.38.edge_list, ...), custom_call_target="tpu_custom_call" | custom-call | tf_op jit(solution)/shard_map/pallas_call | solution.py:71
  85.6 0.0 collective-permute-done.19.near
  85.6 0.0 collective-permute-done.20.away
  85.6 10.0 %shard_map.58 = (bf16[16,384,128]{2,1,0:T(8,128)(2,1)}, f32[6144,128]{1,0:T(8,128)S(1)}, bf16[6144,128]{1,0:T(8,128)(2,1)S(1)}, bf16[6144,256]{1,0:T(8,128)(2,1)S(1)}) custom-call(s32[12]{0:T(128)S(1)} %concatenate.6.info, s32[416]{0:T(512)S(1)} %get-tuple-element.35.full_list, ...), custom_call_target="tpu_custom_call", output_to_operand_aliasing={{1}: (3, {}), {2}: (4, {}), {3}: (5, {})} | custom-call | tf_op jit(solution)/shard_map/pallas_call | solution.py:71
  95.6 3.8 %all-to-all-start = ((bf16[16,384,128]{2,1,0:T(8,128)(2,1)}), bf16[16,384,128]{2,1,0:T(8,128)(2,1)S(1)}, u32[]{:S(2)}, u32[]{:S(2)}) async-start(bf16[16,384,128]{2,1,0:T(8,128)(2,1)} %get-tuple-element.53), calls=%async_computation | async-start | bytes 3145728 | tf_op jit(solution)/shard_map/all_to_all | solution.py:447
  99.4 2.0 %collective-permute-start.24 = (bf16[256,512]{1,0:T(8,128)(2,1)S(1)}, bf16[256,512]{1,0:T(8,128)(2,1)S(1)}, u32[]{:S(2)}, u32[]{:S(2)}) collective-permute-start(bf16[256,512]{1,0:T(8,128)(2,1)S(1)} %copy-done.3), channel_id=1, source_target_pairs={{0,2},{1,3},{2,0},{3,1},{4,6},{5,7},{6,4},{7,5},{8,10},{9,11},{10,... | collective-permute-start | bytes 786440 | tf_op jit(solution)/shard_map/ppermute | solution.py:34
  101.4 14.2 %all-to-all-done.part_ref = bf16[16,384,128]{2,1,0:T(8,128)(2,1)S(1)} async-done(((bf16[16,384,128]{2,1,0:T(8,128)(2,1)}), bf16[16,384,128]{2,1,0:T(8,128)(2,1)S(1)}, u32[]{:S(2)}, u32[]{:S(2)}) %all-to-all-start) | async-done | bytes 1572896 | tf_op jit(solution)/shard_map/all_to_all | solution.py:447
  115.6 1.0 shard_map.59
  116.7 2.0 %collective-permute-start.23 = (bf16[784,128]{1,0:T(8,128)(2,1)S(1)}, bf16[784,128]{1,0:T(8,128)(2,1)S(1)}, u32[]{:S(2)}, u32[]{:S(2)}) collective-permute-start(bf16[784,128]{1,0:T(8,128)(2,1)S(1)} %get-tuple-element.56.refs_0_), channel_id=1, source_target_pairs={{0,2},{1,3},{2,0},{3,1},{4,6},{5,7},{6,4},{7,5},{8,10},{9,11},{10,... | collective-permute-start | bytes 602120 | tf_op jit(solution)/shard_map/ppermute | solution.py:34
  118.7 0.7 collective-permute-start.22
  119.4 0.0 collective-permute-start.21
  119.4 0.0 collective-permute-done.24.refs_5_
  119.4 3.7 %collective-permute-done.23.refs_3_ = bf16[784,128]{1,0:T(8,128)(2,1)S(1)} collective-permute-done((bf16[784,128]{1,0:T(8,128)(2,1)S(1)}, bf16[784,128]{1,0:T(8,128)(2,1)S(1)}, u32[]{:S(2)}, u32[]{:S(2)}) %collective-permute-start.23) | collective-permute-done | bytes 200736 | tf_op jit(solution)/shard_map/ppermute | solution.py:34
  123.1 1.9 %collective-permute-done.22.refs_2_ = bf16[784,128]{1,0:T(8,128)(2,1)S(1)} collective-permute-done((bf16[784,128]{1,0:T(8,128)(2,1)S(1)}, bf16[784,128]{1,0:T(8,128)(2,1)S(1)}, u32[]{:S(2)}, u32[]{:S(2)}) %collective-permute-start.22) | collective-permute-done | bytes 200736 | tf_op jit(solution)/shard_map/ppermute | solution.py:34
  125.0 0.0 collective-permute-done.21.refs_1_
  125.0 1.5 %shard_map.60 = (f32[768,256]{1,0:T(8,128)S(1)}, bf16[784,256]{1,0:T(8,128)(2,1)S(1)}, f32[8,128]{1,0:T(8,128)S(1)}) custom-call(s32[12]{0:T(128)S(1)} %concatenate.6.info, bf16[784,128]{1,0:T(8,128)(2,1)S(1)} %get-tuple-element.56.refs_0_, bf16[784,128]{1,0:T(8,128)(2,1)S(1)} %collective-permute-done.21.refs_1_, ...), custom_call_target="tpu_custom_call" | custom-call | tf_op jit(solution)/shard_map/pallas_call | solution.py:71
  126.5 13.5 %collective-permute-start.25 = (bf16[784,256]{1,0:T(8,128)(2,1)S(1)}, bf16[784,256]{1,0:T(8,128)(2,1)S(1)}, u32[]{:S(2)}, u32[]{:S(2)}) collective-permute-start(bf16[784,256]{1,0:T(8,128)(2,1)S(1)} %get-tuple-element.61), channel_id=1, source_target_pairs={{0,1},{1,0},{2,3},{3,2},{4,5},{5,4},{6,7},{7,6},{8,9},{9,8},{10,11... | collective-permute-start | bytes 1204232 | tf_op jit(solution)/shard_map/ppermute | solution.py:34
  140.1 1.4 collective-permute-done.25.got_ref
  141.4 0.9 finish.1
  (17 shorter events, 0.1 us)
Async XLA Ops:
  0.0 10.8 %collective-permute-start = (bf16[768,256]{1,0:T(8,128)(2,1)}, bf16[768,256]{1,0:T(8,128)(2,1)S(1)}, u32[]{:S(2)}, u32[]{:S(2)}) collective-permute-start(bf16[768,256]{1,0:T(8,128)(2,1)} %ev_ref.1), channel_id=1, source_target_pairs={{0,16},{1,17},{2,18},{3,19},{4,20},{5,21},{6,22},{7,23},{8,24},{9,... | collective-permute-start | bytes 1179656 | tf_op jit(solution)/shard_map/ppermute | solution.py:34
  2.1 11.1 %collective-permute-start.3 = (bf16[768,256]{1,0:T(8,128)(2,1)}, bf16[768,256]{1,0:T(8,128)(2,1)S(1)}, u32[]{:S(2)}, u32[]{:S(2)}) collective-permute-start(bf16[768,256]{1,0:T(8,128)(2,1)} %ev_ref.1), channel_id=1, source_target_pairs={{0,18},{1,19},{2,16},{3,17},{4,22},{5,23},{6,20},{7,21},{8,26},{9,... | collective-permute-start | bytes 1179656 | tf_op jit(solution)/shard_map/ppermute | solution.py:34
  5.5 9.5 %copy-start = (bf16[768,256]{1,0:T(8,128)(2,1)S(1)}, bf16[768,256]{1,0:T(8,128)(2,1)}, u32[]{:S(2)}) copy-start(bf16[768,256]{1,0:T(8,128)(2,1)} %ev_ref.1) | copy-start | bytes 1179652
  13.3 11.1 %collective-permute-start.8 = (bf16[768,256]{1,0:T(8,128)(2,1)S(1)}, bf16[768,256]{1,0:T(8,128)(2,1)S(1)}, u32[]{:S(2)}, u32[]{:S(2)}) collective-permute-start(bf16[768,256]{1,0:T(8,128)(2,1)S(1)} %collective-permute-done.3.refs_2_), channel_id=1, source_target_pairs={{0,1},{1,0},{2,3},{3,2},{4,5},{5,4},{6,7},{7,6},{8,9},{9,8},{10,11... | collective-permute-start | bytes 1179656 | tf_op jit(solution)/shard_map/ppermute | solution.py:34
  15.1 9.3 %collective-permute-start.7 = (bf16[768,256]{1,0:T(8,128)(2,1)S(1)}, bf16[768,256]{1,0:T(8,128)(2,1)S(1)}, u32[]{:S(2)}, u32[]{:S(2)}) collective-permute-start(bf16[768,256]{1,0:T(8,128)(2,1)S(1)} %collective-permute-done.refs_0_), channel_id=1, source_target_pairs={{0,1},{1,0},{2,3},{3,2},{4,5},{5,4},{6,7},{7,6},{8,9},{9,8},{10,11... | collective-permute-start | bytes 1179656 | tf_op jit(solution)/shard_map/ppermute | solution.py:34
  15.1 12.8 %collective-permute-start.1 = (bf16[768,256]{1,0:T(8,128)(2,1)S(1)}, bf16[768,256]{1,0:T(8,128)(2,1)S(1)}, u32[]{:S(2)}, u32[]{:S(2)}) collective-permute-start(bf16[768,256]{1,0:T(8,128)(2,1)S(1)} %copy-done), channel_id=1, source_target_pairs={{0,1},{1,0},{2,3},{3,2},{4,5},{5,4},{6,7},{7,6},{8,9},{9,8},{10,11... | collective-permute-start | bytes 1179656 | tf_op jit(solution)/shard_map/ppermute | solution.py:34
  15.6 6.5 %collective-permute-start.4 = (bf16[384,256]{1,0:T(8,128)(2,1)S(1)}, bf16[384,256]{1,0:T(8,128)(2,1)S(1)}, u32[]{:S(2)}, u32[]{:S(2)}) collective-permute-start(bf16[384,256]{1,0:T(8,128)(2,1)S(1)} %slice.8), channel_id=1, source_target_pairs={{0,16},{1,17},{2,18},{3,19},{4,20},{5,21},{6,22},{7,23},{8,24},{9,... | collective-permute-start | bytes 589832 | tf_op jit(solution)/shard_map/ppermute | solution.py:34
  15.7 7.7 %collective-permute-start.2 = (bf16[384,256]{1,0:T(8,128)(2,1)S(1)}, bf16[384,256]{1,0:T(8,128)(2,1)S(1)}, u32[]{:S(2)}, u32[]{:S(2)}) collective-permute-start(bf16[384,256]{1,0:T(8,128)(2,1)S(1)} %slice.6), channel_id=1, source_target_pairs={{0,18},{1,19},{2,16},{3,17},{4,22},{5,23},{6,20},{7,21},{8,26},{9,... | collective-permute-start | bytes 589832 | tf_op jit(solution)/shard_map/ppermute | solution.py:34
  22.1 5.8 %collective-permute-start.6 = (bf16[384,256]{1,0:T(8,128)(2,1)S(1)}, bf16[384,256]{1,0:T(8,128)(2,1)S(1)}, u32[]{:S(2)}, u32[]{:S(2)}) collective-permute-start(bf16[384,256]{1,0:T(8,128)(2,1)S(1)} %collective-permute-done.4.refs_3_), channel_id=1, source_target_pairs={{0,1},{1,0},{2,3},{3,2},{4,5},{5,4},{6,7},{7,6},{8,9},{9,8},{10,11... | collective-permute-start | bytes 589832 | tf_op jit(solution)/shard_map/ppermute | solution.py:34
  23.5 4.5 %collective-permute-start.5 = (bf16[384,256]{1,0:T(8,128)(2,1)S(1)}, bf16[384,256]{1,0:T(8,128)(2,1)S(1)}, u32[]{:S(2)}, u32[]{:S(2)}) collective-permute-start(bf16[384,256]{1,0:T(8,128)(2,1)S(1)} %collective-permute-done.2.refs_2_), channel_id=1, source_target_pairs={{0,1},{1,0},{2,3},{3,2},{4,5},{5,4},{6,7},{7,6},{8,9},{9,8},{10,11... | collective-permute-start | bytes 589832 | tf_op jit(solution)/shard_map/ppermute | solution.py:34
  27.2 0.7 copy-start.1
  30.6 37.0 %collective-permute-start.16 = (bf16[768,256]{1,0:T(8,128)(2,1)S(1)}, bf16[768,256]{1,0:T(8,128)(2,1)S(1)}, u32[]{:S(2)}, u32[]{:S(2)}) collective-permute-start(bf16[768,256]{1,0:T(8,128)(2,1)S(1)} %get-tuple-element.48.refs_3_), channel_id=1, source_target_pairs={{0,96},{1,97},{2,98},{3,99},{4,100},{5,101},{6,102},{7,103},{8,104... | collective-permute-start | bytes 1179656 | tf_op jit(solution)/shard_map/ppermute | solution.py:34
  34.4 33.1 %collective-permute-start.14 = (bf16[768,256]{1,0:T(8,128)(2,1)S(1)}, bf16[768,256]{1,0:T(8,128)(2,1)S(1)}, u32[]{:S(2)}, u32[]{:S(2)}) collective-permute-start(bf16[768,256]{1,0:T(8,128)(2,1)S(1)} %get-tuple-element.48.refs_3_), channel_id=1, source_target_pairs={{0,32},{1,33},{2,34},{3,35},{4,36},{5,37},{6,38},{7,39},{8,40},{9,... | collective-permute-start | bytes 1179656 | tf_op jit(solution)/shard_map/ppermute | solution.py:34
  34.4 34.9 %collective-permute-start.17 = (bf16[768,256]{1,0:T(8,128)(2,1)S(1)}, bf16[768,256]{1,0:T(8,128)(2,1)S(1)}, u32[]{:S(2)}, u32[]{:S(2)}) collective-permute-start(bf16[768,256]{1,0:T(8,128)(2,1)S(1)} %get-tuple-element.49.refs_4_), channel_id=1, source_target_pairs={{0,96},{1,97},{2,98},{3,99},{4,100},{5,101},{6,102},{7,103},{8,104... | collective-permute-start | bytes 1179656 | tf_op jit(solution)/shard_map/ppermute | solution.py:34
  37.1 32.2 %collective-permute-start.15 = (bf16[768,256]{1,0:T(8,128)(2,1)S(1)}, bf16[768,256]{1,0:T(8,128)(2,1)S(1)}, u32[]{:S(2)}, u32[]{:S(2)}) collective-permute-start(bf16[768,256]{1,0:T(8,128)(2,1)S(1)} %get-tuple-element.49.refs_4_), channel_id=1, source_target_pairs={{0,32},{1,33},{2,34},{3,35},{4,36},{5,37},{6,38},{7,39},{8,40},{9,... | collective-permute-start | bytes 1179656 | tf_op jit(solution)/shard_map/ppermute | solution.py:34
  37.1 19.5 %collective-permute-start.9 = (bf16[384,128]{1,0:T(8,128)(2,1)S(1)}, bf16[384,128]{1,0:T(8,128)(2,1)S(1)}, u32[]{:S(2)}, u32[]{:S(2)}) collective-permute-start(bf16[384,128]{1,0:T(8,128)(2,1)S(1)} %get-tuple-element.45), channel_id=1, source_target_pairs={{0,32},{1,33},{2,34},{3,35},{4,36},{5,37},{6,38},{7,39},{8,40},{9,... | collective-permute-start | bytes 294920 | tf_op jit(solution)/shard_map/ppermute | solution.py:34
  56.5 5.0 %collective-permute-start.10 = (bf16[384,128]{1,0:T(8,128)(2,1)S(1)}, bf16[384,128]{1,0:T(8,128)(2,1)S(1)}, u32[]{:S(2)}, u32[]{:S(2)}) collective-permute-start(bf16[384,128]{1,0:T(8,128)(2,1)S(1)} %get-tuple-element.46), channel_id=1, source_target_pairs={{0,64},{1,65},{2,66},{3,67},{4,68},{5,69},{6,70},{7,71},{8,72},{9,... | collective-permute-start | bytes 294920 | tf_op jit(solution)/shard_map/ppermute | solution.py:34
  61.5 3.5 %collective-permute-start.11 = (bf16[384,128]{1,0:T(8,128)(2,1)S(1)}, bf16[384,128]{1,0:T(8,128)(2,1)S(1)}, u32[]{:S(2)}, u32[]{:S(2)}) collective-permute-start(bf16[384,128]{1,0:T(8,128)(2,1)S(1)} %get-tuple-element.47), channel_id=1, source_target_pairs={{0,96},{1,97},{2,98},{3,99},{4,100},{5,101},{6,102},{7,103},{8,104... | collective-permute-start | bytes 294920 | tf_op jit(solution)/shard_map/ppermute | solution.py:34
  65.0 10.8 %collective-permute-start.13 = (bf16[1536,128]{1,0:T(8,128)(2,1)S(1)}, bf16[1536,128]{1,0:T(8,128)(2,1)S(1)}, u32[]{:S(2)}, u32[]{:S(2)}) collective-permute-start(bf16[1536,128]{1,0:T(8,128)(2,1)S(1)} %constant_dynamic-update-slice_fusion.refs_0_), channel_id=1, source_target_pairs={{0,12},{1,13},{2,14},{3,15},{4,0},{5,1},{6,2},{7,3},{8,4},{9,5},{1... | collective-permute-start | bytes 1179656 | tf_op jit(solution)/shard_map/ppermute | solution.py:34
  67.5 9.9 %collective-permute-start.12 = (bf16[1536,128]{1,0:T(8,128)(2,1)S(1)}, bf16[1536,128]{1,0:T(8,128)(2,1)S(1)}, u32[]{:S(2)}, u32[]{:S(2)}) collective-permute-start(bf16[1536,128]{1,0:T(8,128)(2,1)S(1)} %constant_dynamic-update-slice_fusion.refs_0_), channel_id=1, source_target_pairs={{0,4},{1,5},{2,6},{3,7},{4,8},{5,9},{6,10},{7,11},{8,12},{9,13},{1... | collective-permute-start | bytes 1179656 | tf_op jit(solution)/shard_map/ppermute | solution.py:34
  67.5 18.0 %collective-permute-start.18 = (bf16[1536,128]{1,0:T(8,128)(2,1)S(1)}, bf16[1536,128]{1,0:T(8,128)(2,1)S(1)}, u32[]{:S(2)}, u32[]{:S(2)}) collective-permute-start(bf16[1536,128]{1,0:T(8,128)(2,1)S(1)} %constant_dynamic-update-slice_fusion.refs_0_), channel_id=1, source_target_pairs={{0,8},{1,9},{2,10},{3,11},{4,12},{5,13},{6,14},{7,15},{8,0},{9,1},... | collective-permute-start | bytes 1179656 | tf_op jit(solution)/shard_map/ppermute | solution.py:34
  69.3 16.3 %collective-permute-start.19 = (bf16[768,256]{1,0:T(8,128)(2,1)S(1)}, bf16[768,256]{1,0:T(8,128)(2,1)S(1)}, u32[]{:S(2)}, u32[]{:S(2)}) collective-permute-start(bf16[768,256]{1,0:T(8,128)(2,1)S(1)} %collective-permute-done.14.refs_5_), channel_id=1, source_target_pairs={{0,32},{1,33},{2,34},{3,35},{4,36},{5,37},{6,38},{7,39},{8,40},{9,... | collective-permute-start | bytes 1179656 | tf_op jit(solution)/shard_map/ppermute | solution.py:34
  69.3 16.3 %collective-permute-start.20 = (bf16[768,256]{1,0:T(8,128)(2,1)S(1)}, bf16[768,256]{1,0:T(8,128)(2,1)S(1)}, u32[]{:S(2)}, u32[]{:S(2)}) collective-permute-start(bf16[768,256]{1,0:T(8,128)(2,1)S(1)} %collective-permute-done.17.refs_8_), channel_id=1, source_target_pairs={{0,96},{1,97},{2,98},{3,99},{4,100},{5,101},{6,102},{7,103},{8,104... | collective-permute-start | bytes 1179656 | tf_op jit(solution)/shard_map/ppermute | solution.py:34
  95.6 3.9 %copy-start.3 = (bf16[256,512]{1,0:T(8,128)(2,1)S(1)}, bf16[256,512]{1,0:T(8,128)(2,1)}, u32[]{:S(2)}) copy-start(bf16[256,512]{1,0:T(8,128)(2,1)} %get-tuple-element.59) | copy-start | bytes 786436
  95.6 20.1 %copy-start.2 = (bf16[768,128]{1,0:T(8,128)(2,1)S(1)}, bf16[768,128]{1,0:T(8,128)(2,1)}, u32[]{:S(2)}) copy-start(bf16[768,128]{1,0:T(8,128)(2,1)} %copy-done.1) | copy-start | bytes 589828
  95.6 20.0 %all-to-all-start = ((bf16[16,384,128]{2,1,0:T(8,128)(2,1)}), bf16[16,384,128]{2,1,0:T(8,128)(2,1)S(1)}, u32[]{:S(2)}, u32[]{:S(2)}) async-start(bf16[16,384,128]{2,1,0:T(8,128)(2,1)} %get-tuple-element.53), calls=%async_computation | async-start | bytes 3145728 | tf_op jit(solution)/shard_map/all_to_all | solution.py:447
  99.4 20.0 %collective-permute-start.24 = (bf16[256,512]{1,0:T(8,128)(2,1)S(1)}, bf16[256,512]{1,0:T(8,128)(2,1)S(1)}, u32[]{:S(2)}, u32[]{:S(2)}) collective-permute-start(bf16[256,512]{1,0:T(8,128)(2,1)S(1)} %copy-done.3), channel_id=1, source_target_pairs={{0,2},{1,3},{2,0},{3,1},{4,6},{5,7},{6,4},{7,5},{8,10},{9,11},{10,... | collective-permute-start | bytes 786440 | tf_op jit(solution)/shard_map/ppermute | solution.py:34
  116.7 6.4 %collective-permute-start.23 = (bf16[784,128]{1,0:T(8,128)(2,1)S(1)}, bf16[784,128]{1,0:T(8,128)(2,1)S(1)}, u32[]{:S(2)}, u32[]{:S(2)}) collective-permute-start(bf16[784,128]{1,0:T(8,128)(2,1)S(1)} %get-tuple-element.56.refs_0_), channel_id=1, source_target_pairs={{0,2},{1,3},{2,0},{3,1},{4,6},{5,7},{6,4},{7,5},{8,10},{9,11},{10,... | collective-permute-start | bytes 602120 | tf_op jit(solution)/shard_map/ppermute | solution.py:34
  118.7 6.3 %collective-permute-start.22 = (bf16[784,128]{1,0:T(8,128)(2,1)S(1)}, bf16[784,128]{1,0:T(8,128)(2,1)S(1)}, u32[]{:S(2)}, u32[]{:S(2)}) collective-permute-start(bf16[784,128]{1,0:T(8,128)(2,1)S(1)} %get-tuple-element.57), channel_id=1, source_target_pairs={{0,18},{1,19},{2,16},{3,17},{4,22},{5,23},{6,20},{7,21},{8,26},{9,... | collective-permute-start | bytes 602120 | tf_op jit(solution)/shard_map/ppermute | solution.py:34
  119.4 5.6 %collective-permute-start.21 = (bf16[784,128]{1,0:T(8,128)(2,1)S(1)}, bf16[784,128]{1,0:T(8,128)(2,1)S(1)}, u32[]{:S(2)}, u32[]{:S(2)}) collective-permute-start(bf16[784,128]{1,0:T(8,128)(2,1)S(1)} %get-tuple-element.57), channel_id=1, source_target_pairs={{0,16},{1,17},{2,18},{3,19},{4,20},{5,21},{6,22},{7,23},{8,24},{9,... | collective-permute-start | bytes 602120 | tf_op jit(solution)/shard_map/ppermute | solution.py:34
  126.5 14.9 %collective-permute-start.25 = (bf16[784,256]{1,0:T(8,128)(2,1)S(1)}, bf16[784,256]{1,0:T(8,128)(2,1)S(1)}, u32[]{:S(2)}, u32[]{:S(2)}) collective-permute-start(bf16[784,256]{1,0:T(8,128)(2,1)S(1)} %get-tuple-element.61), channel_id=1, source_target_pairs={{0,1},{1,0},{2,3},{3,2},{4,5},{5,4},{6,7},{7,6},{8,9},{9,8},{10,11... | collective-permute-start | bytes 1204232 | tf_op jit(solution)/shard_map/ppermute | solution.py:34
